TPU v7x, 32 devices: a whole 2x2x4 slice. The times are simulated.
32 devices in a mesh: grp: 8 (over z, x), loc: 4 (over y, core).
Axes of the slice: x: 2, y: 2, z: 4, core: 2. Of those that a mesh axis runs over, the one named last changes fastest.
Arguments:
- features: bfloat16 [32768, 2048], P(('grp', 'loc')), may hold values from -6 to 6
- weight: bfloat16 [2048, 2048], replicated, may hold values from -0.125 to 0.125
- bias: float32 [2048], replicated, may hold values from -2.5 to 2.5
- cotangent: bfloat16 [32768, 2048], P(('grp', 'loc')), may hold values from -6 to 6
- neighbours: int32 [32768, 64], P(('grp', 'loc')), may hold values from 0 to 127, as said below
- edge_mask: int32 [32768, 64], P(('grp', 'loc')), may hold values from 0 to 1, as said below
- cluster_ids: int32 [32768], P(('grp', 'loc')), may hold values from 0 to 127, as said below
- row_mask: int32 [32768], P(('grp', 'loc')), may hold values from 0 to 1
Outputs:
- activations: bfloat16 [32768, 2048], P(('grp', 'loc'))
- grad_features: bfloat16 [32768, 2048], P(('grp', 'loc'))
- grad_weight: float32 [2048, 2048], replicated
- grad_bias: float32 [2048], replicated
Inputs may be any that keep to these rules, and one draw needn't show every extreme that they name: `neighbours`: positions within the node's own tile of 128 slots. `edge_mask`: each row's live entries come first. `cluster_ids`: starts at 0 in every tile, never falls within a tile and rises by at most one from slot to slot.
All inputs are finite; a program needn't handle non-finite values.
Results may differ from a plain program's by a relative error of at most 0.009.
The roundings to bfloat16 on the way count: a program that leaves them out, or rounds other values in their place, can miss the bound.
Values sent between devices are 32-bit elements; how exact they have to be, the bound alone decides.
No kernel may reach another device: no remote copies, remote signals or barrier semaphores. Data moves between devices by JAX's collectives and lax.ppermute only.
A program may use at most 128 MiB of HBM per device.

v0:
```python
import jax
import jax.numpy as jnp
from jax import lax
from jax.sharding import PartitionSpec as P

TILE = 128
NBRS = 64


def build_tile(near, live_edges, clusters, present):
    width = near.shape[0]
    position = jnp.arange(width, dtype=jnp.int32)
    matched = (near[:, :, None] == position[None, None, :]) & (live_edges[:, :, None] == 1)
    edge_hits = jnp.sum(matched.astype(jnp.int32), axis=1)
    allowed = (clusters[:, None] == clusters[None, :]) & (position[:, None] != position[None, :])
    allowed = allowed & (present[:, None] == 1) & (present[None, :] == 1)
    adjacency = jnp.where(allowed, edge_hits, 0).astype(jnp.float32)
    degree = jnp.sum(adjacency, axis=1)
    self_loops = jnp.where(
        (position[:, None] == position[None, :]) & (present[:, None] == 1), 2.0, 0.0
    ).astype(jnp.float32)
    return (adjacency + self_loops) / (degree + 1.0)[:, None]


def per_device(features, weight, bias, cotangent, neighbours, edge_mask, cluster_ids, row_mask):
    rows = features.shape[0]
    width = features.shape[1]
    tile_count = rows // TILE
    pieces = (
        neighbours.reshape(tile_count, TILE, NBRS),
        edge_mask.reshape(tile_count, TILE, NBRS),
        cluster_ids.reshape(tile_count, TILE),
        row_mask.reshape(tile_count, TILE),
    )
    propagator = lax.map(lambda group: build_tile(*group), pieces).astype(jnp.bfloat16)
    mixed = (
        jnp.einsum(
            "tij,tjd->tid",
            propagator,
            features.reshape(tile_count, TILE, width),
            preferred_element_type=jnp.float32,
        )
        .reshape(rows, width)
        .astype(jnp.bfloat16)
    )
    pre = jnp.dot(mixed, weight, preferred_element_type=jnp.float32) + bias
    activations = jnp.maximum(pre, 0.0).astype(jnp.bfloat16)
    grad_pre = jnp.where(pre > 0.0, cotangent.astype(jnp.float32), 0.0).astype(jnp.bfloat16)
    weight_term = lax.dot_general(
        mixed, grad_pre, (((0,), (0,)), ((), ())), preferred_element_type=jnp.float32
    )
    bias_term = jnp.sum(grad_pre.astype(jnp.float32), axis=0)
    shares = (
        lax.psum_scatter(weight_term, "loc", scatter_dimension=0, tiled=True),
        lax.psum_scatter(bias_term, "loc", scatter_dimension=0, tiled=True),
    )
    totals = lax.psum((shares[0], shares[1]), "grp")
    grad_weight, grad_bias = (
        lax.all_gather(totals[0], "loc", axis=0, tiled=True),
        lax.all_gather(totals[1], "loc", axis=0, tiled=True),
    )
    grad_mixed = lax.dot_general(
        grad_pre, weight, (((1,), (1,)), ((), ())), preferred_element_type=jnp.float32
    ).astype(jnp.bfloat16)
    grad_features = (
        jnp.einsum(
            "tji,tjd->tid",
            propagator,
            grad_mixed.reshape(tile_count, TILE, width),
            preferred_element_type=jnp.float32,
        )
        .reshape(rows, width)
        .astype(jnp.bfloat16)
    )
    return (activations, grad_features, grad_weight, grad_bias)


def solution(mesh):
    in_specs = (
        P(("grp", "loc"), None),
        P(),
        P(),
        P(("grp", "loc"), None),
        P(("grp", "loc"), None),
        P(("grp", "loc"), None),
        P(("grp", "loc")),
        P(("grp", "loc")),
    )
    out_specs = (P(("grp", "loc"), None), P(("grp", "loc"), None), P(), P())
    return jax.shard_map(
        per_device, mesh=mesh, in_specs=in_specs, out_specs=out_specs, check_vma=False
    )
```

profile of v0, /device:TPU:19, one launch (start us, length us, event | category | flops | bytes accessed | tf_op | source)
XLA Modules:
  0.0 491.1 jit_solution(9502656532124461445)
XLA Ops:
  7.2 1.1 copy.18
  8.4 1.1 copy.19
  9.5 36.7 %while.10 = (s32[]{:T(128)}, bf16[8,128,128]{2,1,0:T(8,128)(2,1)S(1)}, s32[8,128]{1,0:T(8,128)}, s32[8,128]{1,0:T(8,128)}, s32[8,128,64]{2,1,0:T(8,128)S(1)}, /*index=5*/s32[8,128,64]{2,1,0:T(8,128)S(1)}, s32[]{:T(128)}) while((s32[]{:T(128)}, bf16[8,128,128]{2,1,0:T(8,128)(2,1)S(1)}, s32[8,128]{1,0:T(8,128)}, s32[8,128]{1,0:T(8,128)}, ...), condition=%wide.region_3.4_spmd, body=%wide.region_0.3_spmd.sunk | while | flops 4513922 | bytes 416105 | solution.py:35
  9.5 0.7 compare_bitcast_fusion.2
  11.0 2.8 convert_reduce_fusion.5
  14.1 0.7 compare_bitcast_fusion.2
  15.6 2.8 convert_reduce_fusion.5
  18.7 0.7 compare_bitcast_fusion.2
  20.1 2.8 convert_reduce_fusion.5
  23.3 0.7 compare_bitcast_fusion.2
  24.7 2.8 convert_reduce_fusion.5
  27.9 0.7 compare_bitcast_fusion.2
  29.3 2.8 convert_reduce_fusion.5
  32.5 0.7 compare_bitcast_fusion.2
  33.9 2.8 convert_reduce_fusion.5
  37.1 0.7 compare_bitcast_fusion.2
  38.5 2.8 convert_reduce_fusion.5
  43.1 2.8 convert_reduce_fusion.5
  46.2 3.6 convolution_convert_fusion.2
  49.8 1.0 copy-done
  50.9 12.7 %convert_reduce_fusion.2 = (f32[2048]{0:T(1024)S(1)}, bf16[1024,2048]{1,0:T(8,128)(2,1)S(1)}, bf16[1024,2048]{1,0:T(8,128)(2,1)}) fusion(bf16[1024,2048]{1,0:T(8,128)(2,1)} %param.13, f32[2048]{0:T(1024)S(1)} %copy-done.1, bf16[1024,2048]{1,0:T(8,128)(2,1)S(1)} %bitcast.51, bf16[2048,2048]{1,0:T(8,128)(2,1)S(1)} %copy-done), kind=kOutput, calls=%fused_computation.27 | convolution fusion | flops 8608806912 | bytes 25182208 | tf_op jit(solution)/shard_map/dot_general | solution.py:46
  63.5 2.0 copy-done.3
  65.6 11.7 %fusion.16 = f32[2048,2048]{1,0:T(8,128)} fusion(bf16[1024,2048]{1,0:T(8,128)(2,1)S(1)} %bitcast.52, bf16[1024,2048]{1,0:T(8,128)(2,1)S(1)} %get-tuple-element.50), kind=kOutput, calls=%fused_computation.35 | convolution fusion | flops 8589934592 | bytes 25165824 | tf_op jit(solution)/shard_map/dot_general | solution.py:49
  77.3 127.3 %reduce-scatter.2.cloned.1.call-done = f32[512,2048]{1,0:T(8,128)} async-done(((f32[2048,2048]{1,0:T(8,128)}), f32[512,2048]{1,0:T(8,128)}) %reduce-scatter.2.cloned.1.call-update) | async-done | bytes 4194320 | tf_op jit(solution)/shard_map/reduce_scatter | solution.py:54
  204.7 159.4 %all-reduce.3.cloned.1.call-done = f32[512,2048]{1,0:T(8,128)} async-done(((f32[512,2048]{1,0:T(8,128)}), f32[512,2048]{1,0:T(8,128)}) %all-reduce.3.cloned.1.call-update) | async-done | bytes 4194320 | tf_op jit(solution)/shard_map/psum | solution.py:57
  365.4 5.8 %all-reduce = f32[2048]{0:T(1024)S(1)} all-reduce(f32[2048]{0:T(1024)S(1)} %get-tuple-element.49), channel_id=3, replica_groups=mesh['grp'=8,'loc'=4] {'loc'}, use_global_device_ids=true, to_apply=%region_7.8.clone | all-reduce | flops 2048 | bytes 16384
  371.3 11.2 %psum.15 = f32[512]{0:T(512)S(1)} all-reduce(f32[512]{0:T(512)S(1)} %dynamic-slice.1), channel_id=1, replica_groups=mesh['grp'=8,'loc'=4] {'grp'}, use_global_device_ids=true, to_apply=%region_8.9 | all-reduce | flops 512 | bytes 4096 | tf_op jit(solution)/shard_map/psum | solution.py:57
  382.4 10.0 %all-gather = f32[4,1,512]{2,1,0:T(1,128)S(1)} all-gather(f32[1,1,512]{2,1,0:T(1,128)S(1)} %bitcast.57), channel_id=1, replica_groups=mesh['grp'=8,'loc'=4] {'loc'}, dimensions={0}, use_global_device_ids=true | all-gather | bytes 10240 | tf_op jit(solution)/shard_map/all_gather | solution.py:60
  392.4 12.5 %convolution_convert_fusion = bf16[1024,2048]{1,0:T(8,128)(2,1)S(1)} fusion(bf16[1024,2048]{1,0:T(8,128)(2,1)} %copy-done.3, bf16[2048,2048]{1,0:T(8,128)(2,1)} %param.11), kind=kOutput, calls=%fused_computation.30 | convolution fusion | flops 8592031744 | bytes 16777216 | tf_op jit(solution)/shard_map/dot_general | solution.py:62
  405.0 3.3 convolution_convert_fusion.1
  408.3 63.9 %all-gather.3.cloned.1.call-done = f32[2048,2048]{1,0:T(8,128)} async-done(((f32[512,2048]{1,0:T(8,128)}), f32[2048,2048]{1,0:T(8,128)}) %all-gather.3.cloned.1.call-update) | async-done | bytes 16777232 | tf_op jit(solution)/shard_map/all_gather | solution.py:59
  472.2 11.8 %copy.34 = f32[2048,2048]{1,0:T(8,128)} copy(f32[2048,2048]{1,0:T(8,128)} %all-gather.3.cloned.1.call-done) | data formatting | bytes 33554432
  (65 shorter events, 10.6 us)
Async XLA Ops:
  7.2 197.4 %reduce-scatter.2.cloned.1.call-start = ((), (), s32[]{:S(2)}) async-start(), calls=%async_computation.1 | async-start | bytes 20971520 | tf_op jit(solution)/shard_map/reduce_scatter | solution.py:54
  46.2 4.6 copy-start
  46.2 4.6 copy-start.1
  63.5 2.0 copy-start.3
  77.3 286.8 %all-reduce.3.cloned.1.call-start = ((), (), s32[]{:S(2)}) async-start(), calls=%async_computation.2 | async-start | bytes 8388608 | tf_op jit(solution)/shard_map/psum | solution.py:57
  204.6 159.5 %copy-start.2 = (u32[32]{0:T(128)S(1)}, u32[32]{0:T(128)}, u32[]{:S(2)}) copy-start(u32[32]{0:T(128)} %constant.26) | copy-start | bytes 388
  204.6 267.5 %all-gather.3.cloned.1.call-start = ((), (), s32[]{:S(2)}) async-start(), calls=%async_computation.3 | async-start | bytes 20971520 | tf_op jit(solution)/shard_map/all_gather | solution.py:59
Sparse Core Ops, SparseCore 0:
  77.4 127.1 reduce-scatter.1
  208.7 155.3 all-reduce.2
  365.7 106.3 all-gather.2
where the time goes:
time: 493 us; the launch traced here: 491 us
  waiting for transfers between devices  351 us (71%)
  matrix products  43.8 us (9%)
  other arithmetic  30.7 us (6%)
  blocking collectives  26.9 us (5%)
  local copies, waits for them, and re-layouts  24.1 us (5%)
  between operations  14.5 us (3%)
    psum x1, waiting for transfers between devices, per_device(): totals = lax.psum((shares[0], shares[1]), 'grp')  159 us
    reduce_scatter x1, waiting for transfers between devices, per_device(): lax.psum_scatter(weight_term, 'loc', scatter_dimension=0, tiled=True)  127 us
    all_gather x1, waiting for transfers between devices, per_device(): lax.all_gather(totals[0], 'loc', axis=0, tiled=True)  63.9 us
    reduce_sum x8, other arithmetic, build_tile(): edge_hits = jnp.sum(matched.astype(jnp.int32), axis=1)  22.4 us
    unnamed x14, local copies, waits for them, and re-layouts  18.4 us
    dot_general x1, matrix products, per_device(): pre = jnp.dot(mixed, weight, preferred_element_type=jnp.float32) + bias  12.7 us
    dot_general x1, matrix products, per_device(): lax.dot_general(grad_pre, weight, (((1,), (1,)), ((), ())), preferred_ele...  12.5 us
    dot_general x1, matrix products, per_device(): lax.dot_general(mixed, grad_pre, (((0,), (0,)), ((), ())), preferred_elem...  11.7 us
  transfers between devices with their start and end apart: 3, of which 3 were waited for; matrix products, arithmetic and copies ran while one was open for 3% of the time, Pallas kernels for 0%

commit v1 on v0

v1 whole, which is shorter than its diff:
```python
import functools

import jax
import jax.numpy as jnp
from jax import lax
from jax.experimental import pallas as pl
from jax.experimental.pallas import tpu as pltpu
from jax.sharding import PartitionSpec as P

TILE = 128
BF16 = jnp.bfloat16
F32 = jnp.float32

GROUPS = ((2, "xyz"), (2, "zxy"), (2, "xyz"), (2, "xyz"))
ORDER = (
    "g0", "g1", "r00", "r10", "g2", "r01", "r20", "r02", "g3", "r11", "r21", "r03", "r30", "r12", "r22", "a00",
    "r23", "r31", "a01", "r13", "r32", "a20", "a02", "r33", "a10", "a21", "c0", "w00", "a11", "a30", "w01",
    "a22", "a31", "a12", "f0", "f1", "c2", "f2", "w21", "a32", "f3", "c1", "w10", "w11", "w20", "c3", "w30",
    "w31",
)

COST = pl.CostEstimate(flops=25 * 10**9, bytes_accessed=2**20, transcendentals=0)
DONE = jax.ShapeDtypeStruct((8, 128), F32)
VMEM = pl.BlockSpec(memory_space=pltpu.VMEM)
ANY = pl.BlockSpec(memory_space=pl.ANY)


def tile_kernel(near_ref, live_ref, cluster_ref, present_ref, features_ref, prop_ref, mixed_ref):
    tiles = cluster_ref.shape[0]
    step = pl.program_id(0)
    slot = lax.broadcasted_iota(jnp.int32, (TILE, TILE), 0)
    node = lax.broadcasted_iota(jnp.int32, (TILE, TILE), 1)
    slot_low = slot.astype(F32).astype(BF16)
    one, zero = jnp.ones((TILE, TILE), BF16), jnp.zeros((TILE, TILE), BF16)
    for t in range(tiles):
        part = slice(t * TILE, (t + 1) * TILE)
        near = jnp.where(live_ref[:, part] == 1, near_ref[:, part], -1).astype(F32).astype(BF16)
        hits = zero
        for k in range(near.shape[0]):
            hits = hits + jnp.where(near[k : k + 1, :] == slot_low, one, zero)
        key = jnp.where(present_ref[t] == 1, cluster_ref[t], -1).astype(F32)
        along = jnp.broadcast_to(key, (TILE, TILE))
        down = along.T
        allowed = (along == down) & (along >= 0.0) & (slot != node)
        adjacency = jnp.where(allowed, hits.astype(F32), 0.0)
        degree = jnp.sum(adjacency, axis=0, keepdims=True)
        self_loops = jnp.where((slot == node) & (along >= 0.0), 2.0, 0.0)
        prop_t = (adjacency + self_loops) / (degree + 1.0)
        at = step * tiles + t
        prop_ref[at] = prop_t.astype(BF16)
        prop = prop_t.T.astype(BF16)
        mixed = jnp.dot(prop, features_ref[part, :], preferred_element_type=F32)
        mixed_ref[pl.ds(pl.multiple_of(at * TILE, TILE), TILE), :] = mixed.astype(BF16)


def propagate(features, neighbours, edge_mask, cluster_ids, row_mask):
    rows, width = features.shape
    tiles = rows // TILE
    nbrs = neighbours.shape[1]
    each = 2
    block = each * TILE
    inputs = (
        neighbours.T,
        edge_mask.T,
        cluster_ids.reshape(tiles, 1, TILE),
        row_mask.reshape(tiles, 1, TILE),
        features,
    )
    return pl.pallas_call(
        tile_kernel,
        grid=(tiles // each,),
        in_specs=[
            pl.BlockSpec((nbrs, block), lambda t: (0, t)),
            pl.BlockSpec((nbrs, block), lambda t: (0, t)),
            pl.BlockSpec((each, 1, TILE), lambda t: (t, 0, 0)),
            pl.BlockSpec((each, 1, TILE), lambda t: (t, 0, 0)),
            pl.BlockSpec((block, width), lambda t: (t, 0)),
        ],
        out_specs=[VMEM, VMEM],
        out_shape=[
            jax.ShapeDtypeStruct((tiles, TILE, TILE), BF16),
            jax.ShapeDtypeStruct((rows, width), BF16),
        ],
        compiler_params=pltpu.CompilerParams(vmem_limit_bytes=12 * 2**20),
        cost_estimate=pl.CostEstimate(
            flops=2 * rows * width * width // 2, bytes_accessed=2 * rows * width, transcendentals=0
        ),
        name="propagate",
    )(*(pltpu.with_memory_space_constraint(v, pltpu.HBM) for v in inputs))


def layer_kernel(start, line, base_ref, mixed_ref, weight_ref, bias_ref, cot_ref, token_ref, *rest):
    act_out, gp_ref, theirs_ref, mine_ref, act_ref, cot_in, act_sem, cot_sem = rest[-8:]
    rows, cols = act_ref.shape
    block = min(rows, 512)
    half = (mine_ref.shape[0] - 8) // 2
    chunk = half // 4
    here = slice(start, start + cols)
    load = pltpu.make_async_copy(cot_ref.at[:, pl.ds(start, cols)], cot_in, cot_sem)
    load.start()
    total = jnp.zeros((1, cols), F32)
    for i in range(rows // block):
        part = slice(i * block, (i + 1) * block)
        pre = jnp.dot(mixed_ref[part, :], weight_ref[:, here], preferred_element_type=F32) + bias_ref[:, here]
        act_ref[part, :] = jnp.maximum(pre, 0.0).astype(BF16)
        if i == 0:
            load.wait()
        grad = jnp.where(pre > 0.0, cot_in[part, :].astype(F32), 0.0).astype(BF16)
        gp_ref[part, here] = grad
        total = total + jnp.sum(grad.astype(F32), axis=0, keepdims=True)
    store = pltpu.make_async_copy(act_ref, act_out.at[:, pl.ds(start, cols)], act_sem)
    store.start()

    for side, out_ref in ((0, theirs_ref), (1, mine_ref)):
        for j in range(2):
            from_row = pl.multiple_of((base_ref[line + side] // 8) * 2 * half + j * half, half)
            share = lax.dot_general(
                mixed_ref[:, pl.ds(from_row, half)],
                gp_ref[:, here],
                (((0,), (0,)), ((), ())),
                preferred_element_type=F32,
            )
            for m in range(4):
                spot = ((j * 4 + m) ^ (base_ref[line + side] % 8)) * chunk
                out_ref[pl.ds(pl.multiple_of(spot, chunk), chunk), :] = share[m * chunk : (m + 1) * chunk]
        out_ref[2 * half :, :] = jnp.broadcast_to(total, (8, cols))
    store.wait()


def layer_group(name, base, line, mixed, weight, bias, cotangent, token, carried, start, cols):
    rows, width = mixed.shape
    share = jax.ShapeDtypeStruct((width // 2 + 8, cols), F32)
    return pl.pallas_call(
        functools.partial(layer_kernel, start, line),
        grid_spec=pltpu.PrefetchScalarGridSpec(
            num_scalar_prefetch=1,
            grid=(1,),
            in_specs=[VMEM, VMEM, VMEM, ANY, ANY] + ([ANY, VMEM] if carried else []),
            out_specs=[ANY, VMEM, VMEM, VMEM],
            scratch_shapes=[
                pltpu.VMEM((rows, cols), BF16),
                pltpu.VMEM((rows, cols), BF16),
                pltpu.SemaphoreType.DMA,
                pltpu.SemaphoreType.DMA,
            ],
        ),
        out_shape=[
            jax.ShapeDtypeStruct((rows, width), BF16),
            jax.ShapeDtypeStruct((rows, width), BF16),
            share,
            share,
        ],
        input_output_aliases={6: 0, 7: 1} if carried else {},
        compiler_params=pltpu.CompilerParams(vmem_limit_bytes=10 * 2**20),
        cost_estimate=COST,
        name=name,
    )(base, mixed, weight, bias.reshape(1, width), pltpu.with_memory_space_constraint(cotangent, pltpu.HBM), token, *carried)


def join_kernel(plan, *refs):
    outs = refs[len(refs) - len(plan) :]
    for out_ref, pieces in zip(outs, plan):
        at = 0
        for count, terms in pieces:
            value = refs[terms[0][0]][terms[0][1] : terms[0][1] + count, :]
            for index, row in terms[1:]:
                value = value + refs[index][row : row + count, :]
            out_ref[at : at + count, :] = value
            at += count


def join(name, arrays, token, *plan):
    cols = arrays[0].shape[1]
    return pl.pallas_call(
        functools.partial(join_kernel, plan),
        in_specs=[VMEM] * len(arrays) + [ANY],
        out_specs=[VMEM] * len(plan),
        out_shape=[jax.ShapeDtypeStruct((sum(n for n, _ in pieces), cols), F32) for pieces in plan],
        compiler_params=pltpu.CompilerParams(vmem_limit_bytes=12 * 2**20),
        cost_estimate=COST,
        name=name,
    )(*arrays, token)


def place_kernel(side, at, base_ref, first_ref, second_ref, token_ref, *rest):
    out_ref, done_ref, sem = rest[-3:]
    cols = first_ref.shape[1]
    chunk = first_ref.shape[0] // 4
    copies = []
    for r in range(8):
        source = first_ref if r < 4 else second_ref
        spot = pl.multiple_of((base_ref[side] ^ r) * chunk, chunk)
        copies.append(
            pltpu.make_async_copy(
                source.at[pl.ds((r % 4) * chunk, chunk), :],
                out_ref.at[pl.ds(spot, chunk), pl.ds(at, cols)],
                sem.at[r],
            )
        )
    for copy in copies:
        copy.start()
    done_ref[...] = jnp.zeros_like(done_ref)
    for copy in copies:
        copy.wait()


def place(name, base, side, first, second, token, out, width, at):
    carried = [] if out is None else [out]
    return pl.pallas_call(
        functools.partial(place_kernel, side, at),
        grid_spec=pltpu.PrefetchScalarGridSpec(
            num_scalar_prefetch=1,
            grid=(1,),
            in_specs=[VMEM, VMEM, ANY] + [ANY] * len(carried),
            out_specs=[ANY, VMEM],
            scratch_shapes=[pltpu.SemaphoreType.DMA((8,))],
        ),
        out_shape=[jax.ShapeDtypeStruct((width, width), F32), DONE],
        input_output_aliases={4: 0} if carried else {},
        compiler_params=pltpu.CompilerParams(vmem_limit_bytes=12 * 2**20),
        cost_estimate=COST,
        name=name,
    )(base, first, second, token, *carried)


def back_kernel(index, gp_ref, weight_ref, prop_ref, token_ref, *rest):
    out_ref, done_ref = rest[-2:]
    done_ref[...] = jnp.zeros_like(done_ref)
    part, cols = out_ref.shape
    j = pl.program_id(0)
    cut = pl.ds(pl.multiple_of(j * cols, cols), cols)
    mixed = lax.dot_general(
        gp_ref[index * part : (index + 1) * part, :],
        weight_ref[cut, :],
        (((1,), (1,)), ((), ())),
        preferred_element_type=F32,
    ).astype(BF16)
    for t in range(part // TILE):
        rows = slice(t * TILE, (t + 1) * TILE)
        tile = index * (part // TILE) + t
        out_ref[rows, :] = jnp.dot(prop_ref[tile], mixed[rows], preferred_element_type=F32).astype(BF16)


def back(name, gp, weight, prop_t, token, carried, index, count):
    rows, width = gp.shape
    part = rows // count
    cols = min(width, 512)
    extra = [] if carried is None else [carried]
    return pl.pallas_call(
        functools.partial(back_kernel, index),
        grid=(width // cols,),
        in_specs=[VMEM, VMEM, VMEM, ANY] + [ANY] * len(extra),
        out_specs=[pl.BlockSpec((part, cols), lambda j: (index, j)), VMEM],
        out_shape=[jax.ShapeDtypeStruct((rows, width), BF16), DONE],
        input_output_aliases={4: 0} if extra else {},
        compiler_params=pltpu.CompilerParams(vmem_limit_bytes=16 * 2**20),
        cost_estimate=COST,
        name=name,
    )(gp, weight, prop_t, token, *extra)


def bit_length(n):
    return n.bit_length() - 1


def per_device(groups, locs, features, weight, bias, cotangent, neighbours, edge_mask, cluster_ids, row_mask):
    width = features.shape[1]
    devices = groups * locs
    top, low = bit_length(devices), bit_length(locs)
    y_bits, x_bits, z_bits = list(range(1, low)), list(range(low, top - 2)), [top - 2, top - 1]
    axes = ("grp", "loc")
    number = lax.axis_index("grp") * locs + lax.axis_index("loc")

    def swap(value, pair):
        flip = lambda i: i ^ (1 << pair[i & 1])
        return lax.ppermute(value, axes, [(i, flip(i)) for i in range(devices)])

    core, first, second, near_z = (0, 0), (x_bits[0], y_bits[0]), (y_bits[0], x_bits[0]), (z_bits[0],) * 2
    halving = {"xyz": (first, second, near_z), "zxy": (near_z, first, second)}
    doubling = [(z_bits[1],) * 2] + [(b, b) for b in x_bits[1:] + y_bits[1:]]

    slots, line = [], {}
    for kind in sorted(set(k for _, k in GROUPS)):
        line[kind] = len(slots)
        for side in (1 - number % 2, number % 2):
            spot = side
            for pair in halving[kind]:
                spot = spot * 2 + jnp.where(side == 1, (number >> pair[1]) & 1, (number >> pair[0]) & 1)
            slots.append(spot)
    base = jnp.stack(slots).astype(jnp.int32)

    prop_t, mixed = propagate(features, neighbours, edge_mask, cluster_ids, row_mask)

    count = len(GROUPS)
    unit = width // sum(u for u, _ in GROUPS)
    starts, sizes, kinds = [], [], []
    for u, kind in GROUPS:
        starts.append(sum(sizes))
        sizes.append(u * unit)
        kinds.append(kind)
    fills = sum(e[0] == "f" for e in ORDER)

    terms = [None] * count
    got = [None] * count
    shares = [None] * count
    carried = []
    out = None
    grad_features = None
    token = prop_t
    end = width // 16

    for event in ORDER:
        what, g = event[0], int(event[1])
        stage = int(event[2]) if len(event) > 2 else 0
        if what == "g":
            act, gp, theirs, mine = layer_group(
                event, base, line[kinds[g]], mixed, weight, bias, cotangent, token, carried, starts[g], sizes[g]
            )
            carried = [act, gp]
            terms[g] = [mine, swap(theirs, core)]
            token = theirs
        elif what == "r" and stage < 3:
            n = (width // 2) >> (stage + 1)
            send, keep = join(
                event,
                terms[g],
                token,
                ((n + 8, ((0, n), (1, n))),),
                ((n, ((0, 0), (1, 0))), (8, ((0, 2 * n), (1, 2 * n)))),
            )
            terms[g] = [keep, swap(send, halving[kinds[g]][stage])]
            token = send
        elif what == "r":
            for pair in doubling:
                (total,) = join(event, terms[g], token, ((end + 8, ((0, 0), (1, 0))),))
                terms[g] = [total, swap(total, pair)]
                token = total
        elif what == "a":
            if stage == 0:
                total, shares[g] = join(
                    event, terms[g], token, ((end, ((0, 0), (1, 0))),), ((8, ((0, end), (1, end))),)
                )
            else:
                n = terms[g][0].shape[0]
                (total,) = join(event, terms[g], token, ((n, ((0, 0),)), (n, ((1, 0),))))
            terms[g] = [total, swap(total, halving[kinds[g]][2 - stage])]
            if stage == 2:
                got[g] = [swap(total, core)]
            token = total
        elif what == "c":
            late, _ = lax.optimization_barrier((terms[g][1], token))
            terms[g][1] = late
            got[g].append(swap(late, core))
        elif what == "w":
            pieces = terms[g] if stage == 0 else got[g]
            out, token = place(event, base, line[kinds[g]] + 1 - stage, *pieces, token, out, width, starts[g])
        else:
            grad_features, token = back(event, carried[1], weight, prop_t, token, grad_features, g, fills)
    grad_bias = jnp.concatenate([s[0] for s in shares])
    return carried[0], grad_features, out, grad_bias


def solution(mesh):
    rows = P(("grp", "loc"), None)
    flat = P(("grp", "loc"))
    in_specs = (rows, P(), P(), rows, rows, rows, flat, flat)
    out_specs = (rows, rows, P(), P())
    return jax.shard_map(
        functools.partial(per_device, mesh.shape["grp"], mesh.shape["loc"]),
        mesh=mesh,
        in_specs=in_specs,
        out_specs=out_specs,
        check_vma=False,
    )
```

time: 493 us -> 191 us (0.39)
  waiting for transfers between devices: 351 us -> 60.5 us
  Pallas kernels: 0 us -> 74 us
  starting transfers between devices: 0.12 us -> 49.9 us
  matrix products: 43.8 us -> 0 us
  other arithmetic: 30.7 us -> 0.68 us
  blocking collectives: 26.9 us -> 0 us
  local copies, waits for them, and re-layouts: 24.1 us -> 1.64 us
  between operations: 14.5 us -> 1.24 us
    psum x1 -> x0, waiting for transfers between devices: 159 us -> none  [per_device(): totals = lax.psum((shares[0], shares[1]), 'grp')]
    reduce_scatter x1 -> x0, waiting for transfers between devices: 127 us -> none  [per_device(): lax.psum_scatter(weight_term, 'loc', scatter_dimension=0, tiled=True)]
    pallas_call x0 -> x45, Pallas kernels: none -> 74 us  [the longest x4 24.5 us: layer_group(): pl.pallas_call(functools.partial(layer_kernel, start, line), grid_spec=pl...]
    all_gather x1 -> x0, waiting for transfers between devices: 63.9 us -> none  [per_device(): lax.all_gather(totals[0], 'loc', axis=0, tiled=True)]
    ppermute x0 -> x40, waiting for transfers between devices: none -> 60.5 us  [swap(): return lax.ppermute(value, axes, [(i, flip(i)) for i in range(devices)])]
    ppermute x0 -> x40, starting transfers between devices: none -> 49.9 us  [swap(): return lax.ppermute(value, axes, [(i, flip(i)) for i in range(devices)])]
    dot_general x5 -> x0, matrix products: 43.8 us -> none  [the longest x1 12.7 us: per_device(): pre = jnp.dot(mixed, weight, preferred_element_type=jnp.float32) + bias]
    reduce_sum x16 -> x0, other arithmetic: 23.8 us -> none  [the longest x8 22.4 us: build_tile(): edge_hits = jnp.sum(matched.astype(jnp.int32), axis=1)]
  transfers between devices with their start and end apart: 3 -> 40, of which waited for: 3 -> 20; matrix products, arithmetic and copies ran while one was open for 3% -> 1% of each run, Pallas kernels for 0% -> 32%
where the time goes in v1:
time: 191 us; the launch traced here: 188 us
  Pallas kernels  74 us (39%)
  waiting for transfers between devices  60.5 us (32%)
  starting transfers between devices  49.9 us (26%)
    ppermute x40, waiting for transfers between devices, swap(): return lax.ppermute(value, axes, [(i, flip(i)) for i in range(devices)])  60.5 us
    ppermute x40, starting transfers between devices, swap(): return lax.ppermute(value, axes, [(i, flip(i)) for i in range(devices)])  49.9 us
    pallas_call x4, Pallas kernels, layer_group(): pl.pallas_call(functools.partial(layer_kernel, start, line), grid_spec=pl...  24.5 us
    pallas_call x8, Pallas kernels, place(): pl.pallas_call(functools.partial(place_kernel, side, at), grid_spec=pltpu...  21.1 us
    pallas_call x4, Pallas kernels, back(): pl.pallas_call(functools.partial(back_kernel, index), grid=(width // cols...  17.5 us
    pallas_call x1, Pallas kernels, propagate(): pl.pallas_call(tile_kernel, grid=(tiles // each,), in_specs=[pl.BlockSpec...  6.33 us
    pallas_call x28, Pallas kernels, join(): pl.pallas_call(functools.partial(join_kernel, plan), in_specs=[VMEM] * le...  4.56 us
  transfers between devices with their start and end apart: 40, of which 20 were waited for; matrix products, arithmetic and copies ran while one was open for 1% of the time, Pallas kernels for 32%

profile of v1, /device:TPU:19, one launch (start us, length us, event | category | flops | bytes accessed | tf_op | source)
XLA Modules:
  0.0 188.0 jit_solution(6788504240885181704)
XLA Ops:
  0.8 6.3 %propagate.1 = (bf16[8,128,128]{2,1,0:T(8,128)(2,1)S(1)}, bf16[1024,2048]{1,0:T(8,128)(2,1)S(1)}) custom-call(s32[64,1024]{1,0:T(8,128)} %bitcast.21, s32[64,1024]{1,0:T(8,128)} %bitcast.22, s32[8,1,128]{2,1,0:T(1,128)} %bitcast.23, s32[8,1,128]{2,1,0:T(1,128)} %bitcast.24, bf16[1024,2048]{1,0:T(8,128)(2,1)} %features_ref.1), custom_call_target="tpu_custom_call" | custom-call | flops 4294967296 | bytes 4194304 | tf_op jit(solution)/shard_map/propagate/pallas_call | solution.py:69
  7.1 5.8 %g0.1 = (bf16[1024,2048]{1,0:T(8,128)(2,1)}, bf16[1024,2048]{1,0:T(8,128)(2,1)S(1)}, f32[1032,512]{1,0:T(8,128)S(1)}, f32[1032,512]{1,0:T(8,128)S(1)}) custom-call(s32[4]{0:T(128)S(1)} %pad_add_fusion.base_ref, bf16[1024,2048]{1,0:T(8,128)(2,1)S(1)} %get-tuple-element.81.mixed_ref, bf16[2048,2048]{1,0:T(8,128)(2,1)S(1)} %copy-done, f32[1,2048]{1,0:T(1,128)S(1)} %bitcast.13, ...), custom_call_target="tpu_custom_call" | custom-call | flops 24999999488 | bytes 1048576 | tf_op jit(solution)/shard_map/g0/pallas_call | solution.py:133
  13.7 6.1 %g1.1 = (bf16[1024,2048]{1,0:T(8,128)(2,1)}, bf16[1024,2048]{1,0:T(8,128)(2,1)S(1)}, f32[1032,512]{1,0:T(8,128)S(1)}, f32[1032,512]{1,0:T(8,128)S(1)}) custom-call(s32[4]{0:T(128)S(1)} %pad_add_fusion.base_ref, bf16[1024,2048]{1,0:T(8,128)(2,1)S(1)} %get-tuple-element.81.mixed_ref, ...), custom_call_target="tpu_custom_call", output_to_operand_aliasing={{0}: (6, {}), {1}: (7, {})} | custom-call | flops 24999999488 | bytes 1048576 | tf_op jit(solution)/shard_map/g1/pallas_call | solution.py:133
  21.5 2.6 %collective-permute-done.2.refs_1_ = f32[1032,512]{1,0:T(8,128)S(1)} collective-permute-done((f32[1032,512]{1,0:T(8,128)S(1)}, f32[1032,512]{1,0:T(8,128)S(1)}, u32[]{:S(2)}, u32[]{:S(2)}) %collective-permute-start.2) | collective-permute-done | bytes 2113568 | tf_op jit(solution)/shard_map/ppermute | solution.py:276
  25.8 6.1 %g2.1 = (bf16[1024,2048]{1,0:T(8,128)(2,1)}, bf16[1024,2048]{1,0:T(8,128)(2,1)S(1)}, f32[1032,512]{1,0:T(8,128)S(1)}, f32[1032,512]{1,0:T(8,128)S(1)}) custom-call(s32[4]{0:T(128)S(1)} %pad_add_fusion.base_ref, bf16[1024,2048]{1,0:T(8,128)(2,1)S(1)} %get-tuple-element.81.mixed_ref, ...), custom_call_target="tpu_custom_call", output_to_operand_aliasing={{0}: (6, {}), {1}: (7, {})} | custom-call | flops 24999999488 | bytes 1048576 | tf_op jit(solution)/shard_map/g2/pallas_call | solution.py:133
  32.4 2.0 %collective-permute-done.1.refs_1_ = f32[520,512]{1,0:T(8,128)S(1)} collective-permute-done((f32[520,512]{1,0:T(8,128)S(1)}, f32[520,512]{1,0:T(8,128)S(1)}, u32[]{:S(2)}, u32[]{:S(2)}) %collective-permute-start.1) | collective-permute-done | bytes 1064992 | tf_op jit(solution)/shard_map/ppermute | solution.py:276
  37.8 7.3 %collective-permute-done.3.refs_1_ = f32[264,512]{1,0:T(8,128)S(1)} collective-permute-done((f32[264,512]{1,0:T(8,128)S(1)}, f32[264,512]{1,0:T(8,128)S(1)}, u32[]{:S(2)}, u32[]{:S(2)}) %collective-permute-start.3) | collective-permute-done | bytes 540704 | tf_op jit(solution)/shard_map/ppermute | solution.py:276
  46.5 6.3 %g3.1 = (bf16[1024,2048]{1,0:T(8,128)(2,1)}, bf16[1024,2048]{1,0:T(8,128)(2,1)S(1)}, f32[1032,512]{1,0:T(8,128)S(1)}, f32[1032,512]{1,0:T(8,128)S(1)}) custom-call(s32[4]{0:T(128)S(1)} %pad_add_fusion.base_ref, bf16[1024,2048]{1,0:T(8,128)(2,1)S(1)} %get-tuple-element.81.mixed_ref, ...), custom_call_target="tpu_custom_call", output_to_operand_aliasing={{0}: (6, {}), {1}: (7, {})} | custom-call | flops 24999999488 | bytes 1048576 | tf_op jit(solution)/shard_map/g3/pallas_call | solution.py:133
  52.9 6.3 %collective-permute-start.5 = (f32[1032,512]{1,0:T(8,128)S(1)}, f32[1032,512]{1,0:T(8,128)S(1)}, u32[]{:S(2)}, u32[]{:S(2)}) collective-permute-start(f32[1032,512]{1,0:T(8,128)S(1)} %get-tuple-element.105.refs_2_), channel_id=1, source_target_pairs={{0,1},{1,0},{2,3},{3,2},{4,5},{5,4},{6,7},{7,6},{8,9},{9,8},{10,11... | collective-permute-start | bytes 6340616 | tf_op jit(solution)/shard_map/ppermute | solution.py:276
  64.6 7.8 %collective-permute-done.11.refs_1_ = f32[264,512]{1,0:T(8,128)S(1)} collective-permute-done((f32[264,512]{1,0:T(8,128)S(1)}, f32[264,512]{1,0:T(8,128)S(1)}, u32[]{:S(2)}, u32[]{:S(2)}) %collective-permute-start.11) | collective-permute-done | bytes 540704 | tf_op jit(solution)/shard_map/ppermute | solution.py:276
  72.5 2.6 %collective-permute-done.10.refs_1_ = f32[264,512]{1,0:T(8,128)S(1)} collective-permute-done((f32[264,512]{1,0:T(8,128)S(1)}, f32[264,512]{1,0:T(8,128)S(1)}, u32[]{:S(2)}, u32[]{:S(2)}) %collective-permute-start.10) | collective-permute-done | bytes 540704 | tf_op jit(solution)/shard_map/ppermute | solution.py:276
  77.4 5.0 %collective-permute-done.12.refs_1_ = f32[136,512]{1,0:T(8,128)S(1)} collective-permute-done((f32[136,512]{1,0:T(8,128)S(1)}, f32[136,512]{1,0:T(8,128)S(1)}, u32[]{:S(2)}, u32[]{:S(2)}) %collective-permute-start.12) | collective-permute-done | bytes 278560 | tf_op jit(solution)/shard_map/ppermute | solution.py:276
  82.5 5.5 %collective-permute-done.9.refs_1_ = f32[520,512]{1,0:T(8,128)S(1)} collective-permute-done((f32[520,512]{1,0:T(8,128)S(1)}, f32[520,512]{1,0:T(8,128)S(1)}, u32[]{:S(2)}, u32[]{:S(2)}) %collective-permute-start.9) | collective-permute-done | bytes 1064992 | tf_op jit(solution)/shard_map/ppermute | solution.py:276
  89.9 2.3 %collective-permute-start.21 = (f32[136,512]{1,0:T(8,128)S(1)}, f32[136,512]{1,0:T(8,128)S(1)}, u32[]{:S(2)}, u32[]{:S(2)}) collective-permute-start(f32[136,512]{1,0:T(8,128)S(1)} %r13.1.refs_2_.refs_0_), channel_id=1, source_target_pairs={{0,16},{1,17},{2,18},{3,19},{4,20},{5,21},{6,22},{7,23},{8,24},{9,... | collective-permute-start | bytes 835592 | tf_op jit(solution)/shard_map/ppermute | solution.py:276
  92.2 4.6 %collective-permute-done.14.refs_1_ = f32[264,512]{1,0:T(8,128)S(1)} collective-permute-done((f32[264,512]{1,0:T(8,128)S(1)}, f32[264,512]{1,0:T(8,128)S(1)}, u32[]{:S(2)}, u32[]{:S(2)}) %collective-permute-start.14) | collective-permute-done | bytes 540704 | tf_op jit(solution)/shard_map/ppermute | solution.py:276
  98.4 3.9 %collective-permute-done.18.refs_1_ = f32[256,512]{1,0:T(8,128)S(1)} collective-permute-done((f32[256,512]{1,0:T(8,128)S(1)}, f32[256,512]{1,0:T(8,128)S(1)}, u32[]{:S(2)}, u32[]{:S(2)}) %collective-permute-start.18) | collective-permute-done | bytes 524320 | tf_op jit(solution)/shard_map/ppermute | solution.py:276
  104.7 4.1 %collective-permute-start.27 = (f32[512,512]{1,0:T(8,128)}, f32[512,512]{1,0:T(8,128)}, u32[]{:S(2)}, u32[]{:S(2)}) collective-permute-start(f32[512,512]{1,0:T(8,128)} %a02.1.refs_2_.first_ref), channel_id=1, source_target_pairs={{0,1},{1,0},{2,3},{3,2},{4,5},{5,4},{6,7},{7,6},{8,9},{9,8},{10,11... | collective-permute-start | bytes 3145736 | tf_op jit(solution)/shard_map/ppermute | solution.py:276
  111.3 5.3 %collective-permute-done.24.refs_1_ = f32[128,512]{1,0:T(8,128)S(1)} collective-permute-done((f32[128,512]{1,0:T(8,128)S(1)}, f32[128,512]{1,0:T(8,128)S(1)}, u32[]{:S(2)}, u32[]{:S(2)}) %collective-permute-start.24) | collective-permute-done | bytes 262176 | tf_op jit(solution)/shard_map/ppermute | solution.py:276
  117.6 3.1 %w00.1 = (f32[2048,2048]{1,0:T(8,128)}, f32[8,128]{1,0:T(8,128)S(1)}) custom-call(s32[4]{0:T(128)S(1)} %pad_add_fusion.base_ref, f32[512,512]{1,0:T(8,128)} %a02.1.refs_2_.first_ref, f32[512,512]{1,0:T(8,128)S(1)} %collective-permute-done.23.second_ref, f32[256,512]{1,0:T(8,128)S(1)} %a21.1.token_ref.refs_0_), custom_call_target="tpu_custom_call" | custom-call | flops 24999999488 | bytes 1048576 | tf_op jit(solution)/shard_map/w00/pallas_call | solution.py:209
  120.7 14.7 %collective-permute-start.28 = (f32[512,512]{1,0:T(8,128)S(1)}, f32[512,512]{1,0:T(8,128)S(1)}, u32[]{:S(2)}, u32[]{:S(2)}) collective-permute-start(f32[512,512]{1,0:T(8,128)S(1)} %collective-permute-done.23.second_ref), channel_id=1, source_target_pairs={{0,1},{1,0},{2,3},{3,2},{4,5},{5,4},{6,7},{7,6},{8,9},{9,8},{10,11... | collective-permute-start | bytes 3145736 | tf_op jit(solution)/shard_map/ppermute | solution.py:276
  137.7 3.1 %w01.1 = (f32[2048,2048]{1,0:T(8,128)}, f32[8,128]{1,0:T(8,128)S(1)}) custom-call(s32[4]{0:T(128)S(1)} %pad_add_fusion.base_ref, f32[512,512]{1,0:T(8,128)} %collective-permute-done.27.first_ref, f32[512,512]{1,0:T(8,128)S(1)} %collective-permute-done.28.second_ref, ...), custom_call_target="tpu_custom_call", output_to_operand_aliasing={{0}: (4, {})} | custom-call | flops 24999999488 | bytes 1048576 | tf_op jit(solution)/shard_map/w01/pallas_call | solution.py:209
  141.6 1.9 %collective-permute-done.25.refs_1_ = f32[128,512]{1,0:T(8,128)S(1)} collective-permute-done((f32[128,512]{1,0:T(8,128)S(1)}, f32[128,512]{1,0:T(8,128)S(1)}, u32[]{:S(2)}, u32[]{:S(2)}) %collective-permute-start.25) | collective-permute-done | bytes 262176 | tf_op jit(solution)/shard_map/ppermute | solution.py:276
  147.5 4.4 %f0.1 = (bf16[1024,2048]{1,0:T(8,128)(2,1)}, f32[8,128]{1,0:T(8,128)S(1)}) custom-call(bf16[1024,2048]{1,0:T(8,128)(2,1)S(1)} %get-tuple-element.103.gp_ref, bf16[2048,2048]{1,0:T(8,128)(2,1)S(1)} %copy-done, bf16[8,128,128]{2,1,0:T(8,128)(2,1)S(1)} %get-tuple-element.82.token_ref.prop_ref, f32[512,512]{1,0:T(8,128)} %a12.1.token_ref.first_ref), custom_call_target="tpu_custom_call" | custom-call | flops 24999999488 | bytes 1048576 | tf_op jit(solution)/shard_map/f0/pallas_call | solution.py:249
  151.9 4.4 %f1.1 = (bf16[1024,2048]{1,0:T(8,128)(2,1)}, f32[8,128]{1,0:T(8,128)S(1)}) custom-call(bf16[1024,2048]{1,0:T(8,128)(2,1)S(1)} %get-tuple-element.103.gp_ref, bf16[2048,2048]{1,0:T(8,128)(2,1)S(1)} %copy-done, bf16[8,128,128]{2,1,0:T(8,128)(2,1)S(1)} %get-tuple-element.82.token_ref.prop_ref, ...), custom_call_target="tpu_custom_call", output_to_operand_aliasing={{0}: (4, {})} | custom-call | flops 24999999488 | bytes 1048576 | tf_op jit(solution)/shard_map/f1/pallas_call | solution.py:249
  156.3 4.5 %collective-permute-done.31.second_ref = f32[512,512]{1,0:T(8,128)S(1)} collective-permute-done((f32[512,512]{1,0:T(8,128)S(1)}, f32[512,512]{1,0:T(8,128)S(1)}, u32[]{:S(2)}, u32[]{:S(2)}) %collective-permute-start.31) | collective-permute-done | bytes 1048608 | tf_op jit(solution)/shard_map/ppermute | solution.py:276
  161.7 4.4 %f2.1 = (bf16[1024,2048]{1,0:T(8,128)(2,1)}, f32[8,128]{1,0:T(8,128)S(1)}) custom-call(bf16[1024,2048]{1,0:T(8,128)(2,1)S(1)} %get-tuple-element.103.gp_ref, bf16[2048,2048]{1,0:T(8,128)(2,1)S(1)} %copy-done, bf16[8,128,128]{2,1,0:T(8,128)(2,1)S(1)} %get-tuple-element.82.token_ref.prop_ref, ...), custom_call_target="tpu_custom_call", output_to_operand_aliasing={{0}: (4, {})} | custom-call | flops 24999999488 | bytes 1048576 | tf_op jit(solution)/shard_map/f2/pallas_call | solution.py:249
  166.1 1.9 %w21.1 = (f32[2048,2048]{1,0:T(8,128)}, f32[8,128]{1,0:T(8,128)S(1)}) custom-call(s32[4]{0:T(128)S(1)} %pad_add_fusion.base_ref, f32[512,512]{1,0:T(8,128)S(1)} %collective-permute-done.30.first_ref, f32[512,512]{1,0:T(8,128)S(1)} %collective-permute-done.33.second_ref, f32[8,128]{1,0:T(8,128)S(1)} %get-tuple-element.136.token_ref, ...), custom_call_target="tpu_custom_call", output_to_operand_aliasing={{0}: (4, {})} | custom-call | flops 24999999488 | bytes 1048576 | tf_op jit(solution)/shard_map/w21/pallas_call | solution.py:209
  168.5 4.4 %f3.1 = (bf16[1024,2048]{1,0:T(8,128)(2,1)}, f32[8,128]{1,0:T(8,128)S(1)}) custom-call(bf16[1024,2048]{1,0:T(8,128)(2,1)S(1)} %get-tuple-element.103.gp_ref, bf16[2048,2048]{1,0:T(8,128)(2,1)S(1)} %copy-done, bf16[8,128,128]{2,1,0:T(8,128)(2,1)S(1)} %get-tuple-element.82.token_ref.prop_ref, ...), custom_call_target="tpu_custom_call", output_to_operand_aliasing={{0}: (4, {})} | custom-call | flops 24999999488 | bytes 1048576 | tf_op jit(solution)/shard_map/f3/pallas_call | solution.py:249
  173.2 3.5 %w10.1 = (f32[2048,2048]{1,0:T(8,128)}, f32[8,128]{1,0:T(8,128)S(1)}) custom-call(s32[4]{0:T(128)S(1)} %pad_add_fusion.base_ref, f32[512,512]{1,0:T(8,128)} %a12.1.token_ref.first_ref, f32[512,512]{1,0:T(8,128)} %collective-permute-done.37.second_ref, f32[8,128]{1,0:T(8,128)S(1)} %get-tuple-element.141.token_ref, ...), custom_call_target="tpu_custom_call", output_to_operand_aliasing={{0}: (4, {})} | custom-call | flops 24999999488 | bytes 1048576 | tf_op jit(solution)/shard_map/w10/pallas_call | solution.py:209
  176.7 3.1 %w11.1 = (f32[2048,2048]{1,0:T(8,128)}, f32[8,128]{1,0:T(8,128)S(1)}) custom-call(s32[4]{0:T(128)S(1)} %pad_add_fusion.base_ref, f32[512,512]{1,0:T(8,128)} %collective-permute-done.36.first_ref, f32[512,512]{1,0:T(8,128)S(1)} %collective-permute-done.38.second_ref, f32[8,128]{1,0:T(8,128)S(1)} %get-tuple-element.144.token_ref, ...), custom_call_target="tpu_custom_call", output_to_operand_aliasing={{0}: (4, {})} | custom-call | flops 24999999488 | bytes 1048576 | tf_op jit(solution)/shard_map/w11/pallas_call | solution.py:209
  179.8 1.9 %w20.1 = (f32[2048,2048]{1,0:T(8,128)}, f32[8,128]{1,0:T(8,128)S(1)}) custom-call(s32[4]{0:T(128)S(1)} %pad_add_fusion.base_ref, f32[512,512]{1,0:T(8,128)S(1)} %a22.1.refs_2_.first_ref, f32[512,512]{1,0:T(8,128)S(1)} %collective-permute-done.31.second_ref, f32[8,128]{1,0:T(8,128)S(1)} %get-tuple-element.146.token_ref, ...), custom_call_target="tpu_custom_call", output_to_operand_aliasing={{0}: (4, {})} | custom-call | flops 24999999488 | bytes 1048576 | tf_op jit(solution)/shard_map/w20/pallas_call | solution.py:209
  185.3 2.5 %w31.1 = (f32[2048,2048]{1,0:T(8,128)}, f32[8,128]{1,0:T(8,128)}) custom-call(s32[4]{0:T(128)S(1)} %pad_add_fusion.base_ref, f32[512,512]{1,0:T(8,128)S(1)} %collective-permute-done.34.first_ref, f32[512,512]{1,0:T(8,128)S(1)} %collective-permute-done.39.second_ref, f32[8,128]{1,0:T(8,128)S(1)} %get-tuple-element.151.token_ref, ...), custom_call_target="tpu_custom_call", output_to_operand_aliasing={{0}: (4, {})} | custom-call | flops 24999999488 | bytes 1048576 | tf_op jit(solution)/shard_map/w31/pallas_call | solution.py:209
  (107 shorter events, 38.9 us)
Async XLA Ops:
  20.2 14.2 %collective-permute-start.1 = (f32[520,512]{1,0:T(8,128)S(1)}, f32[520,512]{1,0:T(8,128)S(1)}, u32[]{:S(2)}, u32[]{:S(2)}) collective-permute-start(f32[520,512]{1,0:T(8,128)S(1)} %get-tuple-element.89.refs_2_), channel_id=1, source_target_pairs={{0,4},{1,3},{2,6},{3,1},{4,0},{5,7},{6,2},{7,5},{8,12},{9,11},{10,... | collective-permute-start | bytes 3194888 | tf_op jit(solution)/shard_map/ppermute | solution.py:276
  24.4 34.7 %collective-permute-start.8 = (f32[520,512]{1,0:T(8,128)S(1)}, f32[520,512]{1,0:T(8,128)S(1)}, u32[]{:S(2)}, u32[]{:S(2)}) collective-permute-start(f32[520,512]{1,0:T(8,128)S(1)} %get-tuple-element.91.token_ref), channel_id=1, source_target_pairs={{0,8},{1,9},{2,10},{3,11},{4,12},{5,13},{6,14},{7,15},{8,0},{9,1},... | collective-permute-start | bytes 3194888 | tf_op jit(solution)/shard_map/ppermute | solution.py:276
  34.5 10.6 %collective-permute-start.3 = (f32[264,512]{1,0:T(8,128)S(1)}, f32[264,512]{1,0:T(8,128)S(1)}, u32[]{:S(2)}, u32[]{:S(2)}) collective-permute-start(f32[264,512]{1,0:T(8,128)S(1)} %get-tuple-element.96.refs_2_), channel_id=1, source_target_pairs={{0,2},{1,5},{2,0},{3,7},{4,6},{5,1},{6,4},{7,3},{8,10},{9,13},{10,... | collective-permute-start | bytes 1622024 | tf_op jit(solution)/shard_map/ppermute | solution.py:276
  36.5 24.1 %collective-permute-start.7 = (f32[520,512]{1,0:T(8,128)S(1)}, f32[520,512]{1,0:T(8,128)S(1)}, u32[]{:S(2)}, u32[]{:S(2)}) collective-permute-start(f32[520,512]{1,0:T(8,128)S(1)} %get-tuple-element.98.refs_2_), channel_id=1, source_target_pairs={{0,4},{1,3},{2,6},{3,1},{4,0},{5,7},{6,2},{7,5},{8,12},{9,11},{10,... | collective-permute-start | bytes 3194888 | tf_op jit(solution)/shard_map/ppermute | solution.py:276
  45.2 15.9 %collective-permute-start.6 = (f32[136,512]{1,0:T(8,128)S(1)}, f32[136,512]{1,0:T(8,128)S(1)}, u32[]{:S(2)}, u32[]{:S(2)}) collective-permute-start(f32[136,512]{1,0:T(8,128)S(1)} %get-tuple-element.99.token_ref), channel_id=1, source_target_pairs={{0,8},{1,9},{2,10},{3,11},{4,12},{5,13},{6,14},{7,15},{8,0},{9,1},... | collective-permute-start | bytes 835592 | tf_op jit(solution)/shard_map/ppermute | solution.py:276
  52.9 10.1 %collective-permute-start.5 = (f32[1032,512]{1,0:T(8,128)S(1)}, f32[1032,512]{1,0:T(8,128)S(1)}, u32[]{:S(2)}, u32[]{:S(2)}) collective-permute-start(f32[1032,512]{1,0:T(8,128)S(1)} %get-tuple-element.105.refs_2_), channel_id=1, source_target_pairs={{0,1},{1,0},{2,3},{3,2},{4,5},{5,4},{6,7},{7,6},{8,9},{9,8},{10,11... | collective-permute-start | bytes 6340616 | tf_op jit(solution)/shard_map/ppermute | solution.py:276
  59.3 13.1 %collective-permute-start.11 = (f32[264,512]{1,0:T(8,128)S(1)}, f32[264,512]{1,0:T(8,128)S(1)}, u32[]{:S(2)}, u32[]{:S(2)}) collective-permute-start(f32[264,512]{1,0:T(8,128)S(1)} %get-tuple-element.109.refs_2_), channel_id=1, source_target_pairs={{0,4},{1,3},{2,6},{3,1},{4,0},{5,7},{6,2},{7,5},{8,12},{9,11},{10,... | collective-permute-start | bytes 1622024 | tf_op jit(solution)/shard_map/ppermute | solution.py:276
  60.8 14.4 %collective-permute-start.10 = (f32[264,512]{1,0:T(8,128)S(1)}, f32[264,512]{1,0:T(8,128)S(1)}, u32[]{:S(2)}, u32[]{:S(2)}) collective-permute-start(f32[264,512]{1,0:T(8,128)S(1)} %get-tuple-element.110.refs_2_), channel_id=1, source_target_pairs={{0,2},{1,5},{2,0},{3,7},{4,6},{5,1},{6,4},{7,3},{8,10},{9,13},{10,... | collective-permute-start | bytes 1622024 | tf_op jit(solution)/shard_map/ppermute | solution.py:276
  61.1 14.1 %collective-permute-start.13 = (f32[136,512]{1,0:T(8,128)S(1)}, f32[136,512]{1,0:T(8,128)S(1)}, u32[]{:S(2)}, u32[]{:S(2)}) collective-permute-start(f32[136,512]{1,0:T(8,128)S(1)} %r03.1.refs_2_.refs_0_), channel_id=1, source_target_pairs={{0,16},{1,17},{2,18},{3,19},{4,20},{5,21},{6,22},{7,23},{8,24},{9,... | collective-permute-start | bytes 835592 | tf_op jit(solution)/shard_map/ppermute | solution.py:276
  63.3 24.8 %collective-permute-start.9 = (f32[520,512]{1,0:T(8,128)S(1)}, f32[520,512]{1,0:T(8,128)S(1)}, u32[]{:S(2)}, u32[]{:S(2)}) collective-permute-start(f32[520,512]{1,0:T(8,128)S(1)} %get-tuple-element.112.refs_2_), channel_id=1, source_target_pairs={{0,4},{1,3},{2,6},{3,1},{4,0},{5,7},{6,2},{7,5},{8,12},{9,11},{10,... | collective-permute-start | bytes 3194888 | tf_op jit(solution)/shard_map/ppermute | solution.py:276
  72.5 17.4 %collective-permute-start.15 = (f32[136,512]{1,0:T(8,128)S(1)}, f32[136,512]{1,0:T(8,128)S(1)}, u32[]{:S(2)}, u32[]{:S(2)}) collective-permute-start(f32[136,512]{1,0:T(8,128)S(1)} %get-tuple-element.115.refs_2_), channel_id=1, source_target_pairs={{0,2},{1,5},{2,0},{3,7},{4,6},{5,1},{6,4},{7,3},{8,10},{9,13},{10,... | collective-permute-start | bytes 835592 | tf_op jit(solution)/shard_map/ppermute | solution.py:276
  75.3 13.5 %collective-permute-start.16 = (f32[128,512]{1,0:T(8,128)S(1)}, f32[128,512]{1,0:T(8,128)S(1)}, u32[]{:S(2)}, u32[]{:S(2)}) collective-permute-start(f32[128,512]{1,0:T(8,128)S(1)} %get-tuple-element.118.refs_2_.refs_0_), channel_id=1, source_target_pairs={{0,8},{1,9},{2,10},{3,11},{4,12},{5,13},{6,14},{7,15},{8,0},{9,1},... | collective-permute-start | bytes 786440 | tf_op jit(solution)/shard_map/ppermute | solution.py:276
  82.4 14.5 %collective-permute-start.19 = (f32[136,512]{1,0:T(8,128)S(1)}, f32[136,512]{1,0:T(8,128)S(1)}, u32[]{:S(2)}, u32[]{:S(2)}) collective-permute-start(f32[136,512]{1,0:T(8,128)S(1)} %r23.1.refs_2_.refs_0_), channel_id=1, source_target_pairs={{0,16},{1,17},{2,18},{3,19},{4,20},{5,21},{6,22},{7,23},{8,24},{9,... | collective-permute-start | bytes 835592 | tf_op jit(solution)/shard_map/ppermute | solution.py:276
  88.2 8.6 %collective-permute-start.14 = (f32[264,512]{1,0:T(8,128)S(1)}, f32[264,512]{1,0:T(8,128)S(1)}, u32[]{:S(2)}, u32[]{:S(2)}) collective-permute-start(f32[264,512]{1,0:T(8,128)S(1)} %get-tuple-element.120.refs_2_), channel_id=1, source_target_pairs={{0,2},{1,5},{2,0},{3,7},{4,6},{5,1},{6,4},{7,3},{8,10},{9,13},{10,... | collective-permute-start | bytes 1622024 | tf_op jit(solution)/shard_map/ppermute | solution.py:276
  88.9 13.5 %collective-permute-start.18 = (f32[256,512]{1,0:T(8,128)S(1)}, f32[256,512]{1,0:T(8,128)S(1)}, u32[]{:S(2)}, u32[]{:S(2)}) collective-permute-start(f32[256,512]{1,0:T(8,128)S(1)} %a01.1.refs_2_.refs_0_), channel_id=1, source_target_pairs={{0,2},{1,5},{2,0},{3,7},{4,6},{5,1},{6,4},{7,3},{8,10},{9,13},{10,... | collective-permute-start | bytes 1572872 | tf_op jit(solution)/shard_map/ppermute | solution.py:276
  89.9 21.1 %collective-permute-start.21 = (f32[136,512]{1,0:T(8,128)S(1)}, f32[136,512]{1,0:T(8,128)S(1)}, u32[]{:S(2)}, u32[]{:S(2)}) collective-permute-start(f32[136,512]{1,0:T(8,128)S(1)} %r13.1.refs_2_.refs_0_), channel_id=1, source_target_pairs={{0,16},{1,17},{2,18},{3,19},{4,20},{5,21},{6,22},{7,23},{8,24},{9,... | collective-permute-start | bytes 835592 | tf_op jit(solution)/shard_map/ppermute | solution.py:276
  96.8 14.1 %collective-permute-start.17 = (f32[136,512]{1,0:T(8,128)S(1)}, f32[136,512]{1,0:T(8,128)S(1)}, u32[]{:S(2)}, u32[]{:S(2)}) collective-permute-start(f32[136,512]{1,0:T(8,128)S(1)} %get-tuple-element.123.refs_2_), channel_id=1, source_target_pairs={{0,8},{1,9},{2,10},{3,11},{4,12},{5,13},{6,14},{7,15},{8,0},{9,1},... | collective-permute-start | bytes 835592 | tf_op jit(solution)/shard_map/ppermute | solution.py:276
  96.9 19.6 %collective-permute-start.24 = (f32[128,512]{1,0:T(8,128)S(1)}, f32[128,512]{1,0:T(8,128)S(1)}, u32[]{:S(2)}, u32[]{:S(2)}) collective-permute-start(f32[128,512]{1,0:T(8,128)S(1)} %get-tuple-element.124.refs_2_.refs_0_), channel_id=1, source_target_pairs={{0,8},{1,9},{2,10},{3,11},{4,12},{5,13},{6,14},{7,15},{8,0},{9,1},... | collective-permute-start | bytes 786440 | tf_op jit(solution)/shard_map/ppermute | solution.py:276
  103.4 14.2 %collective-permute-start.23 = (f32[512,512]{1,0:T(8,128)}, f32[512,512]{1,0:T(8,128)S(1)}, u32[]{:S(2)}, u32[]{:S(2)}) collective-permute-start(f32[512,512]{1,0:T(8,128)} %a02.1.refs_2_.first_ref), channel_id=1, source_target_pairs={{0,4},{1,3},{2,6},{3,1},{4,0},{5,7},{6,2},{7,5},{8,12},{9,11},{10,... | collective-permute-start | bytes 3145736 | tf_op jit(solution)/shard_map/ppermute | solution.py:276
  104.7 32.1 %collective-permute-start.27 = (f32[512,512]{1,0:T(8,128)}, f32[512,512]{1,0:T(8,128)}, u32[]{:S(2)}, u32[]{:S(2)}) collective-permute-start(f32[512,512]{1,0:T(8,128)} %a02.1.refs_2_.first_ref), channel_id=1, source_target_pairs={{0,1},{1,0},{2,3},{3,2},{4,5},{5,4},{6,7},{7,6},{8,9},{9,8},{10,11... | collective-permute-start | bytes 3145736 | tf_op jit(solution)/shard_map/ppermute | solution.py:276
  110.9 24.6 %collective-permute-start.20 = (f32[136,512]{1,0:T(8,128)S(1)}, f32[136,512]{1,0:T(8,128)S(1)}, u32[]{:S(2)}, u32[]{:S(2)}) collective-permute-start(f32[136,512]{1,0:T(8,128)S(1)} %r33.1.refs_2_.refs_0_), channel_id=1, source_target_pairs={{0,16},{1,17},{2,18},{3,19},{4,20},{5,21},{6,22},{7,23},{8,24},{9,... | collective-permute-start | bytes 835592 | tf_op jit(solution)/shard_map/ppermute | solution.py:276
  111.0 24.3 %collective-permute-start.22 = (f32[128,512]{1,0:T(8,128)S(1)}, f32[128,512]{1,0:T(8,128)S(1)}, u32[]{:S(2)}, u32[]{:S(2)}) collective-permute-start(f32[128,512]{1,0:T(8,128)S(1)} %get-tuple-element.125.refs_2_.refs_0_), channel_id=1, source_target_pairs={{0,2},{1,5},{2,0},{3,7},{4,6},{5,1},{6,4},{7,3},{8,10},{9,13},{10,... | collective-permute-start | bytes 786440 | tf_op jit(solution)/shard_map/ppermute | solution.py:276
  116.6 24.2 %collective-permute-start.26 = (f32[256,512]{1,0:T(8,128)S(1)}, f32[256,512]{1,0:T(8,128)S(1)}, u32[]{:S(2)}, u32[]{:S(2)}) collective-permute-start(f32[256,512]{1,0:T(8,128)S(1)} %a21.1.token_ref.refs_0_), channel_id=1, source_target_pairs={{0,2},{1,5},{2,0},{3,7},{4,6},{5,1},{6,4},{7,3},{8,10},{9,13},{10,... | collective-permute-start | bytes 1572872 | tf_op jit(solution)/shard_map/ppermute | solution.py:276
  120.7 17.0 %collective-permute-start.28 = (f32[512,512]{1,0:T(8,128)S(1)}, f32[512,512]{1,0:T(8,128)S(1)}, u32[]{:S(2)}, u32[]{:S(2)}) collective-permute-start(f32[512,512]{1,0:T(8,128)S(1)} %collective-permute-done.23.second_ref), channel_id=1, source_target_pairs={{0,1},{1,0},{2,3},{3,2},{4,5},{5,4},{6,7},{7,6},{8,9},{9,8},{10,11... | collective-permute-start | bytes 3145736 | tf_op jit(solution)/shard_map/ppermute | solution.py:276
  135.4 9.3 %collective-permute-start.32 = (f32[256,512]{1,0:T(8,128)S(1)}, f32[256,512]{1,0:T(8,128)S(1)}, u32[]{:S(2)}, u32[]{:S(2)}) collective-permute-start(f32[256,512]{1,0:T(8,128)S(1)} %a11.1.refs_2_.refs_0_), channel_id=1, source_target_pairs={{0,4},{1,3},{2,6},{3,1},{4,0},{5,7},{6,2},{7,5},{8,12},{9,11},{10,... | collective-permute-start | bytes 1572872 | tf_op jit(solution)/shard_map/ppermute | solution.py:276
  140.9 19.9 %collective-permute-start.31 = (f32[512,512]{1,0:T(8,128)S(1)}, f32[512,512]{1,0:T(8,128)S(1)}, u32[]{:S(2)}, u32[]{:S(2)}) collective-permute-start(f32[512,512]{1,0:T(8,128)S(1)} %a22.1.refs_2_.first_ref), channel_id=1, source_target_pairs={{0,4},{1,3},{2,6},{3,1},{4,0},{5,7},{6,2},{7,5},{8,12},{9,11},{10,... | collective-permute-start | bytes 3145736 | tf_op jit(solution)/shard_map/ppermute | solution.py:276
  141.0 25.1 %collective-permute-start.30 = (f32[512,512]{1,0:T(8,128)S(1)}, f32[512,512]{1,0:T(8,128)S(1)}, u32[]{:S(2)}, u32[]{:S(2)}) collective-permute-start(f32[512,512]{1,0:T(8,128)S(1)} %a22.1.refs_2_.first_ref), channel_id=1, source_target_pairs={{0,1},{1,0},{2,3},{3,2},{4,5},{5,4},{6,7},{7,6},{8,9},{9,8},{10,11... | collective-permute-start | bytes 3145736 | tf_op jit(solution)/shard_map/ppermute | solution.py:276
  143.6 24.5 %collective-permute-start.29 = (f32[256,512]{1,0:T(8,128)S(1)}, f32[256,512]{1,0:T(8,128)S(1)}, u32[]{:S(2)}, u32[]{:S(2)}) collective-permute-start(f32[256,512]{1,0:T(8,128)S(1)} %a31.1.refs_2_.refs_0_), channel_id=1, source_target_pairs={{0,2},{1,5},{2,0},{3,7},{4,6},{5,1},{6,4},{7,3},{8,10},{9,13},{10,... | collective-permute-start | bytes 1572872 | tf_op jit(solution)/shard_map/ppermute | solution.py:276
  145.8 27.1 %collective-permute-start.37 = (f32[512,512]{1,0:T(8,128)}, f32[512,512]{1,0:T(8,128)}, u32[]{:S(2)}, u32[]{:S(2)}) collective-permute-start(f32[512,512]{1,0:T(8,128)} %a12.1.token_ref.first_ref), channel_id=1, source_target_pairs={{0,8},{1,9},{2,10},{3,11},{4,12},{5,13},{6,14},{7,15},{8,0},{9,1},... | collective-permute-start | bytes 3145736 | tf_op jit(solution)/shard_map/ppermute | solution.py:276
  146.1 30.5 %collective-permute-start.36 = (f32[512,512]{1,0:T(8,128)}, f32[512,512]{1,0:T(8,128)}, u32[]{:S(2)}, u32[]{:S(2)}) collective-permute-start(f32[512,512]{1,0:T(8,128)} %a12.1.token_ref.first_ref), channel_id=1, source_target_pairs={{0,1},{1,0},{2,3},{3,2},{4,5},{5,4},{6,7},{7,6},{8,9},{9,8},{10,11... | collective-permute-start | bytes 3145736 | tf_op jit(solution)/shard_map/ppermute | solution.py:276
  168.1 14.0 %collective-permute-start.35 = (f32[512,512]{1,0:T(8,128)S(1)}, f32[512,512]{1,0:T(8,128)S(1)}, u32[]{:S(2)}, u32[]{:S(2)}) collective-permute-start(f32[512,512]{1,0:T(8,128)S(1)} %a32.1.token_ref.first_ref), channel_id=1, source_target_pairs={{0,4},{1,3},{2,6},{3,1},{4,0},{5,7},{6,2},{7,5},{8,12},{9,11},{10,... | collective-permute-start | bytes 3145736 | tf_op jit(solution)/shard_map/ppermute | solution.py:276
  168.2 16.7 %collective-permute-start.34 = (f32[512,512]{1,0:T(8,128)S(1)}, f32[512,512]{1,0:T(8,128)S(1)}, u32[]{:S(2)}, u32[]{:S(2)}) collective-permute-start(f32[512,512]{1,0:T(8,128)S(1)} %a32.1.token_ref.first_ref), channel_id=1, source_target_pairs={{0,1},{1,0},{2,3},{3,2},{4,5},{5,4},{6,7},{7,6},{8,9},{9,8},{10,11... | collective-permute-start | bytes 3145736 | tf_op jit(solution)/shard_map/ppermute | solution.py:276
  (12 other events, 57.0 us)

commit v2 on v1

v2 whole, which is shorter than its diff:
```python
import functools

import jax
import jax.numpy as jnp
from jax import lax
from jax.experimental import pallas as pl
from jax.experimental.pallas import tpu as pltpu
from jax.sharding import PartitionSpec as P

TILE = 128
BF16 = jnp.bfloat16
F32 = jnp.float32

GROUPS = ((2, "xyz"), (2, "zxy"), (2, "yxz"), (2, "xyz"))
ORDER = (
    "g0", "g1", "r00", "r10", "g2", "r01", "r20", "g3", "r02", "f0", "r11+c3_", "r03", "r21", "r30", "r12",
    "r22", "r13+R03", "a00", "r31", "r23", "a10", "r32", "a01", "f1", "a20+A10", "a11", "r33", "a02", "f2",
    "a30+A11+A20+C00", "a21", "a12+A02", "f3", "a31+C10", "c0", "a22", "a32+C01", "w01+C20", "w00", "c1",
    "w10+C30", "w11", "c2", "w20", "w21", "c3", "w30", "w31",
)

COST = pl.CostEstimate(flops=25 * 10**9, bytes_accessed=2**20, transcendentals=0)
DONE = jax.ShapeDtypeStruct((8, 128), F32)
VMEM = pl.BlockSpec(memory_space=pltpu.VMEM)
ANY = pl.BlockSpec(memory_space=pl.ANY)


def tile_kernel(near_ref, live_ref, cluster_ref, present_ref, features_ref, base_ref, prop_ref, mixed_ref):
    tiles = cluster_ref.shape[0]
    step = pl.program_id(0)
    slot = lax.broadcasted_iota(jnp.int32, (TILE, TILE), 0)
    node = lax.broadcasted_iota(jnp.int32, (TILE, TILE), 1)
    slot_low = slot.astype(F32).astype(BF16)
    one, zero = jnp.ones((TILE, TILE), BF16), jnp.zeros((TILE, TILE), BF16)
    for t in range(tiles):
        part = slice(t * TILE, (t + 1) * TILE)
        near = jnp.where(live_ref[:, part] == 1, near_ref[:, part], -1).astype(F32).astype(BF16)
        hits = zero
        for k in range(near.shape[0]):
            hits = hits + jnp.where(near[k : k + 1, :] == slot_low, one, zero)
        key = jnp.where(present_ref[t] == 1, cluster_ref[t], -1).astype(F32)
        along = jnp.broadcast_to(key, (TILE, TILE))
        down = along.T
        allowed = (along == down) & (along >= 0.0) & (slot != node)
        adjacency = jnp.where(allowed, hits.astype(F32), 0.0)
        degree = jnp.sum(adjacency, axis=0, keepdims=True)
        self_loops = jnp.where((slot == node) & (along >= 0.0), 2.0, 0.0)
        prop_t = (adjacency + self_loops) / (degree + 1.0)
        at = step * tiles + t
        prop_ref[at] = prop_t.astype(BF16)
        prop = prop_t.T.astype(BF16)
        mixed = jnp.dot(prop, features_ref[part, :], preferred_element_type=F32)
        mixed_ref[pl.ds(pl.multiple_of(at * TILE, TILE), TILE), :] = mixed.astype(BF16)


def propagate(features, neighbours, edge_mask, cluster_ids, row_mask, base):
    rows, width = features.shape
    tiles = rows // TILE
    nbrs = neighbours.shape[1]
    each = 2
    block = each * TILE
    inputs = (
        neighbours.T,
        edge_mask.T,
        cluster_ids.reshape(tiles, 1, TILE),
        row_mask.reshape(tiles, 1, TILE),
        features,
    )
    return pl.pallas_call(
        tile_kernel,
        grid=(tiles // each,),
        in_specs=[
            pl.BlockSpec((nbrs, block), lambda t: (0, t)),
            pl.BlockSpec((nbrs, block), lambda t: (0, t)),
            pl.BlockSpec((each, 1, TILE), lambda t: (t, 0, 0)),
            pl.BlockSpec((each, 1, TILE), lambda t: (t, 0, 0)),
            pl.BlockSpec((block, width), lambda t: (t, 0)),
            ANY,
        ],
        out_specs=[VMEM, VMEM],
        out_shape=[
            jax.ShapeDtypeStruct((tiles, TILE, TILE), BF16),
            jax.ShapeDtypeStruct((rows, width), BF16),
        ],
        compiler_params=pltpu.CompilerParams(vmem_limit_bytes=12 * 2**20),
        cost_estimate=pl.CostEstimate(
            flops=2 * rows * width * width // 2, bytes_accessed=2 * rows * width, transcendentals=0
        ),
        name="propagate",
    )(*(pltpu.with_memory_space_constraint(v, pltpu.HBM) for v in inputs), base)


def layer_kernel(start, line, base_ref, mixed_ref, weight_ref, bias_ref, cot_ref, *rest):
    act_ref, cot_in, act_sem, cot_sem = rest[-4:]
    act_out, gp_ref, theirs_ref, mine_ref = rest[-8:-4]
    rows, cols = act_ref.shape
    block = min(rows, 512)
    half = mixed_ref.shape[1] // 4
    chunk = half // 4
    here = slice(start, start + cols)
    load = pltpu.make_async_copy(cot_ref.at[:, pl.ds(start, cols)], cot_in, cot_sem)
    load.start()
    total = jnp.zeros((1, cols), F32)
    for i in range(rows // block):
        part = slice(i * block, (i + 1) * block)
        pre = jnp.dot(mixed_ref[part, :], weight_ref[:, here], preferred_element_type=F32) + bias_ref[:, here]
        act_ref[part, :] = jnp.maximum(pre, 0.0).astype(BF16)
        if i == 0:
            load.wait()
        grad = jnp.where(pre > 0.0, cot_in[part, :].astype(F32), 0.0).astype(BF16)
        gp_ref[part, here] = grad
        total = total + jnp.sum(grad.astype(F32), axis=0, keepdims=True)
    store = pltpu.make_async_copy(act_ref, act_out.at[:, pl.ds(start, cols)], act_sem)
    store.start()

    def share_of(from_row):
        return lax.dot_general(
            mixed_ref[:, pl.ds(from_row, half)],
            gp_ref[:, here],
            (((0,), (0,)), ((), ())),
            preferred_element_type=F32,
        )

    total = jnp.broadcast_to(total, (8, cols))
    for side, out_ref in ((0, theirs_ref), (1, mine_ref)):
        for j in range(2):
            share = share_of(pl.multiple_of((base_ref[line + side] // 8) * 2 * half + j * half, half))
            for m in range(4):
                spot = ((j * 4 + m) ^ (base_ref[line + side] % 8)) * chunk
                out_ref[pl.ds(pl.multiple_of(spot, chunk), chunk), :] = share[m * chunk : (m + 1) * chunk]
        out_ref[2 * half :, :] = total
    store.wait()


def layer_group(name, base, line, mixed, weight, bias, cotangent, waits, carried, start, cols):
    rows, width = mixed.shape
    share = jax.ShapeDtypeStruct((width // 2 + 8, cols), F32)
    return pl.pallas_call(
        functools.partial(layer_kernel, start, line),
        grid_spec=pltpu.PrefetchScalarGridSpec(
            num_scalar_prefetch=1,
            grid=(1,),
            in_specs=[VMEM, VMEM, VMEM, ANY] + [ANY] * len(waits) + ([ANY, VMEM] if carried else []),
            out_specs=[ANY, VMEM, VMEM, VMEM],
            scratch_shapes=[
                pltpu.VMEM((rows, cols), BF16),
                pltpu.VMEM((rows, cols), BF16),
                pltpu.SemaphoreType.DMA,
                pltpu.SemaphoreType.DMA,
            ],
        ),
        out_shape=[
            jax.ShapeDtypeStruct((rows, width), BF16),
            jax.ShapeDtypeStruct((rows, width), BF16),
            share,
            share,
        ],
        input_output_aliases={5 + len(waits): 0, 6 + len(waits): 1} if carried else {},
        compiler_params=pltpu.CompilerParams(vmem_limit_bytes=10 * 2**20),
        cost_estimate=COST,
        name=name,
    )(
        base,
        mixed,
        weight,
        bias.reshape(1, width),
        pltpu.with_memory_space_constraint(cotangent, pltpu.HBM),
        *waits,
        *carried,
    )


def join_kernel(plan, *refs):
    outs = refs[len(refs) - len(plan) :]
    for out_ref, pieces in zip(outs, plan):
        at = 0
        for count, terms in pieces:
            value = refs[terms[0][0]][terms[0][1] : terms[0][1] + count, :]
            for index, row in terms[1:]:
                value = value + refs[index][row : row + count, :]
            out_ref[at : at + count, :] = value
            at += count


def join(name, arrays, waits, *plan):
    cols = arrays[0].shape[1]
    return pl.pallas_call(
        functools.partial(join_kernel, plan),
        in_specs=[VMEM] * len(arrays) + [ANY] * len(waits),
        out_specs=[VMEM] * len(plan),
        out_shape=[jax.ShapeDtypeStruct((sum(n for n, _ in pieces), cols), F32) for pieces in plan],
        compiler_params=pltpu.CompilerParams(vmem_limit_bytes=12 * 2**20),
        cost_estimate=COST,
        name=name,
    )(*arrays, *waits)


def placing(base_ref, jobs, refs, out_ref, sems):
    copies = []
    for n, (side, at) in enumerate(jobs):
        cols = refs[2 * n].shape[1]
        chunk = refs[2 * n].shape[0] // 4
        for r in range(8):
            spot = pl.multiple_of((base_ref[side] ^ r) * chunk, chunk)
            copies.append(
                pltpu.make_async_copy(
                    refs[2 * n + r // 4].at[pl.ds((r % 4) * chunk, chunk), :],
                    out_ref.at[pl.ds(spot, chunk), pl.ds(at, cols)],
                    sems.at[8 * n + r],
                )
            )
    return copies


def place_kernel(jobs, base_ref, *rest):
    out_ref, done_ref, sems = rest[-3:]
    copies = placing(base_ref, jobs, rest[: 2 * len(jobs)], out_ref, sems)
    for copy in copies:
        copy.start()
    done_ref[...] = jnp.zeros_like(done_ref)
    for copy in copies:
        copy.wait()


def place(name, base, jobs, pieces, waits, out, width):
    carried = [] if out is None else [out]
    return pl.pallas_call(
        functools.partial(place_kernel, jobs),
        grid_spec=pltpu.PrefetchScalarGridSpec(
            num_scalar_prefetch=1,
            grid=(1,),
            in_specs=[VMEM] * len(pieces) + [ANY] * (len(waits) + len(carried)),
            out_specs=[ANY, VMEM],
            scratch_shapes=[pltpu.SemaphoreType.DMA((8 * len(jobs),))],
        ),
        out_shape=[jax.ShapeDtypeStruct((width, width), F32), DONE],
        input_output_aliases={1 + len(pieces) + len(waits): 0} if carried else {},
        compiler_params=pltpu.CompilerParams(vmem_limit_bytes=12 * 2**20),
        cost_estimate=COST,
        name=name,
    )(base, *pieces, *waits, *carried)


def line_up(shares, width):
    def kernel(*refs):
        at = 0
        for ref in refs[:-1]:
            cols = ref.shape[1]
            refs[-1][:, at : at + cols] = ref[0:1, :]
            at += cols

    return pl.pallas_call(
        kernel,
        in_specs=[VMEM] * len(shares),
        out_specs=VMEM,
        out_shape=jax.ShapeDtypeStruct((1, width), F32),
        name="bias",
    )(*shares).reshape(width)


def back_kernel(index, jobs, base_ref, gp_ref, weight_ref, prop_ref, *rest):
    if jobs:
        out_ref, done_ref, whole_ref, sems = rest[-4:]
        copies = placing(base_ref, jobs, rest[: 2 * len(jobs)], whole_ref, sems)
    else:
        out_ref, done_ref = rest[-2:]
        copies = []
    part, cols = out_ref.shape
    j = pl.program_id(0)

    @pl.when(j == 0)
    def _():
        done_ref[...] = jnp.zeros_like(done_ref)
        for copy in copies:
            copy.start()

    cut = pl.ds(pl.multiple_of(j * cols, cols), cols)
    mixed = lax.dot_general(
        gp_ref[index * part : (index + 1) * part, :],
        weight_ref[cut, :],
        (((1,), (1,)), ((), ())),
        preferred_element_type=F32,
    ).astype(BF16)
    for t in range(part // TILE):
        rows = slice(t * TILE, (t + 1) * TILE)
        tile = index * (part // TILE) + t
        out_ref[rows, :] = jnp.dot(prop_ref[tile], mixed[rows], preferred_element_type=F32).astype(BF16)

    @pl.when(j == pl.num_programs(0) - 1)
    def _():
        for copy in copies:
            copy.wait()


def back(name, base, gp, weight, prop_t, waits, carried, index, count, jobs, pieces, out):
    rows, width = gp.shape
    part = rows // count
    cols = min(width, 1024)
    before = [] if carried is None else [carried]
    whole = [out] if jobs and out is not None else []
    at = 4 + len(pieces) + len(waits)
    aliases = {at: 0} if before else {}
    if whole:
        aliases[at + len(before)] = 2
    return pl.pallas_call(
        functools.partial(back_kernel, index, jobs),
        grid_spec=pltpu.PrefetchScalarGridSpec(
            num_scalar_prefetch=1,
            grid=(width // cols,),
            in_specs=[VMEM] * (3 + len(pieces)) + [ANY] * (len(waits) + len(before) + len(whole)),
            out_specs=[pl.BlockSpec((part, cols), lambda j, b: (index, j)), VMEM] + ([ANY] if jobs else []),
            scratch_shapes=[pltpu.SemaphoreType.DMA((8 * len(jobs),))] if jobs else [],
        ),
        out_shape=[jax.ShapeDtypeStruct((rows, width), BF16), DONE]
        + ([jax.ShapeDtypeStruct((width, width), F32)] if jobs else []),
        input_output_aliases=aliases,
        compiler_params=pltpu.CompilerParams(vmem_limit_bytes=20 * 2**20),
        cost_estimate=COST,
        name=name,
    )(base, gp, weight, prop_t, *pieces, *waits, *before, *whole)


def bit_length(n):
    return n.bit_length() - 1


def per_device(groups, locs, features, weight, bias, cotangent, neighbours, edge_mask, cluster_ids, row_mask):
    width = features.shape[1]
    devices = groups * locs
    top, low = bit_length(devices), bit_length(locs)
    y_bits, x_bits, z_bits = list(range(1, low)), list(range(low, top - 2)), [top - 2, top - 1]
    axes = ("grp", "loc")
    number = lax.axis_index("grp") * locs + lax.axis_index("loc")

    def swap(value, pair):
        flip = lambda i: i ^ (1 << pair[i & 1])
        return lax.ppermute(value, axes, [(i, flip(i)) for i in range(devices)])

    core, first, second, near_z = (0, 0), (x_bits[0], y_bits[0]), (y_bits[0], x_bits[0]), (z_bits[0],) * 2
    stages = {"x": first, "y": second, "z": near_z}
    halving = {kind: [stages[k] for k in kind] for _, kind in GROUPS}
    doubling = [(z_bits[1],) * 2] + [(b, b) for b in x_bits[1:] + y_bits[1:]]

    slots, line = [], {}
    for kind in sorted(halving):
        line[kind] = len(slots)
        for side in (1 - number % 2, number % 2):
            spot = side
            for pair in halving[kind]:
                spot = spot * 2 + jnp.where(side == 1, (number >> pair[1]) & 1, (number >> pair[0]) & 1)
            slots.append(spot)
    base = jnp.stack(slots).astype(jnp.int32)

    prop_t, mixed = propagate(features, neighbours, edge_mask, cluster_ids, row_mask, base)

    count = len(GROUPS)
    unit = width // sum(u for u, _ in GROUPS)
    starts, sizes, kinds = [], [], []
    for u, kind in GROUPS:
        starts.append(sum(sizes))
        sizes.append(u * unit)
        kinds.append(kind)
    fills = sum(e[0] == "f" for e in ORDER)

    terms = [None] * count
    got = [None] * count
    shares = [None] * count
    carried = []
    out = None
    grad_features = None
    token = prop_t
    end = width // 16

    flight = {}

    def halves(names):
        jobs, pieces = [], []
        for name in names:
            n, which = int(name[1]), int(name[2])
            jobs.append((line[kinds[n]] + 1 - which, starts[n]))
            pieces += terms[n] if which == 0 else got[n]
        return tuple(jobs), pieces

    for event in ORDER:
        event, *early = event.split("+")
        event, *riders = event.split("*")
        what, g = event[0], int(event[1])
        stage = int(event[2]) if len(event) > 2 else 0
        waits = [token] + [flight[name] for name in early]
        if what == "g":
            act, gp, theirs, mine = layer_group(
                event, base, line[kinds[g]], mixed, weight, bias, cotangent, waits, carried, starts[g], sizes[g]
            )
            carried = [act, gp]
            token = theirs
            terms[g] = [mine, swap(theirs, core)]
            flight[f"c{g}_"] = terms[g][1]
        elif what == "r" and stage < 3:
            n = (width // 2) >> (stage + 1)
            send, keep = join(
                event,
                terms[g],
                waits,
                ((n + 8, ((0, n), (1, n))),),
                ((n, ((0, 0), (1, 0))), (8, ((0, 2 * n), (1, 2 * n)))),
            )
            terms[g] = [keep, swap(send, halving[kinds[g]][stage])]
            flight[f"R{g}{stage}"] = terms[g][1]
            token = send
        elif what == "r":
            for pair in doubling:
                (total,) = join(event, terms[g], waits, ((end + 8, ((0, 0), (1, 0))),))
                terms[g] = [total, swap(total, pair)]
                token = total
                waits = [token]
            flight[f"R{g}{stage}"] = terms[g][1]
        elif what == "a":
            if stage == 0:
                total, shares[g] = join(
                    event, terms[g], waits, ((end, ((0, 0), (1, 0))),), ((8, ((0, end), (1, end))),)
                )
            else:
                n = terms[g][0].shape[0]
                (total,) = join(event, terms[g], waits, ((n, ((0, 0),)), (n, ((1, 0),))))
            terms[g] = [total, swap(total, halving[kinds[g]][2 - stage])]
            flight[f"A{g}{stage}"] = terms[g][1]
            if stage == 2:
                got[g] = [swap(total, core)]
                flight[f"C{g}0"] = got[g][0]
            token = total
        elif what == "c":
            late, _ = lax.optimization_barrier((terms[g][1], token))
            terms[g][1] = late
            got[g].append(swap(late, core))
            flight[f"C{g}1"] = got[g][1]
        elif what == "w":
            jobs, pieces = halves([event])
            out, token = place(event, base, jobs, pieces, waits, out, width)
        else:
            jobs, pieces = halves(riders)
            grad_features, token, *more = back(
                event, base, carried[1], weight, prop_t, waits, grad_features, g, fills, jobs, pieces, out
            )
            out = more[0] if more else out
    return carried[0], grad_features, out, line_up(shares, width)


def solution(mesh):
    rows = P(("grp", "loc"), None)
    flat = P(("grp", "loc"))
    in_specs = (rows, P(), P(), rows, rows, rows, flat, flat)
    out_specs = (rows, rows, P(), P())
    return jax.shard_map(
        functools.partial(per_device, mesh.shape["grp"], mesh.shape["loc"]),
        mesh=mesh,
        in_specs=in_specs,
        out_specs=out_specs,
        check_vma=False,
    )
```

time: 191 us -> 172 us (0.901)
  waiting for transfers between devices: 60.5 us -> 46.5 us
  starting transfers between devices: 49.9 us -> 40.4 us
  local copies, waits for them, and re-layouts: 1.64 us -> 5.16 us
  Pallas kernels: 74 us -> 76.3 us
    ppermute x40, waiting for transfers between devices: 60.5 us -> 46.5 us  [swap(): return lax.ppermute(value, axes, [(i, flip(i)) for i in range(devices)])]
    ppermute x40, starting transfers between devices: 49.9 us -> 40.4 us  [swap(): return lax.ppermute(value, axes, [(i, flip(i)) for i in range(devices)])]
    unnamed x8 -> x30, local copies, waits for them, and re-layouts: 0.47 us -> 5.08 us
    pallas_call x28, Pallas kernels: 4.56 us -> 7.62 us  [join(): pl.pallas_call(functools.partial(join_kernel, plan), in_specs=[VMEM] * le...]
    pallas_call x12 -> x13, Pallas kernels: 38.6 us -> 37.8 us  [the longest x8 19 us: place(): pl.pallas_call(functools.partial(place_kernel, jobs), grid_spec=pltpu.Pre...]
  transfers between devices with their start and end apart: 40 -> 40, of which waited for: 20 -> 15; matrix products, arithmetic and copies ran while one was open for 1% -> 0% of each run, Pallas kernels for 32% -> 36%
where the time goes in v2:
time: 172 us; the launch traced here: 170 us
  Pallas kernels  76.3 us (44%)
  waiting for transfers between devices  46.5 us (27%)
  starting transfers between devices  40.4 us (23%)
  local copies, waits for them, and re-layouts  5.16 us (3%)
    ppermute x40, waiting for transfers between devices, swap(): return lax.ppermute(value, axes, [(i, flip(i)) for i in range(devices)])  46.5 us
    ppermute x40, starting transfers between devices, swap(): return lax.ppermute(value, axes, [(i, flip(i)) for i in range(devices)])  40.4 us
    pallas_call x4, Pallas kernels, layer_group(): pl.pallas_call(functools.partial(layer_kernel, start, line), grid_spec=pl...  24.6 us
    pallas_call x8, Pallas kernels, place(): pl.pallas_call(functools.partial(place_kernel, jobs), grid_spec=pltpu.Pre...  19 us
    pallas_call x4, Pallas kernels, back(): pl.pallas_call(functools.partial(back_kernel, index, jobs), grid_spec=plt...  17.4 us
    pallas_call x28, Pallas kernels, join(): pl.pallas_call(functools.partial(join_kernel, plan), in_specs=[VMEM] * le...  7.62 us
    pallas_call x1, Pallas kernels, propagate(): pl.pallas_call(tile_kernel, grid=(tiles // each,), in_specs=[pl.BlockSpec...  6.33 us
    unnamed x30, local copies, waits for them, and re-layouts  5.08 us
  transfers between devices with their start and end apart: 40, of which 15 were waited for; matrix products, arithmetic and copies ran while one was open for 0% of the time, Pallas kernels for 36%

profile of v2, /device:TPU:19, one launch (start us, length us, event | category | flops | bytes accessed | tf_op | source)
XLA Modules:
  0.0 169.7 jit_solution(17709997257378517907)
XLA Ops:
  0.8 6.3 %propagate.1 = (bf16[8,128,128]{2,1,0:T(8,128)(2,1)S(1)}, bf16[1024,2048]{1,0:T(8,128)(2,1)S(1)}) custom-call(s32[64,1024]{1,0:T(8,128)} %bitcast.19, s32[64,1024]{1,0:T(8,128)} %bitcast.20, s32[8,1,128]{2,1,0:T(1,128)} %bitcast.21, s32[8,1,128]{2,1,0:T(1,128)} %bitcast.22, bf16[1024,2048]{1,0:T(8,128)(2,1)} %features_ref.1, s32[6]{0:T(128)S(1)} %stack.27.base_ref), custom_call_target="tpu_custom_call" | custom-call | flops 4294967296 | bytes 4194304 | tf_op jit(solution)/shard_map/propagate/pallas_call | solution.py:69
  7.1 5.9 %g0.1 = (bf16[1024,2048]{1,0:T(8,128)(2,1)}, bf16[1024,2048]{1,0:T(8,128)(2,1)S(1)}, f32[1032,512]{1,0:T(8,128)S(1)}, f32[1032,512]{1,0:T(8,128)S(1)}) custom-call(s32[6]{0:T(128)S(1)} %stack.27.base_ref, bf16[1024,2048]{1,0:T(8,128)(2,1)S(1)} %get-tuple-element.81.mixed_ref, bf16[2048,2048]{1,0:T(8,128)(2,1)S(1)} %copy-done.4, f32[1,2048]{1,0:T(1,128)S(1)} %bitcast.14, ...), custom_call_target="tpu_custom_call" | custom-call | flops 24999999488 | bytes 1048576 | tf_op jit(solution)/shard_map/g0/pallas_call | solution.py:138
  13.8 6.2 %g1.1 = (bf16[1024,2048]{1,0:T(8,128)(2,1)}, bf16[1024,2048]{1,0:T(8,128)(2,1)S(1)}, f32[1032,512]{1,0:T(8,128)S(1)}, f32[1032,512]{1,0:T(8,128)S(1)}) custom-call(s32[6]{0:T(128)S(1)} %stack.27.base_ref, bf16[1024,2048]{1,0:T(8,128)(2,1)S(1)} %get-tuple-element.81.mixed_ref, ...), custom_call_target="tpu_custom_call", output_to_operand_aliasing={{0}: (6, {}), {1}: (7, {})} | custom-call | flops 24999999488 | bytes 1048576 | tf_op jit(solution)/shard_map/g1/pallas_call | solution.py:138
  21.6 2.6 %collective-permute-done.refs_1_ = f32[1032,512]{1,0:T(8,128)S(1)} collective-permute-done((f32[1032,512]{1,0:T(8,128)S(1)}, f32[1032,512]{1,0:T(8,128)S(1)}, u32[]{:S(2)}, u32[]{:S(2)}) %collective-permute-start) | collective-permute-done | bytes 2113568 | tf_op jit(solution)/shard_map/ppermute | solution.py:337
  26.8 6.2 %g2.1 = (bf16[1024,2048]{1,0:T(8,128)(2,1)}, bf16[1024,2048]{1,0:T(8,128)(2,1)S(1)}, f32[1032,512]{1,0:T(8,128)S(1)}, f32[1032,512]{1,0:T(8,128)S(1)}) custom-call(s32[6]{0:T(128)S(1)} %stack.27.base_ref, bf16[1024,2048]{1,0:T(8,128)(2,1)S(1)} %get-tuple-element.81.mixed_ref, ...), custom_call_target="tpu_custom_call", output_to_operand_aliasing={{0}: (6, {}), {1}: (7, {})} | custom-call | flops 24999999488 | bytes 1048576 | tf_op jit(solution)/shard_map/g2/pallas_call | solution.py:138
  35.0 2.2 %collective-permute-done.2.refs_1_ = f32[1032,512]{1,0:T(8,128)S(1)} collective-permute-done((f32[1032,512]{1,0:T(8,128)S(1)}, f32[1032,512]{1,0:T(8,128)S(1)}, u32[]{:S(2)}, u32[]{:S(2)}) %collective-permute-start.2) | collective-permute-done | bytes 2113568 | tf_op jit(solution)/shard_map/ppermute | solution.py:337
  37.9 6.4 %g3.1 = (bf16[1024,2048]{1,0:T(8,128)(2,1)}, bf16[1024,2048]{1,0:T(8,128)(2,1)S(1)}, f32[1032,512]{1,0:T(8,128)S(1)}, f32[1032,512]{1,0:T(8,128)S(1)}) custom-call(s32[6]{0:T(128)S(1)} %stack.27.base_ref, bf16[1024,2048]{1,0:T(8,128)(2,1)S(1)} %get-tuple-element.81.mixed_ref, ...), custom_call_target="tpu_custom_call", output_to_operand_aliasing={{0}: (6, {}), {1}: (7, {})} | custom-call | flops 24999999488 | bytes 1048576 | tf_op jit(solution)/shard_map/g3/pallas_call | solution.py:138
  44.2 1.7 %collective-permute-start.6 = (f32[1032,512]{1,0:T(8,128)S(1)}, f32[1032,512]{1,0:T(8,128)S(1)}, u32[]{:S(2)}, u32[]{:S(2)}) collective-permute-start(f32[1032,512]{1,0:T(8,128)S(1)} %get-tuple-element.104.refs_2_), channel_id=1, source_target_pairs={{0,1},{1,0},{2,3},{3,2},{4,5},{5,4},{6,7},{7,6},{8,9},{9,8},{10,11... | collective-permute-start | bytes 6340616 | tf_op jit(solution)/shard_map/ppermute | solution.py:337
  46.9 4.4 %f0.1 = (bf16[1024,2048]{1,0:T(8,128)(2,1)}, f32[8,128]{1,0:T(8,128)S(1)}) custom-call(s32[6]{0:T(128)S(1)} %stack.27.base_ref, bf16[1024,2048]{1,0:T(8,128)(2,1)S(1)} %get-tuple-element.101.gp_ref, bf16[2048,2048]{1,0:T(8,128)(2,1)S(1)} %copy-done.4, bf16[8,128,128]{2,1,0:T(8,128)(2,1)S(1)} %copy-done.11, f32[136,512]{1,0:T(8,128)S(1)} %get-tuple-element.105.rest_0_), custom_call_target="tpu_custom_call" | custom-call | flops 24999999488 | bytes 1048576 | tf_op jit(solution)/shard_map/f0/pallas_call | solution.py:305
  53.4 3.2 %collective-permute-done.9.refs_1_ = f32[136,512]{1,0:T(8,128)S(1)} collective-permute-done((f32[136,512]{1,0:T(8,128)S(1)}, f32[136,512]{1,0:T(8,128)S(1)}, u32[]{:S(2)}, u32[]{:S(2)}) %collective-permute-start.9) | collective-permute-done | bytes 278560 | tf_op jit(solution)/shard_map/ppermute | solution.py:337
  58.7 3.4 %collective-permute-done.7.refs_1_ = f32[264,512]{1,0:T(8,128)S(1)} collective-permute-done((f32[264,512]{1,0:T(8,128)S(1)}, f32[264,512]{1,0:T(8,128)S(1)}, u32[]{:S(2)}, u32[]{:S(2)}) %collective-permute-start.7) | collective-permute-done | bytes 540704 | tf_op jit(solution)/shard_map/ppermute | solution.py:337
  62.5 6.9 %collective-permute-done.11.refs_1_ = f32[264,512]{1,0:T(8,128)S(1)} collective-permute-done((f32[264,512]{1,0:T(8,128)S(1)}, f32[264,512]{1,0:T(8,128)S(1)}, u32[]{:S(2)}, u32[]{:S(2)}) %collective-permute-start.11) | collective-permute-done | bytes 540704 | tf_op jit(solution)/shard_map/ppermute | solution.py:337
  71.9 2.2 %collective-permute-start.18 = (f32[128,512]{1,0:T(8,128)S(1)}, f32[128,512]{1,0:T(8,128)S(1)}, u32[]{:S(2)}, u32[]{:S(2)}) collective-permute-start(f32[128,512]{1,0:T(8,128)S(1)} %get-tuple-element.120.refs_2_.refs_0_), channel_id=1, source_target_pairs={{0,8},{1,9},{2,10},{3,11},{4,12},{5,13},{6,14},{7,15},{8,0},{9,1},... | collective-permute-start | bytes 786440 | tf_op jit(solution)/shard_map/ppermute | solution.py:337
  74.1 8.2 %collective-permute-done.15.refs_1_ = f32[520,512]{1,0:T(8,128)S(1)} collective-permute-done((f32[520,512]{1,0:T(8,128)S(1)}, f32[520,512]{1,0:T(8,128)S(1)}, u32[]{:S(2)}, u32[]{:S(2)}) %collective-permute-start.15) | collective-permute-done | bytes 1064992 | tf_op jit(solution)/shard_map/ppermute | solution.py:337
  84.8 6.2 %collective-permute-done.19.refs_1_ = f32[264,512]{1,0:T(8,128)S(1)} collective-permute-done((f32[264,512]{1,0:T(8,128)S(1)}, f32[264,512]{1,0:T(8,128)S(1)}, u32[]{:S(2)}, u32[]{:S(2)}) %collective-permute-start.19) | collective-permute-done | bytes 540704 | tf_op jit(solution)/shard_map/ppermute | solution.py:337
  94.6 4.4 %f1.1 = (bf16[1024,2048]{1,0:T(8,128)(2,1)}, f32[8,128]{1,0:T(8,128)S(1)}) custom-call(s32[6]{0:T(128)S(1)} %stack.27.base_ref, bf16[1024,2048]{1,0:T(8,128)(2,1)S(1)} %get-tuple-element.101.gp_ref, bf16[2048,2048]{1,0:T(8,128)(2,1)S(1)} %bitcast.13, bf16[8,128,128]{2,1,0:T(8,128)(2,1)S(1)} %copy-done.12, ...), custom_call_target="tpu_custom_call", output_to_operand_aliasing={{0}: (5, {})} | custom-call | flops 24999999488 | bytes 1048576 | tf_op jit(solution)/shard_map/f1/pallas_call | solution.py:305
  102.4 2.7 %collective-permute-start.25 = (f32[512,512]{1,0:T(8,128)S(1)}, f32[512,512]{1,0:T(8,128)S(1)}, u32[]{:S(2)}, u32[]{:S(2)}) collective-permute-start(f32[512,512]{1,0:T(8,128)S(1)} %a02.1.rest_0_), channel_id=1, source_target_pairs={{0,1},{1,0},{2,3},{3,2},{4,5},{5,4},{6,7},{7,6},{8,9},{9,8},{10,11... | collective-permute-start | bytes 3145736 | tf_op jit(solution)/shard_map/ppermute | solution.py:337
  106.4 4.4 %f2.1 = (bf16[1024,2048]{1,0:T(8,128)(2,1)}, f32[8,128]{1,0:T(8,128)S(1)}) custom-call(s32[6]{0:T(128)S(1)} %stack.27.base_ref, bf16[1024,2048]{1,0:T(8,128)(2,1)S(1)} %get-tuple-element.101.gp_ref, bf16[2048,2048]{1,0:T(8,128)(2,1)S(1)} %bitcast.13, bf16[8,128,128]{2,1,0:T(8,128)(2,1)S(1)} %copy-done.12, ...), custom_call_target="tpu_custom_call", output_to_operand_aliasing={{0}: (5, {})} | custom-call | flops 24999999488 | bytes 1048576 | tf_op jit(solution)/shard_map/f2/pallas_call | solution.py:305
  112.8 5.6 %collective-permute-start.27 = (f32[128,512]{1,0:T(8,128)S(1)}, f32[128,512]{1,0:T(8,128)}, u32[]{:S(2)}, u32[]{:S(2)}) collective-permute-start(f32[128,512]{1,0:T(8,128)S(1)} %get-tuple-element.131.refs_2_.refs_0_), channel_id=1, source_target_pairs={{0,8},{1,9},{2,10},{3,11},{4,12},{5,13},{6,14},{7,15},{8,0},{9,1},... | collective-permute-start | bytes 786440 | tf_op jit(solution)/shard_map/ppermute | solution.py:337
  121.6 2.9 %collective-permute-start.28 = (f32[512,512]{1,0:T(8,128)}, f32[512,512]{1,0:T(8,128)S(1)}, u32[]{:S(2)}, u32[]{:S(2)}) collective-permute-start(f32[512,512]{1,0:T(8,128)} %a12.1.rest_0_), channel_id=1, source_target_pairs={{0,1},{1,0},{2,3},{3,2},{4,5},{5,4},{6,7},{7,6},{8,9},{9,8},{10,11... | collective-permute-start | bytes 3145736 | tf_op jit(solution)/shard_map/ppermute | solution.py:337
  124.6 4.4 %f3.1 = (bf16[1024,2048]{1,0:T(8,128)(2,1)}, f32[8,128]{1,0:T(8,128)S(1)}) custom-call(s32[6]{0:T(128)S(1)} %stack.27.base_ref, bf16[1024,2048]{1,0:T(8,128)(2,1)S(1)} %get-tuple-element.101.gp_ref, bf16[2048,2048]{1,0:T(8,128)(2,1)S(1)} %bitcast.13, bf16[8,128,128]{2,1,0:T(8,128)(2,1)S(1)} %copy-done.12, ...), custom_call_target="tpu_custom_call", output_to_operand_aliasing={{0}: (5, {})} | custom-call | flops 24999999488 | bytes 1048576 | tf_op jit(solution)/shard_map/f3/pallas_call | solution.py:305
  133.7 6.1 %collective-permute-done.29.refs_1_ = f32[256,512]{1,0:T(8,128)S(1)} collective-permute-done((f32[256,512]{1,0:T(8,128)S(1)}, f32[256,512]{1,0:T(8,128)S(1)}, u32[]{:S(2)}, u32[]{:S(2)}) %collective-permute-start.29) | collective-permute-done | bytes 524320 | tf_op jit(solution)/shard_map/ppermute | solution.py:337
  143.2 1.9 %w01.1 = (f32[2048,2048]{1,0:T(8,128)}, f32[8,128]{1,0:T(8,128)S(1)}) custom-call(s32[6]{0:T(128)S(1)} %stack.27.base_ref, f32[512,512]{1,0:T(8,128)S(1)} %copy-done.8, f32[512,512]{1,0:T(8,128)S(1)} %collective-permute-done.31.refs_3_.rest_1_, f32[512,512]{1,0:T(8,128)} %a32.1.rest_2_.rest_0_, f32[512,512]{1,0:T(8,128)S(1)} %collective-permute-done.34.rest_3_.rest_0_), custom_call_target="tpu_custom_call" | custom-call | flops 24999999488 | bytes 1048576 | tf_op jit(solution)/shard_map/w01/pallas_call | solution.py:227
  145.1 1.9 %w00.1 = (f32[2048,2048]{1,0:T(8,128)}, f32[8,128]{1,0:T(8,128)S(1)}) custom-call(s32[6]{0:T(128)S(1)} %stack.27.base_ref, f32[512,512]{1,0:T(8,128)S(1)} %copy-done.6, f32[512,512]{1,0:T(8,128)S(1)} %collective-permute-done.26.refs_3_.rest_1_, f32[8,128]{1,0:T(8,128)S(1)} %get-tuple-element.136.rest_2_, ...), custom_call_target="tpu_custom_call", output_to_operand_aliasing={{0}: (4, {})} | custom-call | flops 24999999488 | bytes 1048576 | tf_op jit(solution)/shard_map/w00/pallas_call | solution.py:227
  147.1 2.5 %collective-permute-done.36.rest_1_ = f32[512,512]{1,0:T(8,128)} collective-permute-done((f32[512,512]{1,0:T(8,128)}, f32[512,512]{1,0:T(8,128)}, u32[]{:S(2)}, u32[]{:S(2)}) %collective-permute-start.36) | collective-permute-done | bytes 1048608 | tf_op jit(solution)/shard_map/ppermute | solution.py:337
  150.3 3.5 %w10.1 = (f32[2048,2048]{1,0:T(8,128)}, f32[8,128]{1,0:T(8,128)S(1)}) custom-call(s32[6]{0:T(128)S(1)} %stack.27.base_ref, f32[512,512]{1,0:T(8,128)} %a12.1.rest_0_, f32[512,512]{1,0:T(8,128)} %collective-permute-done.36.rest_1_, f32[8,128]{1,0:T(8,128)S(1)} %get-tuple-element.138.rest_2_, ...), custom_call_target="tpu_custom_call", output_to_operand_aliasing={{0}: (5, {})} | custom-call | flops 24999999488 | bytes 1048576 | tf_op jit(solution)/shard_map/w10/pallas_call | solution.py:227
  153.8 1.9 %w11.1 = (f32[2048,2048]{1,0:T(8,128)}, f32[8,128]{1,0:T(8,128)S(1)}) custom-call(s32[6]{0:T(128)S(1)} %stack.27.base_ref, f32[512,512]{1,0:T(8,128)S(1)} %collective-permute-done.28.refs_3_.rest_0_, f32[512,512]{1,0:T(8,128)S(1)} %collective-permute-done.37.rest_1_, f32[8,128]{1,0:T(8,128)S(1)} %get-tuple-element.141.rest_2_, ...), custom_call_target="tpu_custom_call", output_to_operand_aliasing={{0}: (4, {})} | custom-call | flops 24999999488 | bytes 1048576 | tf_op jit(solution)/shard_map/w11/pallas_call | solution.py:227
  156.6 2.3 %collective-permute-start.38 = (f32[512,512]{1,0:T(8,128)S(1)}, f32[512,512]{1,0:T(8,128)S(1)}, u32[]{:S(2)}, u32[]{:S(2)}) collective-permute-start(f32[512,512]{1,0:T(8,128)S(1)} %collective-permute-done.35.rest_1_), channel_id=1, source_target_pairs={{0,1},{1,0},{2,3},{3,2},{4,5},{5,4},{6,7},{7,6},{8,9},{9,8},{10,11... | collective-permute-start | bytes 3145736 | tf_op jit(solution)/shard_map/ppermute | solution.py:337
  158.9 1.9 %w20.1 = (f32[2048,2048]{1,0:T(8,128)}, f32[8,128]{1,0:T(8,128)S(1)}) custom-call(s32[6]{0:T(128)S(1)} %stack.27.base_ref, f32[512,512]{1,0:T(8,128)S(1)} %a22.1.refs_2_.rest_0_, f32[512,512]{1,0:T(8,128)S(1)} %collective-permute-done.35.rest_1_, f32[8,128]{1,0:T(8,128)S(1)} %get-tuple-element.143.rest_2_, ...), custom_call_target="tpu_custom_call", output_to_operand_aliasing={{0}: (4, {})} | custom-call | flops 24999999488 | bytes 1048576 | tf_op jit(solution)/shard_map/w20/pallas_call | solution.py:227
  161.2 1.9 %w21.1 = (f32[2048,2048]{1,0:T(8,128)}, f32[8,128]{1,0:T(8,128)S(1)}) custom-call(s32[6]{0:T(128)S(1)} %stack.27.base_ref, f32[512,512]{1,0:T(8,128)S(1)} %collective-permute-done.34.rest_3_.rest_0_, f32[512,512]{1,0:T(8,128)S(1)} %collective-permute-done.38.rest_1_, f32[8,128]{1,0:T(8,128)S(1)} %get-tuple-element.146.rest_2_, ...), custom_call_target="tpu_custom_call", output_to_operand_aliasing={{0}: (4, {})} | custom-call | flops 24999999488 | bytes 1048576 | tf_op jit(solution)/shard_map/w21/pallas_call | solution.py:227
  163.5 3.5 %w30.1 = (f32[2048,2048]{1,0:T(8,128)}, f32[8,128]{1,0:T(8,128)S(1)}) custom-call(s32[6]{0:T(128)S(1)} %stack.27.base_ref, f32[512,512]{1,0:T(8,128)} %a32.1.rest_2_.rest_0_, f32[512,512]{1,0:T(8,128)} %collective-permute-done.33.rest_1_, f32[8,128]{1,0:T(8,128)S(1)} %get-tuple-element.148.rest_2_, ...), custom_call_target="tpu_custom_call", output_to_operand_aliasing={{0}: (4, {})} | custom-call | flops 24999999488 | bytes 1048576 | tf_op jit(solution)/shard_map/w30/pallas_call | solution.py:227
  167.0 2.5 %w31.1 = (f32[2048,2048]{1,0:T(8,128)}, f32[8,128]{1,0:T(8,128)}) custom-call(s32[6]{0:T(128)S(1)} %stack.27.base_ref, f32[512,512]{1,0:T(8,128)S(1)} %collective-permute-done.32.rest_3_.rest_0_, f32[512,512]{1,0:T(8,128)S(1)} %collective-permute-done.39.rest_1_, f32[8,128]{1,0:T(8,128)S(1)} %get-tuple-element.151.rest_2_, ...), custom_call_target="tpu_custom_call", output_to_operand_aliasing={{0}: (4, {})} | custom-call | flops 24999999488 | bytes 1048576 | tf_op jit(solution)/shard_map/w31/pallas_call | solution.py:227
  (126 shorter events, 42.3 us)
Async XLA Ops:
  20.3 14.3 %collective-permute-start.3 = (f32[520,512]{1,0:T(8,128)S(1)}, f32[520,512]{1,0:T(8,128)S(1)}, u32[]{:S(2)}, u32[]{:S(2)}) collective-permute-start(f32[520,512]{1,0:T(8,128)S(1)} %get-tuple-element.89.refs_2_), channel_id=1, source_target_pairs={{0,4},{1,3},{2,6},{3,1},{4,0},{5,7},{6,2},{7,5},{8,12},{9,11},{10,... | collective-permute-start | bytes 3194888 | tf_op jit(solution)/shard_map/ppermute | solution.py:337
  25.5 25.8 %collective-permute-start.4 = (f32[520,512]{1,0:T(8,128)}, f32[520,512]{1,0:T(8,128)}, u32[]{:S(2)}, u32[]{:S(2)}) collective-permute-start(f32[520,512]{1,0:T(8,128)} %get-tuple-element.90.rest_0_), channel_id=1, source_target_pairs={{0,8},{1,9},{2,10},{3,11},{4,12},{5,13},{6,14},{7,15},{8,0},{9,1},... | collective-permute-start | bytes 3194888 | tf_op jit(solution)/shard_map/ppermute | solution.py:337
  34.7 11.2 %collective-permute-start.5 = (f32[264,512]{1,0:T(8,128)S(1)}, f32[264,512]{1,0:T(8,128)S(1)}, u32[]{:S(2)}, u32[]{:S(2)}) collective-permute-start(f32[264,512]{1,0:T(8,128)S(1)} %get-tuple-element.96.refs_2_), channel_id=1, source_target_pairs={{0,2},{1,5},{2,0},{3,7},{4,6},{5,1},{6,4},{7,3},{8,10},{9,13},{10,... | collective-permute-start | bytes 1622024 | tf_op jit(solution)/shard_map/ppermute | solution.py:337
  37.5 19.2 %collective-permute-start.8 = (f32[520,512]{1,0:T(8,128)S(1)}, f32[520,512]{1,0:T(8,128)S(1)}, u32[]{:S(2)}, u32[]{:S(2)}) collective-permute-start(f32[520,512]{1,0:T(8,128)S(1)} %get-tuple-element.97.rest_0_), channel_id=1, source_target_pairs={{0,2},{1,5},{2,0},{3,7},{4,6},{5,1},{6,4},{7,3},{8,10},{9,13},{10,... | collective-permute-start | bytes 3194888 | tf_op jit(solution)/shard_map/ppermute | solution.py:337
  46.0 10.6 %collective-permute-start.9 = (f32[136,512]{1,0:T(8,128)S(1)}, f32[136,512]{1,0:T(8,128)S(1)}, u32[]{:S(2)}, u32[]{:S(2)}) collective-permute-start(f32[136,512]{1,0:T(8,128)S(1)} %get-tuple-element.105.rest_0_), channel_id=1, source_target_pairs={{0,8},{1,9},{2,10},{3,11},{4,12},{5,13},{6,14},{7,15},{8,0},{9,1},... | collective-permute-start | bytes 835592 | tf_op jit(solution)/shard_map/ppermute | solution.py:337
  52.6 9.6 %collective-permute-start.7 = (f32[264,512]{1,0:T(8,128)S(1)}, f32[264,512]{1,0:T(8,128)S(1)}, u32[]{:S(2)}, u32[]{:S(2)}) collective-permute-start(f32[264,512]{1,0:T(8,128)S(1)} %get-tuple-element.108.refs_2_), channel_id=1, source_target_pairs={{0,4},{1,3},{2,6},{3,1},{4,0},{5,7},{6,2},{7,5},{8,12},{9,11},{10,... | collective-permute-start | bytes 1622024 | tf_op jit(solution)/shard_map/ppermute | solution.py:337
  56.7 14.3 %collective-permute-start.12 = (f32[136,512]{1,0:T(8,128)S(1)}, f32[136,512]{1,0:T(8,128)S(1)}, u32[]{:S(2)}, u32[]{:S(2)}) collective-permute-start(f32[136,512]{1,0:T(8,128)S(1)} %r03.1.refs_2_.refs_0_), channel_id=1, source_target_pairs={{0,16},{1,17},{2,18},{3,19},{4,20},{5,21},{6,22},{7,23},{8,24},{9,... | collective-permute-start | bytes 835592 | tf_op jit(solution)/shard_map/ppermute | solution.py:337
  56.9 12.6 %collective-permute-start.11 = (f32[264,512]{1,0:T(8,128)S(1)}, f32[264,512]{1,0:T(8,128)S(1)}, u32[]{:S(2)}, u32[]{:S(2)}) collective-permute-start(f32[264,512]{1,0:T(8,128)S(1)} %get-tuple-element.112.refs_2_), channel_id=1, source_target_pairs={{0,4},{1,3},{2,6},{3,1},{4,0},{5,7},{6,2},{7,5},{8,12},{9,11},{10,... | collective-permute-start | bytes 1622024 | tf_op jit(solution)/shard_map/ppermute | solution.py:337
  58.5 23.9 %collective-permute-start.15 = (f32[520,512]{1,0:T(8,128)S(1)}, f32[520,512]{1,0:T(8,128)S(1)}, u32[]{:S(2)}, u32[]{:S(2)}) collective-permute-start(f32[520,512]{1,0:T(8,128)S(1)} %get-tuple-element.113.refs_2_), channel_id=1, source_target_pairs={{0,4},{1,3},{2,6},{3,1},{4,0},{5,7},{6,2},{7,5},{8,12},{9,11},{10,... | collective-permute-start | bytes 3194888 | tf_op jit(solution)/shard_map/ppermute | solution.py:337
  62.2 8.8 %collective-permute-start.10 = (f32[136,512]{1,0:T(8,128)S(1)}, f32[136,512]{1,0:T(8,128)S(1)}, u32[]{:S(2)}, u32[]{:S(2)}) collective-permute-start(f32[136,512]{1,0:T(8,128)S(1)} %get-tuple-element.115.refs_2_), channel_id=1, source_target_pairs={{0,2},{1,5},{2,0},{3,7},{4,6},{5,1},{6,4},{7,3},{8,10},{9,13},{10,... | collective-permute-start | bytes 835592 | tf_op jit(solution)/shard_map/ppermute | solution.py:337
  69.6 13.2 %collective-permute-start.14 = (f32[136,512]{1,0:T(8,128)S(1)}, f32[136,512]{1,0:T(8,128)S(1)}, u32[]{:S(2)}, u32[]{:S(2)}) collective-permute-start(f32[136,512]{1,0:T(8,128)S(1)} %get-tuple-element.117.refs_2_), channel_id=1, source_target_pairs={{0,8},{1,9},{2,10},{3,11},{4,12},{5,13},{6,14},{7,15},{8,0},{9,1},... | collective-permute-start | bytes 835592 | tf_op jit(solution)/shard_map/ppermute | solution.py:337
  71.1 11.8 %collective-permute-start.13 = (f32[136,512]{1,0:T(8,128)S(1)}, f32[136,512]{1,0:T(8,128)S(1)}, u32[]{:S(2)}, u32[]{:S(2)}) collective-permute-start(f32[136,512]{1,0:T(8,128)S(1)} %r13.1.refs_2_.refs_0_), channel_id=1, source_target_pairs={{0,16},{1,17},{2,18},{3,19},{4,20},{5,21},{6,22},{7,23},{8,24},{9,... | collective-permute-start | bytes 835592 | tf_op jit(solution)/shard_map/ppermute | solution.py:337
  71.9 20.6 %collective-permute-start.18 = (f32[128,512]{1,0:T(8,128)S(1)}, f32[128,512]{1,0:T(8,128)S(1)}, u32[]{:S(2)}, u32[]{:S(2)}) collective-permute-start(f32[128,512]{1,0:T(8,128)S(1)} %get-tuple-element.120.refs_2_.refs_0_), channel_id=1, source_target_pairs={{0,8},{1,9},{2,10},{3,11},{4,12},{5,13},{6,14},{7,15},{8,0},{9,1},... | collective-permute-start | bytes 786440 | tf_op jit(solution)/shard_map/ppermute | solution.py:337
  82.5 8.6 %collective-permute-start.19 = (f32[264,512]{1,0:T(8,128)S(1)}, f32[264,512]{1,0:T(8,128)S(1)}, u32[]{:S(2)}, u32[]{:S(2)}) collective-permute-start(f32[264,512]{1,0:T(8,128)S(1)} %get-tuple-element.121.refs_2_), channel_id=1, source_target_pairs={{0,2},{1,5},{2,0},{3,7},{4,6},{5,1},{6,4},{7,3},{8,10},{9,13},{10,... | collective-permute-start | bytes 1622024 | tf_op jit(solution)/shard_map/ppermute | solution.py:337
  82.8 16.1 %collective-permute-start.17 = (f32[136,512]{1,0:T(8,128)S(1)}, f32[136,512]{1,0:T(8,128)S(1)}, u32[]{:S(2)}, u32[]{:S(2)}) collective-permute-start(f32[136,512]{1,0:T(8,128)S(1)} %r23.1.refs_2_.refs_0_), channel_id=1, source_target_pairs={{0,16},{1,17},{2,18},{3,19},{4,20},{5,21},{6,22},{7,23},{8,24},{9,... | collective-permute-start | bytes 835592 | tf_op jit(solution)/shard_map/ppermute | solution.py:337
  83.6 15.4 %collective-permute-start.16 = (f32[128,512]{1,0:T(8,128)S(1)}, f32[128,512]{1,0:T(8,128)S(1)}, u32[]{:S(2)}, u32[]{:S(2)}) collective-permute-start(f32[128,512]{1,0:T(8,128)S(1)} %get-tuple-element.122.refs_2_.refs_0_), channel_id=1, source_target_pairs={{0,2},{1,5},{2,0},{3,7},{4,6},{5,1},{6,4},{7,3},{8,10},{9,13},{10,... | collective-permute-start | bytes 786440 | tf_op jit(solution)/shard_map/ppermute | solution.py:337
  91.1 11.1 %collective-permute-start.22 = (f32[136,512]{1,0:T(8,128)S(1)}, f32[136,512]{1,0:T(8,128)S(1)}, u32[]{:S(2)}, u32[]{:S(2)}) collective-permute-start(f32[136,512]{1,0:T(8,128)S(1)} %get-tuple-element.124.refs_2_), channel_id=1, source_target_pairs={{0,8},{1,9},{2,10},{3,11},{4,12},{5,13},{6,14},{7,15},{8,0},{9,1},... | collective-permute-start | bytes 835592 | tf_op jit(solution)/shard_map/ppermute | solution.py:337
  92.5 9.8 %collective-permute-start.24 = (f32[256,512]{1,0:T(8,128)S(1)}, f32[256,512]{1,0:T(8,128)S(1)}, u32[]{:S(2)}, u32[]{:S(2)}) collective-permute-start(f32[256,512]{1,0:T(8,128)S(1)} %a01.1.rest_0_.refs_0_), channel_id=1, source_target_pairs={{0,2},{1,5},{2,0},{3,7},{4,6},{5,1},{6,4},{7,3},{8,10},{9,13},{10,... | collective-permute-start | bytes 1572872 | tf_op jit(solution)/shard_map/ppermute | solution.py:337
  99.6 11.2 %collective-permute-start.21 = (f32[128,512]{1,0:T(8,128)S(1)}, f32[128,512]{1,0:T(8,128)S(1)}, u32[]{:S(2)}, u32[]{:S(2)}) collective-permute-start(f32[128,512]{1,0:T(8,128)S(1)} %get-tuple-element.127.refs_2_.refs_0_), channel_id=1, source_target_pairs={{0,8},{1,9},{2,10},{3,11},{4,12},{5,13},{6,14},{7,15},{8,0},{9,1},... | collective-permute-start | bytes 786440 | tf_op jit(solution)/shard_map/ppermute | solution.py:337
  100.9 9.8 %collective-permute-start.20 = (f32[256,512]{1,0:T(8,128)S(1)}, f32[256,512]{1,0:T(8,128)S(1)}, u32[]{:S(2)}, u32[]{:S(2)}) collective-permute-start(f32[256,512]{1,0:T(8,128)S(1)} %a11.1.refs_2_.refs_0_), channel_id=1, source_target_pairs={{0,4},{1,3},{2,6},{3,1},{4,0},{5,7},{6,2},{7,5},{8,12},{9,11},{10,... | collective-permute-start | bytes 1572872 | tf_op jit(solution)/shard_map/ppermute | solution.py:337
  102.2 9.6 %collective-permute-start.23 = (f32[136,512]{1,0:T(8,128)S(1)}, f32[136,512]{1,0:T(8,128)S(1)}, u32[]{:S(2)}, u32[]{:S(2)}) collective-permute-start(f32[136,512]{1,0:T(8,128)S(1)} %r33.1.refs_2_.refs_0_), channel_id=1, source_target_pairs={{0,16},{1,17},{2,18},{3,19},{4,20},{5,21},{6,22},{7,23},{8,24},{9,... | collective-permute-start | bytes 835592 | tf_op jit(solution)/shard_map/ppermute | solution.py:337
  102.4 9.4 %collective-permute-start.25 = (f32[512,512]{1,0:T(8,128)S(1)}, f32[512,512]{1,0:T(8,128)S(1)}, u32[]{:S(2)}, u32[]{:S(2)}) collective-permute-start(f32[512,512]{1,0:T(8,128)S(1)} %a02.1.rest_0_), channel_id=1, source_target_pairs={{0,1},{1,0},{2,3},{3,2},{4,5},{5,4},{6,7},{7,6},{8,9},{9,8},{10,11... | collective-permute-start | bytes 3145736 | tf_op jit(solution)/shard_map/ppermute | solution.py:337
  105.1 15.4 %collective-permute-start.26 = (f32[512,512]{1,0:T(8,128)S(1)}, f32[512,512]{1,0:T(8,128)S(1)}, u32[]{:S(2)}, u32[]{:S(2)}) collective-permute-start(f32[512,512]{1,0:T(8,128)S(1)} %a02.1.rest_0_), channel_id=1, source_target_pairs={{0,4},{1,3},{2,6},{3,1},{4,0},{5,7},{6,2},{7,5},{8,12},{9,11},{10,... | collective-permute-start | bytes 3145736 | tf_op jit(solution)/shard_map/ppermute | solution.py:337
  112.8 17.6 %collective-permute-start.27 = (f32[128,512]{1,0:T(8,128)S(1)}, f32[128,512]{1,0:T(8,128)}, u32[]{:S(2)}, u32[]{:S(2)}) collective-permute-start(f32[128,512]{1,0:T(8,128)S(1)} %get-tuple-element.131.refs_2_.refs_0_), channel_id=1, source_target_pairs={{0,8},{1,9},{2,10},{3,11},{4,12},{5,13},{6,14},{7,15},{8,0},{9,1},... | collective-permute-start | bytes 786440 | tf_op jit(solution)/shard_map/ppermute | solution.py:337
  118.4 14.8 %collective-permute-start.30 = (f32[256,512]{1,0:T(8,128)S(1)}, f32[256,512]{1,0:T(8,128)S(1)}, u32[]{:S(2)}, u32[]{:S(2)}) collective-permute-start(f32[256,512]{1,0:T(8,128)S(1)} %a21.1.refs_2_.refs_0_), channel_id=1, source_target_pairs={{0,4},{1,3},{2,6},{3,1},{4,0},{5,7},{6,2},{7,5},{8,12},{9,11},{10,... | collective-permute-start | bytes 1572872 | tf_op jit(solution)/shard_map/ppermute | solution.py:337
  121.6 8.8 %collective-permute-start.28 = (f32[512,512]{1,0:T(8,128)}, f32[512,512]{1,0:T(8,128)S(1)}, u32[]{:S(2)}, u32[]{:S(2)}) collective-permute-start(f32[512,512]{1,0:T(8,128)} %a12.1.rest_0_), channel_id=1, source_target_pairs={{0,1},{1,0},{2,3},{3,2},{4,5},{5,4},{6,7},{7,6},{8,9},{9,8},{10,11... | collective-permute-start | bytes 3145736 | tf_op jit(solution)/shard_map/ppermute | solution.py:337
  124.5 25.1 %collective-permute-start.36 = (f32[512,512]{1,0:T(8,128)}, f32[512,512]{1,0:T(8,128)}, u32[]{:S(2)}, u32[]{:S(2)}) collective-permute-start(f32[512,512]{1,0:T(8,128)} %a12.1.rest_0_), channel_id=1, source_target_pairs={{0,8},{1,9},{2,10},{3,11},{4,12},{5,13},{6,14},{7,15},{8,0},{9,1},... | collective-permute-start | bytes 3145736 | tf_op jit(solution)/shard_map/ppermute | solution.py:337
  131.3 8.5 %collective-permute-start.29 = (f32[256,512]{1,0:T(8,128)S(1)}, f32[256,512]{1,0:T(8,128)S(1)}, u32[]{:S(2)}, u32[]{:S(2)}) collective-permute-start(f32[256,512]{1,0:T(8,128)S(1)} %a31.1.refs_2_.refs_0_), channel_id=1, source_target_pairs={{0,2},{1,5},{2,0},{3,7},{4,6},{5,1},{6,4},{7,3},{8,10},{9,13},{10,... | collective-permute-start | bytes 1572872 | tf_op jit(solution)/shard_map/ppermute | solution.py:337
  133.3 9.9 %collective-permute-start.34 = (f32[512,512]{1,0:T(8,128)S(1)}, f32[512,512]{1,0:T(8,128)S(1)}, u32[]{:S(2)}, u32[]{:S(2)}) collective-permute-start(f32[512,512]{1,0:T(8,128)S(1)} %a22.1.refs_2_.rest_0_), channel_id=1, source_target_pairs={{0,1},{1,0},{2,3},{3,2},{4,5},{5,4},{6,7},{7,6},{8,9},{9,8},{10,11... | collective-permute-start | bytes 3145736 | tf_op jit(solution)/shard_map/ppermute | solution.py:337
  133.4 23.2 %collective-permute-start.35 = (f32[512,512]{1,0:T(8,128)S(1)}, f32[512,512]{1,0:T(8,128)S(1)}, u32[]{:S(2)}, u32[]{:S(2)}) collective-permute-start(f32[512,512]{1,0:T(8,128)S(1)} %a22.1.refs_2_.rest_0_), channel_id=1, source_target_pairs={{0,2},{1,5},{2,0},{3,7},{4,6},{5,1},{6,4},{7,3},{8,10},{9,13},{10,... | collective-permute-start | bytes 3145736 | tf_op jit(solution)/shard_map/ppermute | solution.py:337
  140.9 9.4 %collective-permute-start.32 = (f32[512,512]{1,0:T(8,128)}, f32[512,512]{1,0:T(8,128)S(1)}, u32[]{:S(2)}, u32[]{:S(2)}) collective-permute-start(f32[512,512]{1,0:T(8,128)} %a32.1.rest_2_.rest_0_), channel_id=1, source_target_pairs={{0,1},{1,0},{2,3},{3,2},{4,5},{5,4},{6,7},{7,6},{8,9},{9,8},{10,11... | collective-permute-start | bytes 3145736 | tf_op jit(solution)/shard_map/ppermute | solution.py:337
  142.0 21.1 %collective-permute-start.33 = (f32[512,512]{1,0:T(8,128)}, f32[512,512]{1,0:T(8,128)}, u32[]{:S(2)}, u32[]{:S(2)}) collective-permute-start(f32[512,512]{1,0:T(8,128)} %a32.1.rest_2_.rest_0_), channel_id=1, source_target_pairs={{0,4},{1,3},{2,6},{3,1},{4,0},{5,7},{6,2},{7,5},{8,12},{9,11},{10,... | collective-permute-start | bytes 3145736 | tf_op jit(solution)/shard_map/ppermute | solution.py:337
  (23 other events, 102.9 us)

commit v3 on v2

--- a/solution.py
+++ b/solution.py
@@ -11,12 +11,12 @@
 BF16 = jnp.bfloat16
 F32 = jnp.float32
 
-GROUPS = ((2, "xyz"), (2, "zxy"), (2, "yxz"), (2, "xyz"))
+GROUPS = ((4, "xyz"), (4, "zxy"), (4, "xyz"), (4, "xyz"))
 ORDER = (
-    "g0", "g1", "r00", "r10", "g2", "r01", "r20", "g3", "r02", "f0", "r11+c3_", "r03", "r21", "r30", "r12",
-    "r22", "r13+R03", "a00", "r31", "r23", "a10", "r32", "a01", "f1", "a20+A10", "a11", "r33", "a02", "f2",
-    "a30+A11+A20+C00", "a21", "a12+A02", "f3", "a31+C10", "c0", "a22", "a32+C01", "w01+C20", "w00", "c1",
-    "w10+C30", "w11", "c2", "w20", "w21", "c3", "w30", "w31",
+    "g0", "g1", "r00", "g2", "r10", "r20", "r01", "g3", "f0", "r02+c3_", "r21", "r30", "r11", "r03", "r22",
+    "f1", "r31", "a00", "r23", "r12", "r32", "a01", "r13", "a20", "a02", "r33", "a10+C00", "f2", "a21",
+    "a30+A02+A10", "a11", "a22", "c0", "a31", "a12+C20", "w01", "a32+C10", "c2", "w20", "f3*w00*w21+C30", "c1",
+    "w10", "c3", "w11", "w30", "w31",
 )
 
 COST = pl.CostEstimate(flops=25 * 10**9, bytes_accessed=2**20, transcendentals=0)
@@ -57,7 +57,7 @@
     rows, width = features.shape
     tiles = rows // TILE
     nbrs = neighbours.shape[1]
-    each = 2
+    each = 4
     block = each * TILE
     inputs = (
         neighbours.T,
@@ -333,13 +333,18 @@
     number = lax.axis_index("grp") * locs + lax.axis_index("loc")
 
     def swap(value, pair):
-        flip = lambda i: i ^ (1 << pair[i & 1])
-        return lax.ppermute(value, axes, [(i, flip(i)) for i in range(devices)])
-
-    core, first, second, near_z = (0, 0), (x_bits[0], y_bits[0]), (y_bits[0], x_bits[0]), (z_bits[0],) * 2
+        return lax.ppermute(value, axes, [(i, i ^ pair[i & 1]) for i in range(devices)])
+
+    x, y, z, far_z = 1 << x_bits[0], 1 << y_bits[0], 1 << z_bits[0], 3 << z_bits[0]
+    core, first, second, near_z = (1, 1), (x, y), (y, x), (z, z)
     stages = {"x": first, "y": second, "z": near_z}
     halving = {kind: [stages[k] for k in kind] for _, kind in GROUPS}
-    doubling = [(z_bits[1],) * 2] + [(b, b) for b in x_bits[1:] + y_bits[1:]]
+    doubling = [(far_z, far_z)] + [(1 << b, 1 << b) for b in x_bits[1:] + y_bits[1:]]
+
+    def side_of(mask):
+        bit = (number & mask) != 0
+        return (bit ^ ((number & (mask << 1)) != 0) if mask == z else bit).astype(jnp.int32)
+
 
     slots, line = [], {}
     for kind in sorted(halving):
@@ -347,7 +352,7 @@
         for side in (1 - number % 2, number % 2):
             spot = side
             for pair in halving[kind]:
-                spot = spot * 2 + jnp.where(side == 1, (number >> pair[1]) & 1, (number >> pair[0]) & 1)
+                spot = spot * 2 + jnp.where(side == 1, side_of(pair[1]), side_of(pair[0]))
             slots.append(spot)
     base = jnp.stack(slots).astype(jnp.int32)
 

time: 172 us -> 166 us (0.965); the launches traced: 170 us -> 166 us
  starting transfers between devices: 40.4 us -> 50.4 us
  Pallas kernels: 76.3 us -> 68.1 us
  waiting for transfers between devices: 46.5 us -> 41.7 us
    ppermute x40, starting transfers between devices: 40.4 us -> 50.4 us  [swap(): lax.ppermute(value, axes, [(i, i ^ pair[i & 1]) for i in range(devices)])]
    pallas_call x8 -> x6, Pallas kernels: 19 us -> 12.1 us  [place(): pl.pallas_call(functools.partial(place_kernel, jobs), grid_spec=pltpu.Pre...]
    ppermute x40, waiting for transfers between devices: 46.5 us -> 41.7 us  [swap(): lax.ppermute(value, axes, [(i, i ^ pair[i & 1]) for i in range(devices)])]
    unnamed x30 -> x36, local copies, waits for them, and re-layouts: 5.08 us -> 4.49 us
  transfers between devices with their start and end apart: 40 -> 40, of which waited for: 15 -> 20; matrix products, arithmetic and copies ran while one was open for 0% -> 0% of each run, Pallas kernels for 36% -> 33%
where the time goes in v3:
time: 166 us
  Pallas kernels  68.1 us (41%)
  starting transfers between devices  50.4 us (30%)
  waiting for transfers between devices  41.7 us (25%)
  local copies, waits for them, and re-layouts  4.49 us (3%)
    ppermute x40, starting transfers between devices, swap(): lax.ppermute(value, axes, [(i, i ^ pair[i & 1]) for i in range(devices)])  50.4 us
    ppermute x40, waiting for transfers between devices, swap(): lax.ppermute(value, axes, [(i, i ^ pair[i & 1]) for i in range(devices)])  41.7 us
    pallas_call x4, Pallas kernels, layer_group(): pl.pallas_call(functools.partial(layer_kernel, start, line), grid_spec=pl...  24.5 us
    pallas_call x4, Pallas kernels, back(): pl.pallas_call(functools.partial(back_kernel, index, jobs), grid_spec=plt...  17.7 us
    pallas_call x6, Pallas kernels, place(): pl.pallas_call(functools.partial(place_kernel, jobs), grid_spec=pltpu.Pre...  12.1 us
    pallas_call x28, Pallas kernels, join(): pl.pallas_call(functools.partial(join_kernel, plan), in_specs=[VMEM] * le...  7.34 us
    pallas_call x1, Pallas kernels, propagate(): pl.pallas_call(tile_kernel, grid=(tiles // each,), in_specs=[pl.BlockSpec...  5.04 us
    unnamed x36, local copies, waits for them, and re-layouts  4.49 us
  transfers between devices with their start and end apart: 40, of which 20 were waited for; matrix products, arithmetic and copies ran while one was open for 0% of the time, Pallas kernels for 33%

profile of v3, /device:TPU:19, one launch (start us, length us, event | category | flops | bytes accessed | tf_op | source)
XLA Modules:
  0.0 166.1 jit_solution(2230108331707131534)
XLA Ops:
  0.8 5.0 %propagate.1 = (bf16[8,128,128]{2,1,0:T(8,128)(2,1)S(1)}, bf16[1024,2048]{1,0:T(8,128)(2,1)S(1)}) custom-call(s32[64,1024]{1,0:T(8,128)} %bitcast.17, s32[64,1024]{1,0:T(8,128)} %bitcast.18, s32[8,1,128]{2,1,0:T(1,128)} %bitcast.19, s32[8,1,128]{2,1,0:T(1,128)} %bitcast.20, bf16[1024,2048]{1,0:T(8,128)(2,1)} %features_ref.1, s32[4]{0:T(128)S(1)} %pad_add_fusion.base_ref), custom_call_target="tpu_custom_call" | custom-call | flops 4294967296 | bytes 4194304 | tf_op jit(solution)/shard_map/propagate/pallas_call | solution.py:69
  5.8 5.9 %g0.1 = (bf16[1024,2048]{1,0:T(8,128)(2,1)}, bf16[1024,2048]{1,0:T(8,128)(2,1)S(1)}, f32[1032,512]{1,0:T(8,128)S(1)}, f32[1032,512]{1,0:T(8,128)S(1)}) custom-call(s32[4]{0:T(128)S(1)} %pad_add_fusion.base_ref, bf16[1024,2048]{1,0:T(8,128)(2,1)S(1)} %get-tuple-element.78.mixed_ref, bf16[2048,2048]{1,0:T(8,128)(2,1)S(1)} %copy-done.6, ...), custom_call_target="tpu_custom_call" | custom-call | flops 24999999488 | bytes 1048576 | tf_op jit(solution)/shard_map/g0/pallas_call | solution.py:138
  12.4 6.2 %g1.1 = (bf16[1024,2048]{1,0:T(8,128)(2,1)}, bf16[1024,2048]{1,0:T(8,128)(2,1)S(1)}, f32[1032,512]{1,0:T(8,128)S(1)}, f32[1032,512]{1,0:T(8,128)S(1)}) custom-call(s32[4]{0:T(128)S(1)} %pad_add_fusion.base_ref, bf16[1024,2048]{1,0:T(8,128)(2,1)S(1)} %get-tuple-element.78.mixed_ref, ...), custom_call_target="tpu_custom_call", output_to_operand_aliasing={{0}: (6, {}), {1}: (7, {})} | custom-call | flops 24999999488 | bytes 1048576 | tf_op jit(solution)/shard_map/g1/pallas_call | solution.py:138
  20.2 6.1 %g2.1 = (bf16[1024,2048]{1,0:T(8,128)(2,1)}, bf16[1024,2048]{1,0:T(8,128)(2,1)S(1)}, f32[1032,512]{1,0:T(8,128)S(1)}, f32[1032,512]{1,0:T(8,128)S(1)}) custom-call(s32[4]{0:T(128)S(1)} %pad_add_fusion.base_ref, bf16[1024,2048]{1,0:T(8,128)(2,1)S(1)} %get-tuple-element.78.mixed_ref, ...), custom_call_target="tpu_custom_call", output_to_operand_aliasing={{0}: (6, {}), {1}: (7, {})} | custom-call | flops 24999999488 | bytes 1048576 | tf_op jit(solution)/shard_map/g2/pallas_call | solution.py:138
  33.7 6.4 %g3.1 = (bf16[1024,2048]{1,0:T(8,128)(2,1)}, bf16[1024,2048]{1,0:T(8,128)(2,1)S(1)}, f32[1032,512]{1,0:T(8,128)S(1)}, f32[1032,512]{1,0:T(8,128)S(1)}) custom-call(s32[4]{0:T(128)S(1)} %pad_add_fusion.base_ref, bf16[1024,2048]{1,0:T(8,128)(2,1)S(1)} %get-tuple-element.78.mixed_ref, ...), custom_call_target="tpu_custom_call", output_to_operand_aliasing={{0}: (6, {}), {1}: (7, {})} | custom-call | flops 24999999488 | bytes 1048576 | tf_op jit(solution)/shard_map/g3/pallas_call | solution.py:138
  40.0 2.5 %collective-permute-start.5 = (f32[1032,512]{1,0:T(8,128)S(1)}, f32[1032,512]{1,0:T(8,128)S(1)}, u32[]{:S(2)}, u32[]{:S(2)}) collective-permute-start(f32[1032,512]{1,0:T(8,128)S(1)} %get-tuple-element.100.rest_0_), channel_id=1, source_target_pairs={{0,1},{1,0},{2,3},{3,2},{4,5},{5,4},{6,7},{7,6},{8,9},{9,8},{10,11... | collective-permute-start | bytes 6340616 | tf_op jit(solution)/shard_map/ppermute | solution.py:336
  42.6 4.4 %f0.1 = (bf16[1024,2048]{1,0:T(8,128)(2,1)}, f32[8,128]{1,0:T(8,128)S(1)}) custom-call(s32[4]{0:T(128)S(1)} %pad_add_fusion.base_ref, bf16[1024,2048]{1,0:T(8,128)(2,1)S(1)} %get-tuple-element.98.gp_ref, bf16[2048,2048]{1,0:T(8,128)(2,1)S(1)} %copy-done.6, bf16[8,128,128]{2,1,0:T(8,128)(2,1)S(1)} %get-tuple-element.79.rest_0_.prop_ref, ...), custom_call_target="tpu_custom_call" | custom-call | flops 24999999488 | bytes 1048576 | tf_op jit(solution)/shard_map/f0/pallas_call | solution.py:305
  53.3 2.2 %r11.1 = (f32[264,512]{1,0:T(8,128)}, f32[264,512]{1,0:T(8,128)S(1)}) custom-call(f32[520,512]{1,0:T(8,128)S(1)} %get-tuple-element.104.refs_0_, f32[520,512]{1,0:T(8,128)} %collective-permute-done.7.refs_1_, f32[520,512]{1,0:T(8,128)S(1)} %get-tuple-element.108.refs_2_), custom_call_target="tpu_custom_call" | custom-call | flops 24999999488 | bytes 1048576 | tf_op jit(solution)/shard_map/r11/pallas_call | solution.py:187
  56.3 2.1 %collective-permute-done.6.refs_1_ = f32[136,512]{1,0:T(8,128)S(1)} collective-permute-done((f32[136,512]{1,0:T(8,128)S(1)}, f32[136,512]{1,0:T(8,128)S(1)}, u32[]{:S(2)}, u32[]{:S(2)}) %collective-permute-start.6) | collective-permute-done | bytes 278560 | tf_op jit(solution)/shard_map/ppermute | solution.py:336
  58.7 3.7 %collective-permute-done.11.refs_1_ = f32[264,512]{1,0:T(8,128)S(1)} collective-permute-done((f32[264,512]{1,0:T(8,128)S(1)}, f32[264,512]{1,0:T(8,128)S(1)}, u32[]{:S(2)}, u32[]{:S(2)}) %collective-permute-start.11) | collective-permute-done | bytes 540704 | tf_op jit(solution)/shard_map/ppermute | solution.py:336
  63.8 4.4 %f1.1 = (bf16[1024,2048]{1,0:T(8,128)(2,1)}, f32[8,128]{1,0:T(8,128)S(1)}) custom-call(s32[4]{0:T(128)S(1)} %pad_add_fusion.base_ref, bf16[1024,2048]{1,0:T(8,128)(2,1)S(1)} %get-tuple-element.98.gp_ref, bf16[2048,2048]{1,0:T(8,128)(2,1)S(1)} %copy-done.6, ...), custom_call_target="tpu_custom_call", output_to_operand_aliasing={{0}: (5, {})} | custom-call | flops 24999999488 | bytes 1048576 | tf_op jit(solution)/shard_map/f1/pallas_call | solution.py:305
  68.2 3.9 %collective-permute-done.10.refs_1_ = f32[520,512]{1,0:T(8,128)S(1)} collective-permute-done((f32[520,512]{1,0:T(8,128)S(1)}, f32[520,512]{1,0:T(8,128)S(1)}, u32[]{:S(2)}, u32[]{:S(2)}) %collective-permute-start.10) | collective-permute-done | bytes 1064992 | tf_op jit(solution)/shard_map/ppermute | solution.py:336
  74.7 4.2 %collective-permute-done.14.refs_1_ = f32[264,512]{1,0:T(8,128)} collective-permute-done((f32[264,512]{1,0:T(8,128)}, f32[264,512]{1,0:T(8,128)}, u32[]{:S(2)}, u32[]{:S(2)}) %collective-permute-start.14) | collective-permute-done | bytes 540704 | tf_op jit(solution)/shard_map/ppermute | solution.py:336
  80.9 1.8 %collective-permute-done.13.refs_1_ = f32[264,512]{1,0:T(8,128)S(1)} collective-permute-done((f32[264,512]{1,0:T(8,128)S(1)}, f32[264,512]{1,0:T(8,128)S(1)}, u32[]{:S(2)}, u32[]{:S(2)}) %collective-permute-start.13) | collective-permute-done | bytes 540704 | tf_op jit(solution)/shard_map/ppermute | solution.py:336
  88.9 3.6 %collective-permute-done.16.refs_1_ = f32[256,512]{1,0:T(8,128)S(1)} collective-permute-done((f32[256,512]{1,0:T(8,128)S(1)}, f32[256,512]{1,0:T(8,128)S(1)}, u32[]{:S(2)}, u32[]{:S(2)}) %collective-permute-start.16) | collective-permute-done | bytes 524320 | tf_op jit(solution)/shard_map/ppermute | solution.py:336
  92.6 2.5 %collective-permute-start.23 = (f32[512,512]{1,0:T(8,128)S(1)}, f32[512,512]{1,0:T(8,128)S(1)}, u32[]{:S(2)}, u32[]{:S(2)}) collective-permute-start(f32[512,512]{1,0:T(8,128)S(1)} %a02.1.refs_2_.rest_0_), channel_id=1, source_target_pairs={{0,1},{1,0},{2,3},{3,2},{4,5},{5,4},{6,7},{7,6},{8,9},{9,8},{10,11... | collective-permute-start | bytes 3145736 | tf_op jit(solution)/shard_map/ppermute | solution.py:336
  96.4 2.9 %collective-permute-done.21.refs_1_ = f32[136,512]{1,0:T(8,128)S(1)} collective-permute-done((f32[136,512]{1,0:T(8,128)S(1)}, f32[136,512]{1,0:T(8,128)S(1)}, u32[]{:S(2)}, u32[]{:S(2)}) %collective-permute-start.21) | collective-permute-done | bytes 278560 | tf_op jit(solution)/shard_map/ppermute | solution.py:336
  101.0 4.4 %f2.1 = (bf16[1024,2048]{1,0:T(8,128)(2,1)}, f32[8,128]{1,0:T(8,128)S(1)}) custom-call(s32[4]{0:T(128)S(1)} %pad_add_fusion.base_ref, bf16[1024,2048]{1,0:T(8,128)(2,1)S(1)} %get-tuple-element.98.gp_ref, bf16[2048,2048]{1,0:T(8,128)(2,1)S(1)} %copy-done.6, ...), custom_call_target="tpu_custom_call", output_to_operand_aliasing={{0}: (5, {})} | custom-call | flops 24999999488 | bytes 1048576 | tf_op jit(solution)/shard_map/f2/pallas_call | solution.py:305
  106.9 5.0 %collective-permute-done.26.refs_1_ = f32[136,512]{1,0:T(8,128)S(1)} collective-permute-done((f32[136,512]{1,0:T(8,128)S(1)}, f32[136,512]{1,0:T(8,128)S(1)}, u32[]{:S(2)}, u32[]{:S(2)}) %collective-permute-start.26) | collective-permute-done | bytes 278560 | tf_op jit(solution)/shard_map/ppermute | solution.py:336
  111.9 4.5 %collective-permute-start.29 = (f32[128,512]{1,0:T(8,128)S(1)}, f32[128,512]{1,0:T(8,128)}, u32[]{:S(2)}, u32[]{:S(2)}) collective-permute-start(f32[128,512]{1,0:T(8,128)S(1)} %get-tuple-element.128.refs_2_.refs_0_), channel_id=1, source_target_pairs={{0,8},{1,9},{2,10},{3,11},{4,12},{5,13},{6,14},{7,15},{8,0},{9,1},... | collective-permute-start | bytes 786440 | tf_op jit(solution)/shard_map/ppermute | solution.py:336
  118.1 4.5 %collective-permute-start.27 = (f32[512,512]{1,0:T(8,128)S(1)}, f32[512,512]{1,0:T(8,128)S(1)}, u32[]{:S(2)}, u32[]{:S(2)}) collective-permute-start(f32[512,512]{1,0:T(8,128)S(1)} %a22.1.refs_2_.rest_0_), channel_id=1, source_target_pairs={{0,1},{1,0},{2,3},{3,2},{4,5},{5,4},{6,7},{7,6},{8,9},{9,8},{10,11... | collective-permute-start | bytes 3145736 | tf_op jit(solution)/shard_map/ppermute | solution.py:336
  122.6 2.1 %collective-permute-start.31 = (f32[512,512]{1,0:T(8,128)S(1)}, f32[512,512]{1,0:T(8,128)S(1)}, u32[]{:S(2)}, u32[]{:S(2)}) collective-permute-start(f32[512,512]{1,0:T(8,128)S(1)} %collective-permute-done.19.refs_3_.rest_1_), channel_id=1, source_target_pairs={{0,1},{1,0},{2,3},{3,2},{4,5},{5,4},{6,7},{7,6},{8,9},{9,8},{10,11... | collective-permute-start | bytes 3145736 | tf_op jit(solution)/shard_map/ppermute | solution.py:336
  125.8 5.8 %collective-permute-start.33 = (f32[512,512]{1,0:T(8,128)S(1)}, f32[512,512]{1,0:T(8,128)S(1)}, u32[]{:S(2)}, u32[]{:S(2)}) collective-permute-start(f32[512,512]{1,0:T(8,128)S(1)} %a12.1.rest_2_.rest_0_), channel_id=1, source_target_pairs={{0,1},{1,0},{2,3},{3,2},{4,5},{5,4},{6,7},{7,6},{8,9},{9,8},{10,11... | collective-permute-start | bytes 3145736 | tf_op jit(solution)/shard_map/ppermute | solution.py:336
  131.8 1.9 %w01.1 = (f32[2048,2048]{1,0:T(8,128)}, f32[8,128]{1,0:T(8,128)S(1)}) custom-call(s32[4]{0:T(128)S(1)} %copy-done.5, f32[512,512]{1,0:T(8,128)S(1)} %copy-done.10, f32[512,512]{1,0:T(8,128)S(1)} %collective-permute-done.31.rest_1_, f32[512,512]{1,0:T(8,128)S(1)} %a12.1.rest_2_.rest_0_), custom_call_target="tpu_custom_call" | custom-call | flops 24999999488 | bytes 1048576 | tf_op jit(solution)/shard_map/w01/pallas_call | solution.py:227
  133.8 6.0 %collective-permute-done.30.refs_1_ = f32[256,512]{1,0:T(8,128)S(1)} collective-permute-done((f32[256,512]{1,0:T(8,128)S(1)}, f32[256,512]{1,0:T(8,128)S(1)}, u32[]{:S(2)}, u32[]{:S(2)}) %collective-permute-start.30) | collective-permute-done | bytes 524320 | tf_op jit(solution)/shard_map/ppermute | solution.py:336
  142.1 4.9 %collective-permute-start.34 = (f32[512,512]{1,0:T(8,128)S(1)}, f32[512,512]{1,0:T(8,128)S(1)}, u32[]{:S(2)}, u32[]{:S(2)}) collective-permute-start(f32[512,512]{1,0:T(8,128)S(1)} %collective-permute-done.28.rest_1_), channel_id=1, source_target_pairs={{0,1},{1,0},{2,3},{3,2},{4,5},{5,4},{6,7},{7,6},{8,9},{9,8},{10,11... | collective-permute-start | bytes 3145736 | tf_op jit(solution)/shard_map/ppermute | solution.py:336
  147.1 1.9 %w20.1 = (f32[2048,2048]{1,0:T(8,128)}, f32[8,128]{1,0:T(8,128)S(1)}) custom-call(s32[4]{0:T(128)S(1)} %copy-done.5, f32[512,512]{1,0:T(8,128)S(1)} %a22.1.refs_2_.rest_0_, f32[512,512]{1,0:T(8,128)S(1)} %collective-permute-done.28.rest_1_, f32[512,512]{1,0:T(8,128)S(1)} %a32.1.rest_2_.rest_0_, ...), custom_call_target="tpu_custom_call", output_to_operand_aliasing={{0}: (4, {})} | custom-call | flops 24999999488 | bytes 1048576 | tf_op jit(solution)/shard_map/w20/pallas_call | solution.py:227
  151.7 4.6 %f3.1 = (bf16[1024,2048]{1,0:T(8,128)(2,1)}, f32[8,128]{1,0:T(8,128)S(1)}, f32[2048,2048]{1,0:T(8,128)}) custom-call(s32[4]{0:T(128)S(1)} %copy-done.5, bf16[1024,2048]{1,0:T(8,128)(2,1)S(1)} %copy-done.15, bf16[2048,2048]{1,0:T(8,128)(2,1)S(1)} %bitcast.11, bf16[8,128,128]{2,1,0:T(8,128)(2,1)S(1)} %copy-done.13, ...), custom_call_target="tpu_custom_call", output_to_operand_aliasing={{0}: (10, {}), {2}: (11, {})} | custom-call | flops 24999999488 | bytes 1048576 | tf_op jit(solution)/shard_map/f3/pallas_call | solution.py:305
  157.3 1.9 %w10.1 = (f32[2048,2048]{1,0:T(8,128)}, f32[8,128]{1,0:T(8,128)S(1)}) custom-call(s32[4]{0:T(128)S(1)} %copy-done.5, f32[512,512]{1,0:T(8,128)S(1)} %a12.1.rest_2_.rest_0_, f32[512,512]{1,0:T(8,128)S(1)} %collective-permute-done.37.rest_1_, f32[8,128]{1,0:T(8,128)S(1)} %get-tuple-element.137.rest_2_, ...), custom_call_target="tpu_custom_call", output_to_operand_aliasing={{0}: (4, {})} | custom-call | flops 24999999488 | bytes 1048576 | tf_op jit(solution)/shard_map/w10/pallas_call | solution.py:227
  159.6 1.9 %w11.1 = (f32[2048,2048]{1,0:T(8,128)}, f32[8,128]{1,0:T(8,128)S(1)}) custom-call(s32[4]{0:T(128)S(1)} %copy-done.5, f32[512,512]{1,0:T(8,128)S(1)} %collective-permute-done.33.refs_3_.rest_0_, f32[512,512]{1,0:T(8,128)S(1)} %collective-permute-done.39.rest_1_, f32[8,128]{1,0:T(8,128)S(1)} %get-tuple-element.140.rest_2_, ...), custom_call_target="tpu_custom_call", output_to_operand_aliasing={{0}: (4, {})} | custom-call | flops 24999999488 | bytes 1048576 | tf_op jit(solution)/shard_map/w11/pallas_call | solution.py:227
  161.5 1.9 %w30.1 = (f32[2048,2048]{1,0:T(8,128)}, f32[8,128]{1,0:T(8,128)S(1)}) custom-call(s32[4]{0:T(128)S(1)} %copy-done.5, f32[512,512]{1,0:T(8,128)S(1)} %a32.1.rest_2_.rest_0_, f32[512,512]{1,0:T(8,128)S(1)} %collective-permute-done.36.rest_1_, f32[8,128]{1,0:T(8,128)S(1)} %get-tuple-element.143.rest_2_, ...), custom_call_target="tpu_custom_call", output_to_operand_aliasing={{0}: (4, {})} | custom-call | flops 24999999488 | bytes 1048576 | tf_op jit(solution)/shard_map/w30/pallas_call | solution.py:227
  163.4 2.5 %w31.1 = (f32[2048,2048]{1,0:T(8,128)}, f32[8,128]{1,0:T(8,128)}) custom-call(s32[4]{0:T(128)S(1)} %copy-done.5, f32[512,512]{1,0:T(8,128)S(1)} %collective-permute-done.35.rest_5_.rest_0_, f32[512,512]{1,0:T(8,128)S(1)} %collective-permute-done.38.rest_1_, f32[8,128]{1,0:T(8,128)S(1)} %get-tuple-element.145.rest_2_, ...), custom_call_target="tpu_custom_call", output_to_operand_aliasing={{0}: (4, {})} | custom-call | flops 24999999488 | bytes 1048576 | tf_op jit(solution)/shard_map/w31/pallas_call | solution.py:227
  (130 shorter events, 43.2 us)
Async XLA Ops:
  18.6 7.9 %collective-permute-start.3 = (f32[1032,512]{1,0:T(8,128)S(1)}, f32[1032,512]{1,0:T(8,128)S(1)}, u32[]{:S(2)}, u32[]{:S(2)}) collective-permute-start(f32[1032,512]{1,0:T(8,128)S(1)} %get-tuple-element.84.refs_2_), channel_id=1, source_target_pairs={{0,1},{1,0},{2,3},{3,2},{4,5},{5,4},{6,7},{7,6},{8,9},{9,8},{10,11... | collective-permute-start | bytes 6340616 | tf_op jit(solution)/shard_map/ppermute | solution.py:336
  18.9 14.3 %collective-permute-start.1 = (f32[520,512]{1,0:T(8,128)S(1)}, f32[520,512]{1,0:T(8,128)S(1)}, u32[]{:S(2)}, u32[]{:S(2)}) collective-permute-start(f32[520,512]{1,0:T(8,128)S(1)} %get-tuple-element.86.rest_0_), channel_id=1, source_target_pairs={{0,4},{1,3},{2,6},{3,1},{4,0},{5,7},{6,2},{7,5},{8,12},{9,11},{10,... | collective-permute-start | bytes 3194888 | tf_op jit(solution)/shard_map/ppermute | solution.py:336
  27.7 25.6 %collective-permute-start.7 = (f32[520,512]{1,0:T(8,128)}, f32[520,512]{1,0:T(8,128)}, u32[]{:S(2)}, u32[]{:S(2)}) collective-permute-start(f32[520,512]{1,0:T(8,128)} %get-tuple-element.92.refs_2_), channel_id=1, source_target_pairs={{0,8},{1,9},{2,10},{3,11},{4,12},{5,13},{6,14},{7,15},{8,0},{9,1},... | collective-permute-start | bytes 3194888 | tf_op jit(solution)/shard_map/ppermute | solution.py:336
  30.9 20.1 %collective-permute-start.8 = (f32[520,512]{1,0:T(8,128)S(1)}, f32[520,512]{1,0:T(8,128)S(1)}, u32[]{:S(2)}, u32[]{:S(2)}) collective-permute-start(f32[520,512]{1,0:T(8,128)S(1)} %get-tuple-element.93.refs_2_), channel_id=1, source_target_pairs={{0,4},{1,3},{2,6},{3,1},{4,0},{5,7},{6,2},{7,5},{8,12},{9,11},{10,... | collective-permute-start | bytes 3194888 | tf_op jit(solution)/shard_map/ppermute | solution.py:336
  33.3 14.5 %collective-permute-start.4 = (f32[264,512]{1,0:T(8,128)S(1)}, f32[264,512]{1,0:T(8,128)S(1)}, u32[]{:S(2)}, u32[]{:S(2)}) collective-permute-start(f32[264,512]{1,0:T(8,128)S(1)} %get-tuple-element.94.rest_0_), channel_id=1, source_target_pairs={{0,2},{1,5},{2,0},{3,7},{4,6},{5,1},{6,4},{7,3},{8,10},{9,13},{10,... | collective-permute-start | bytes 1622024 | tf_op jit(solution)/shard_map/ppermute | solution.py:336
  40.0 7.8 %collective-permute-start.5 = (f32[1032,512]{1,0:T(8,128)S(1)}, f32[1032,512]{1,0:T(8,128)S(1)}, u32[]{:S(2)}, u32[]{:S(2)}) collective-permute-start(f32[1032,512]{1,0:T(8,128)S(1)} %get-tuple-element.100.rest_0_), channel_id=1, source_target_pairs={{0,1},{1,0},{2,3},{3,2},{4,5},{5,4},{6,7},{7,6},{8,9},{9,8},{10,11... | collective-permute-start | bytes 6340616 | tf_op jit(solution)/shard_map/ppermute | solution.py:336
  47.9 10.5 %collective-permute-start.6 = (f32[136,512]{1,0:T(8,128)S(1)}, f32[136,512]{1,0:T(8,128)S(1)}, u32[]{:S(2)}, u32[]{:S(2)}) collective-permute-start(f32[136,512]{1,0:T(8,128)S(1)} %get-tuple-element.103.refs_2_), channel_id=1, source_target_pairs={{0,8},{1,9},{2,10},{3,11},{4,12},{5,13},{6,14},{7,15},{8,0},{9,1},... | collective-permute-start | bytes 835592 | tf_op jit(solution)/shard_map/ppermute | solution.py:336
  51.1 11.3 %collective-permute-start.11 = (f32[264,512]{1,0:T(8,128)S(1)}, f32[264,512]{1,0:T(8,128)S(1)}, u32[]{:S(2)}, u32[]{:S(2)}) collective-permute-start(f32[264,512]{1,0:T(8,128)S(1)} %get-tuple-element.107.refs_2_), channel_id=1, source_target_pairs={{0,2},{1,5},{2,0},{3,7},{4,6},{5,1},{6,4},{7,3},{8,10},{9,13},{10,... | collective-permute-start | bytes 1622024 | tf_op jit(solution)/shard_map/ppermute | solution.py:336
  52.0 20.1 %collective-permute-start.10 = (f32[520,512]{1,0:T(8,128)S(1)}, f32[520,512]{1,0:T(8,128)S(1)}, u32[]{:S(2)}, u32[]{:S(2)}) collective-permute-start(f32[520,512]{1,0:T(8,128)S(1)} %get-tuple-element.108.refs_2_), channel_id=1, source_target_pairs={{0,4},{1,3},{2,6},{3,1},{4,0},{5,7},{6,2},{7,5},{8,12},{9,11},{10,... | collective-permute-start | bytes 3194888 | tf_op jit(solution)/shard_map/ppermute | solution.py:336
  55.5 23.4 %collective-permute-start.14 = (f32[264,512]{1,0:T(8,128)}, f32[264,512]{1,0:T(8,128)}, u32[]{:S(2)}, u32[]{:S(2)}) collective-permute-start(f32[264,512]{1,0:T(8,128)} %get-tuple-element.109.refs_2_), channel_id=1, source_target_pairs={{0,4},{1,3},{2,6},{3,1},{4,0},{5,7},{6,2},{7,5},{8,12},{9,11},{10,... | collective-permute-start | bytes 1622024 | tf_op jit(solution)/shard_map/ppermute | solution.py:336
  58.5 14.7 %collective-permute-start.9 = (f32[136,512]{1,0:T(8,128)S(1)}, f32[136,512]{1,0:T(8,128)S(1)}, u32[]{:S(2)}, u32[]{:S(2)}) collective-permute-start(f32[136,512]{1,0:T(8,128)S(1)} %r03.1.refs_2_.refs_0_), channel_id=1, source_target_pairs={{0,24},{1,25},{2,26},{3,27},{4,28},{5,29},{6,30},{7,31},{8,16},{9,... | collective-permute-start | bytes 835592 | tf_op jit(solution)/shard_map/ppermute | solution.py:336
  62.5 12.1 %collective-permute-start.15 = (f32[136,512]{1,0:T(8,128)S(1)}, f32[136,512]{1,0:T(8,128)S(1)}, u32[]{:S(2)}, u32[]{:S(2)}) collective-permute-start(f32[136,512]{1,0:T(8,128)S(1)} %get-tuple-element.112.rest_0_), channel_id=1, source_target_pairs={{0,8},{1,9},{2,10},{3,11},{4,12},{5,13},{6,14},{7,15},{8,0},{9,1},... | collective-permute-start | bytes 835592 | tf_op jit(solution)/shard_map/ppermute | solution.py:336
  72.2 10.4 %collective-permute-start.13 = (f32[264,512]{1,0:T(8,128)S(1)}, f32[264,512]{1,0:T(8,128)S(1)}, u32[]{:S(2)}, u32[]{:S(2)}) collective-permute-start(f32[264,512]{1,0:T(8,128)S(1)} %get-tuple-element.115.refs_2_), channel_id=1, source_target_pairs={{0,2},{1,5},{2,0},{3,7},{4,6},{5,1},{6,4},{7,3},{8,10},{9,13},{10,... | collective-permute-start | bytes 1622024 | tf_op jit(solution)/shard_map/ppermute | solution.py:336
  73.2 10.9 %collective-permute-start.12 = (f32[128,512]{1,0:T(8,128)S(1)}, f32[128,512]{1,0:T(8,128)S(1)}, u32[]{:S(2)}, u32[]{:S(2)}) collective-permute-start(f32[128,512]{1,0:T(8,128)S(1)} %get-tuple-element.116.refs_2_.refs_0_), channel_id=1, source_target_pairs={{0,8},{1,9},{2,10},{3,11},{4,12},{5,13},{6,14},{7,15},{8,0},{9,1},... | collective-permute-start | bytes 786440 | tf_op jit(solution)/shard_map/ppermute | solution.py:336
  74.6 12.8 %collective-permute-start.17 = (f32[136,512]{1,0:T(8,128)S(1)}, f32[136,512]{1,0:T(8,128)S(1)}, u32[]{:S(2)}, u32[]{:S(2)}) collective-permute-start(f32[136,512]{1,0:T(8,128)S(1)} %r23.1.refs_2_.refs_0_), channel_id=1, source_target_pairs={{0,24},{1,25},{2,26},{3,27},{4,28},{5,29},{6,30},{7,31},{8,16},{9,... | collective-permute-start | bytes 835592 | tf_op jit(solution)/shard_map/ppermute | solution.py:336
  82.7 13.6 %collective-permute-start.22 = (f32[136,512]{1,0:T(8,128)S(1)}, f32[136,512]{1,0:T(8,128)S(1)}, u32[]{:S(2)}, u32[]{:S(2)}) collective-permute-start(f32[136,512]{1,0:T(8,128)S(1)} %get-tuple-element.121.refs_2_), channel_id=1, source_target_pairs={{0,8},{1,9},{2,10},{3,11},{4,12},{5,13},{6,14},{7,15},{8,0},{9,1},... | collective-permute-start | bytes 835592 | tf_op jit(solution)/shard_map/ppermute | solution.py:336
  84.1 8.4 %collective-permute-start.16 = (f32[256,512]{1,0:T(8,128)S(1)}, f32[256,512]{1,0:T(8,128)S(1)}, u32[]{:S(2)}, u32[]{:S(2)}) collective-permute-start(f32[256,512]{1,0:T(8,128)S(1)} %a01.1.refs_2_.refs_0_), channel_id=1, source_target_pairs={{0,2},{1,5},{2,0},{3,7},{4,6},{5,1},{6,4},{7,3},{8,10},{9,13},{10,... | collective-permute-start | bytes 1572872 | tf_op jit(solution)/shard_map/ppermute | solution.py:336
  85.8 13.6 %collective-permute-start.21 = (f32[136,512]{1,0:T(8,128)S(1)}, f32[136,512]{1,0:T(8,128)S(1)}, u32[]{:S(2)}, u32[]{:S(2)}) collective-permute-start(f32[136,512]{1,0:T(8,128)S(1)} %r13.1.refs_2_.refs_0_), channel_id=1, source_target_pairs={{0,24},{1,25},{2,26},{3,27},{4,28},{5,29},{6,30},{7,31},{8,16},{9,... | collective-permute-start | bytes 835592 | tf_op jit(solution)/shard_map/ppermute | solution.py:336
  88.0 17.3 %collective-permute-start.20 = (f32[128,512]{1,0:T(8,128)S(1)}, f32[128,512]{1,0:T(8,128)S(1)}, u32[]{:S(2)}, u32[]{:S(2)}) collective-permute-start(f32[128,512]{1,0:T(8,128)S(1)} %get-tuple-element.123.refs_2_.refs_0_), channel_id=1, source_target_pairs={{0,8},{1,9},{2,10},{3,11},{4,12},{5,13},{6,14},{7,15},{8,0},{9,1},... | collective-permute-start | bytes 786440 | tf_op jit(solution)/shard_map/ppermute | solution.py:336
  95.1 16.8 %collective-permute-start.19 = (f32[512,512]{1,0:T(8,128)S(1)}, f32[512,512]{1,0:T(8,128)S(1)}, u32[]{:S(2)}, u32[]{:S(2)}) collective-permute-start(f32[512,512]{1,0:T(8,128)S(1)} %a02.1.refs_2_.rest_0_), channel_id=1, source_target_pairs={{0,4},{1,3},{2,6},{3,1},{4,0},{5,7},{6,2},{7,5},{8,12},{9,11},{10,... | collective-permute-start | bytes 3145736 | tf_op jit(solution)/shard_map/ppermute | solution.py:336
  96.4 15.5 %collective-permute-start.26 = (f32[136,512]{1,0:T(8,128)S(1)}, f32[136,512]{1,0:T(8,128)S(1)}, u32[]{:S(2)}, u32[]{:S(2)}) collective-permute-start(f32[136,512]{1,0:T(8,128)S(1)} %r33.1.refs_2_.refs_0_), channel_id=1, source_target_pairs={{0,24},{1,25},{2,26},{3,27},{4,28},{5,29},{6,30},{7,31},{8,16},{9,... | collective-permute-start | bytes 835592 | tf_op jit(solution)/shard_map/ppermute | solution.py:336
  100.9 10.9 %collective-permute-start.25 = (f32[128,512]{1,0:T(8,128)S(1)}, f32[128,512]{1,0:T(8,128)S(1)}, u32[]{:S(2)}, u32[]{:S(2)}) collective-permute-start(f32[128,512]{1,0:T(8,128)S(1)} %get-tuple-element.125.rest_0_.refs_0_), channel_id=1, source_target_pairs={{0,2},{1,5},{2,0},{3,7},{4,6},{5,1},{6,4},{7,3},{8,10},{9,13},{10,... | collective-permute-start | bytes 786440 | tf_op jit(solution)/shard_map/ppermute | solution.py:336
  105.4 12.6 %collective-permute-start.24 = (f32[256,512]{1,0:T(8,128)S(1)}, f32[256,512]{1,0:T(8,128)S(1)}, u32[]{:S(2)}, u32[]{:S(2)}) collective-permute-start(f32[256,512]{1,0:T(8,128)S(1)} %a21.1.refs_2_.refs_0_), channel_id=1, source_target_pairs={{0,2},{1,5},{2,0},{3,7},{4,6},{5,1},{6,4},{7,3},{8,10},{9,13},{10,... | collective-permute-start | bytes 1572872 | tf_op jit(solution)/shard_map/ppermute | solution.py:336
  111.9 12.7 %collective-permute-start.29 = (f32[128,512]{1,0:T(8,128)S(1)}, f32[128,512]{1,0:T(8,128)}, u32[]{:S(2)}, u32[]{:S(2)}) collective-permute-start(f32[128,512]{1,0:T(8,128)S(1)} %get-tuple-element.128.refs_2_.refs_0_), channel_id=1, source_target_pairs={{0,8},{1,9},{2,10},{3,11},{4,12},{5,13},{6,14},{7,15},{8,0},{9,1},... | collective-permute-start | bytes 786440 | tf_op jit(solution)/shard_map/ppermute | solution.py:336
  116.5 9.3 %collective-permute-start.32 = (f32[256,512]{1,0:T(8,128)S(1)}, f32[256,512]{1,0:T(8,128)S(1)}, u32[]{:S(2)}, u32[]{:S(2)}) collective-permute-start(f32[256,512]{1,0:T(8,128)S(1)} %a11.1.refs_2_.refs_0_), channel_id=1, source_target_pairs={{0,4},{1,3},{2,6},{3,1},{4,0},{5,7},{6,2},{7,5},{8,12},{9,11},{10,... | collective-permute-start | bytes 1572872 | tf_op jit(solution)/shard_map/ppermute | solution.py:336
  122.6 19.6 %collective-permute-start.28 = (f32[512,512]{1,0:T(8,128)S(1)}, f32[512,512]{1,0:T(8,128)S(1)}, u32[]{:S(2)}, u32[]{:S(2)}) collective-permute-start(f32[512,512]{1,0:T(8,128)S(1)} %a22.1.refs_2_.rest_0_), channel_id=1, source_target_pairs={{0,4},{1,3},{2,6},{3,1},{4,0},{5,7},{6,2},{7,5},{8,12},{9,11},{10,... | collective-permute-start | bytes 3145736 | tf_op jit(solution)/shard_map/ppermute | solution.py:336
  122.6 9.2 %collective-permute-start.31 = (f32[512,512]{1,0:T(8,128)S(1)}, f32[512,512]{1,0:T(8,128)S(1)}, u32[]{:S(2)}, u32[]{:S(2)}) collective-permute-start(f32[512,512]{1,0:T(8,128)S(1)} %collective-permute-done.19.refs_3_.rest_1_), channel_id=1, source_target_pairs={{0,1},{1,0},{2,3},{3,2},{4,5},{5,4},{6,7},{7,6},{8,9},{9,8},{10,11... | collective-permute-start | bytes 3145736 | tf_op jit(solution)/shard_map/ppermute | solution.py:336
  125.7 14.1 %collective-permute-start.30 = (f32[256,512]{1,0:T(8,128)S(1)}, f32[256,512]{1,0:T(8,128)S(1)}, u32[]{:S(2)}, u32[]{:S(2)}) collective-permute-start(f32[256,512]{1,0:T(8,128)S(1)} %a31.1.refs_2_.refs_0_), channel_id=1, source_target_pairs={{0,2},{1,5},{2,0},{3,7},{4,6},{5,1},{6,4},{7,3},{8,10},{9,13},{10,... | collective-permute-start | bytes 1572872 | tf_op jit(solution)/shard_map/ppermute | solution.py:336
  125.8 13.9 %collective-permute-start.33 = (f32[512,512]{1,0:T(8,128)S(1)}, f32[512,512]{1,0:T(8,128)S(1)}, u32[]{:S(2)}, u32[]{:S(2)}) collective-permute-start(f32[512,512]{1,0:T(8,128)S(1)} %a12.1.rest_2_.rest_0_), channel_id=1, source_target_pairs={{0,1},{1,0},{2,3},{3,2},{4,5},{5,4},{6,7},{7,6},{8,9},{9,8},{10,11... | collective-permute-start | bytes 3145736 | tf_op jit(solution)/shard_map/ppermute | solution.py:336
  131.7 24.7 %collective-permute-start.37 = (f32[512,512]{1,0:T(8,128)S(1)}, f32[512,512]{1,0:T(8,128)S(1)}, u32[]{:S(2)}, u32[]{:S(2)}) collective-permute-start(f32[512,512]{1,0:T(8,128)S(1)} %a12.1.rest_2_.rest_0_), channel_id=1, source_target_pairs={{0,8},{1,9},{2,10},{3,11},{4,12},{5,13},{6,14},{7,15},{8,0},{9,1},... | collective-permute-start | bytes 3145736 | tf_op jit(solution)/shard_map/ppermute | solution.py:336
  139.8 9.5 %collective-permute-start.35 = (f32[512,512]{1,0:T(8,128)S(1)}, f32[512,512]{1,0:T(8,128)S(1)}, u32[]{:S(2)}, u32[]{:S(2)}) collective-permute-start(f32[512,512]{1,0:T(8,128)S(1)} %a32.1.rest_2_.rest_0_), channel_id=1, source_target_pairs={{0,1},{1,0},{2,3},{3,2},{4,5},{5,4},{6,7},{7,6},{8,9},{9,8},{10,11... | collective-permute-start | bytes 3145736 | tf_op jit(solution)/shard_map/ppermute | solution.py:336
  141.5 17.7 %collective-permute-start.36 = (f32[512,512]{1,0:T(8,128)S(1)}, f32[512,512]{1,0:T(8,128)S(1)}, u32[]{:S(2)}, u32[]{:S(2)}) collective-permute-start(f32[512,512]{1,0:T(8,128)S(1)} %a32.1.rest_2_.rest_0_), channel_id=1, source_target_pairs={{0,4},{1,3},{2,6},{3,1},{4,0},{5,7},{6,2},{7,5},{8,12},{9,11},{10,... | collective-permute-start | bytes 3145736 | tf_op jit(solution)/shard_map/ppermute | solution.py:336
  (26 other events, 360.6 us)

commit v4 on v3

--- a/solution.py
+++ b/solution.py
@@ -14,9 +14,9 @@
 GROUPS = ((4, "xyz"), (4, "zxy"), (4, "xyz"), (4, "xyz"))
 ORDER = (
     "g0", "g1", "r00", "g2", "r10", "r20", "r01", "g3", "f0", "r02+c3_", "r21", "r30", "r11", "r03", "r22",
-    "f1", "r31", "a00", "r23", "r12", "r32", "a01", "r13", "a20", "a02", "r33", "a10+C00", "f2", "a21",
-    "a30+A02+A10", "a11", "a22", "c0", "a31", "a12+C20", "w01", "a32+C10", "c2", "w20", "f3*w00*w21+C30", "c1",
-    "w10", "c3", "w11", "w30", "w31",
+    "f1", "r31", "a00", "r23", "r12", "r32", "a01", "r13", "a20", "a02", "f2", "r33+C00", "a10", "a21",
+    "a30+A02+A10", "a11", "a22", "c0", "a31", "a12+C01+C20", "w01", "a32+C10", "w00", "c2", "w20",
+    "f3*w21+C30", "c1", "w10", "c3", "w11", "w30", "w31",
 )
 
 COST = pl.CostEstimate(flops=25 * 10**9, bytes_accessed=2**20, transcendentals=0)
@@ -90,13 +90,28 @@
     )(*(pltpu.with_memory_space_constraint(v, pltpu.HBM) for v in inputs), base)
 
 
-def layer_kernel(start, line, base_ref, mixed_ref, weight_ref, bias_ref, cot_ref, *rest):
+def emit_half(slot, here, base_ref, mixed_ref, gp_ref, total, out_ref):
+    half = mixed_ref.shape[1] // 4
+    chunk = half // 4
+    for j in range(2):
+        from_row = pl.multiple_of((base_ref[slot] // 8) * 2 * half + j * half, half)
+        share = lax.dot_general(
+            mixed_ref[:, pl.ds(from_row, half)],
+            gp_ref[:, here],
+            (((0,), (0,)), ((), ())),
+            preferred_element_type=F32,
+        )
+        for m in range(4):
+            spot = ((j * 4 + m) ^ (base_ref[slot] % 8)) * chunk
+            out_ref[pl.ds(pl.multiple_of(spot, chunk), chunk), :] = share[m * chunk : (m + 1) * chunk]
+    out_ref[2 * half :, :] = total
+
+
+def layer_kernel(start, line, halves, base_ref, mixed_ref, weight_ref, bias_ref, cot_ref, *rest):
     act_ref, cot_in, act_sem, cot_sem = rest[-4:]
-    act_out, gp_ref, theirs_ref, mine_ref = rest[-8:-4]
+    act_out, gp_ref, *outs = rest[-6 - halves : -4]
     rows, cols = act_ref.shape
     block = min(rows, 512)
-    half = mixed_ref.shape[1] // 4
-    chunk = half // 4
     here = slice(start, start + cols)
     load = pltpu.make_async_copy(cot_ref.at[:, pl.ds(start, cols)], cot_in, cot_sem)
     load.start()
@@ -113,35 +128,44 @@
     store = pltpu.make_async_copy(act_ref, act_out.at[:, pl.ds(start, cols)], act_sem)
     store.start()
 
-    def share_of(from_row):
-        return lax.dot_general(
-            mixed_ref[:, pl.ds(from_row, half)],
-            gp_ref[:, here],
-            (((0,), (0,)), ((), ())),
-            preferred_element_type=F32,
-        )
-
     total = jnp.broadcast_to(total, (8, cols))
-    for side, out_ref in ((0, theirs_ref), (1, mine_ref)):
-        for j in range(2):
-            share = share_of(pl.multiple_of((base_ref[line + side] // 8) * 2 * half + j * half, half))
-            for m in range(4):
-                spot = ((j * 4 + m) ^ (base_ref[line + side] % 8)) * chunk
-                out_ref[pl.ds(pl.multiple_of(spot, chunk), chunk), :] = share[m * chunk : (m + 1) * chunk]
-        out_ref[2 * half :, :] = total
+    for side, out_ref in enumerate(outs):
+        emit_half(line + side, here, base_ref, mixed_ref, gp_ref, total, out_ref)
     store.wait()
 
 
-def layer_group(name, base, line, mixed, weight, bias, cotangent, waits, carried, start, cols):
+def other_half_kernel(slot, start, base_ref, mixed_ref, gp_ref, theirs_ref, *rest):
+    out_ref = rest[-1]
+    here = slice(start, start + out_ref.shape[1])
+    emit_half(slot, here, base_ref, mixed_ref, gp_ref, theirs_ref[out_ref.shape[0] - 8 :, :], out_ref)
+
+
+def other_half(name, base, slot, mixed, gp, theirs, waits, start):
+    return pl.pallas_call(
+        functools.partial(other_half_kernel, slot, start),
+        grid_spec=pltpu.PrefetchScalarGridSpec(
+            num_scalar_prefetch=1,
+            grid=(1,),
+            in_specs=[VMEM] * 3 + [ANY] * len(waits),
+            out_specs=VMEM,
+        ),
+        out_shape=jax.ShapeDtypeStruct(theirs.shape, F32),
+        compiler_params=pltpu.CompilerParams(vmem_limit_bytes=10 * 2**20),
+        cost_estimate=COST,
+        name=name,
+    )(base, mixed, gp, theirs, *waits)
+
+
+def layer_group(name, base, line, halves, mixed, weight, bias, cotangent, waits, carried, start, cols):
     rows, width = mixed.shape
     share = jax.ShapeDtypeStruct((width // 2 + 8, cols), F32)
     return pl.pallas_call(
-        functools.partial(layer_kernel, start, line),
+        functools.partial(layer_kernel, start, line, halves),
         grid_spec=pltpu.PrefetchScalarGridSpec(
             num_scalar_prefetch=1,
             grid=(1,),
             in_specs=[VMEM, VMEM, VMEM, ANY] + [ANY] * len(waits) + ([ANY, VMEM] if carried else []),
-            out_specs=[ANY, VMEM, VMEM, VMEM],
+            out_specs=[ANY, VMEM] + [VMEM] * halves,
             scratch_shapes=[
                 pltpu.VMEM((rows, cols), BF16),
                 pltpu.VMEM((rows, cols), BF16),
@@ -152,9 +176,8 @@
         out_shape=[
             jax.ShapeDtypeStruct((rows, width), BF16),
             jax.ShapeDtypeStruct((rows, width), BF16),
-            share,
-            share,
-        ],
+        ]
+        + [share] * halves,
         input_output_aliases={5 + len(waits): 0, 6 + len(waits): 1} if carried else {},
         compiler_params=pltpu.CompilerParams(vmem_limit_bytes=10 * 2**20),
         cost_estimate=COST,
@@ -376,7 +399,7 @@
     token = prop_t
     end = width // 16
 
-    flight = {}
+    flight, sent = {}, {}
 
     def halves(names):
         jobs, pieces = [], []
@@ -393,13 +416,28 @@
         stage = int(event[2]) if len(event) > 2 else 0
         waits = [token] + [flight[name] for name in early]
         if what == "g":
-            act, gp, theirs, mine = layer_group(
-                event, base, line[kinds[g]], mixed, weight, bias, cotangent, waits, carried, starts[g], sizes[g]
+            act, gp, theirs, *mine = layer_group(
+                event,
+                base,
+                line[kinds[g]],
+                1 if f"m{g}" in ORDER else 2,
+                mixed,
+                weight,
+                bias,
+                cotangent,
+                waits,
+                carried,
+                starts[g],
+                sizes[g],
             )
             carried = [act, gp]
+            sent[g] = theirs
+            terms[g] = mine + [swap(theirs, core)]
+            flight[f"c{g}_"] = terms[g][-1]
             token = theirs
-            terms[g] = [mine, swap(theirs, core)]
-            flight[f"c{g}_"] = terms[g][1]
+        elif what == "m":
+            token = other_half(event, base, line[kinds[g]] + 1, mixed, carried[1], sent[g], waits, starts[g])
+            terms[g] = [token] + terms[g]
         elif what == "r" and stage < 3:
             n = (width // 2) >> (stage + 1)
             send, keep = join(

time: 166 us -> 164 us (0.988)
  starting transfers between devices: 50.4 us -> 39.5 us
  waiting for transfers between devices: 41.7 us -> 48.2 us
  Pallas kernels: 68.1 us -> 69.9 us
    ppermute x40, starting transfers between devices: 50.4 us -> 39.5 us  [swap(): lax.ppermute(value, axes, [(i, i ^ pair[i & 1]) for i in range(devices)])]
    ppermute x40, waiting for transfers between devices: 41.7 us -> 48.2 us  [swap(): lax.ppermute(value, axes, [(i, i ^ pair[i & 1]) for i in range(devices)])]
    pallas_call x6 -> x7, Pallas kernels: 12.1 us -> 14 us  [place(): pl.pallas_call(functools.partial(place_kernel, jobs), grid_spec=pltpu.Pre...]
  transfers between devices with their start and end apart: 40 -> 40, of which waited for: 20 -> 20; matrix products, arithmetic and copies ran while one was open for 0% -> 0% of each run, Pallas kernels for 33% -> 35%
where the time goes in v4:
time: 164 us; the launch traced here: 163 us
  Pallas kernels  69.9 us (43%)
  waiting for transfers between devices  48.2 us (29%)
  starting transfers between devices  39.5 us (24%)
  local copies, waits for them, and re-layouts  4.28 us (3%)
    ppermute x40, waiting for transfers between devices, swap(): lax.ppermute(value, axes, [(i, i ^ pair[i & 1]) for i in range(devices)])  48.2 us
    ppermute x40, starting transfers between devices, swap(): lax.ppermute(value, axes, [(i, i ^ pair[i & 1]) for i in range(devices)])  39.5 us
    pallas_call x4, Pallas kernels, layer_group(): pl.pallas_call(functools.partial(layer_kernel, start, line, halves), grid...  24.5 us
    pallas_call x4, Pallas kernels, back(): pl.pallas_call(functools.partial(back_kernel, index, jobs), grid_spec=plt...  17.6 us
    pallas_call x7, Pallas kernels, place(): pl.pallas_call(functools.partial(place_kernel, jobs), grid_spec=pltpu.Pre...  14 us
    pallas_call x28, Pallas kernels, join(): pl.pallas_call(functools.partial(join_kernel, plan), in_specs=[VMEM] * le...  7.33 us
    pallas_call x1, Pallas kernels, propagate(): pl.pallas_call(tile_kernel, grid=(tiles // each,), in_specs=[pl.BlockSpec...  5.04 us
    unnamed x36, local copies, waits for them, and re-layouts  4.28 us
  transfers between devices with their start and end apart: 40, of which 20 were waited for; matrix products, arithmetic and copies ran while one was open for 0% of the time, Pallas kernels for 35%

profile of v4, /device:TPU:19, one launch (start us, length us, event | category | flops | bytes accessed | tf_op | source)
XLA Modules:
  0.0 163.2 jit_solution(10299128179489199414)
XLA Ops:
  0.8 5.0 %propagate.1 = (bf16[8,128,128]{2,1,0:T(8,128)(2,1)S(1)}, bf16[1024,2048]{1,0:T(8,128)(2,1)S(1)}) custom-call(s32[64,1024]{1,0:T(8,128)} %bitcast.17, s32[64,1024]{1,0:T(8,128)} %bitcast.18, s32[8,1,128]{2,1,0:T(1,128)} %bitcast.19, s32[8,1,128]{2,1,0:T(1,128)} %bitcast.20, bf16[1024,2048]{1,0:T(8,128)(2,1)} %features_ref.1, s32[4]{0:T(128)S(1)} %pad_add_fusion.base_ref), custom_call_target="tpu_custom_call" | custom-call | flops 4294967296 | bytes 4194304 | tf_op jit(solution)/shard_map/propagate/pallas_call | solution.py:69
  5.8 5.9 %g0.1 = (bf16[1024,2048]{1,0:T(8,128)(2,1)}, bf16[1024,2048]{1,0:T(8,128)(2,1)S(1)}, f32[1032,512]{1,0:T(8,128)S(1)}, f32[1032,512]{1,0:T(8,128)S(1)}) custom-call(s32[4]{0:T(128)S(1)} %pad_add_fusion.base_ref, bf16[1024,2048]{1,0:T(8,128)(2,1)S(1)} %get-tuple-element.80.mixed_ref, bf16[2048,2048]{1,0:T(8,128)(2,1)S(1)} %copy-done.6, ...), custom_call_target="tpu_custom_call" | custom-call | flops 24999999488 | bytes 1048576 | tf_op jit(solution)/shard_map/g0/pallas_call | solution.py:162
  12.4 6.2 %g1.1 = (bf16[1024,2048]{1,0:T(8,128)(2,1)}, bf16[1024,2048]{1,0:T(8,128)(2,1)S(1)}, f32[1032,512]{1,0:T(8,128)S(1)}, f32[1032,512]{1,0:T(8,128)S(1)}) custom-call(s32[4]{0:T(128)S(1)} %pad_add_fusion.base_ref, bf16[1024,2048]{1,0:T(8,128)(2,1)S(1)} %get-tuple-element.80.mixed_ref, ...), custom_call_target="tpu_custom_call", output_to_operand_aliasing={{0}: (6, {}), {1}: (7, {})} | custom-call | flops 24999999488 | bytes 1048576 | tf_op jit(solution)/shard_map/g1/pallas_call | solution.py:162
  20.2 6.1 %g2.1 = (bf16[1024,2048]{1,0:T(8,128)(2,1)}, bf16[1024,2048]{1,0:T(8,128)(2,1)S(1)}, f32[1032,512]{1,0:T(8,128)S(1)}, f32[1032,512]{1,0:T(8,128)S(1)}) custom-call(s32[4]{0:T(128)S(1)} %pad_add_fusion.base_ref, bf16[1024,2048]{1,0:T(8,128)(2,1)S(1)} %get-tuple-element.80.mixed_ref, ...), custom_call_target="tpu_custom_call", output_to_operand_aliasing={{0}: (6, {}), {1}: (7, {})} | custom-call | flops 24999999488 | bytes 1048576 | tf_op jit(solution)/shard_map/g2/pallas_call | solution.py:162
  33.7 6.4 %g3.1 = (bf16[1024,2048]{1,0:T(8,128)(2,1)}, bf16[1024,2048]{1,0:T(8,128)(2,1)S(1)}, f32[1032,512]{1,0:T(8,128)S(1)}, f32[1032,512]{1,0:T(8,128)S(1)}) custom-call(s32[4]{0:T(128)S(1)} %pad_add_fusion.base_ref, bf16[1024,2048]{1,0:T(8,128)(2,1)S(1)} %get-tuple-element.80.mixed_ref, ...), custom_call_target="tpu_custom_call", output_to_operand_aliasing={{0}: (6, {}), {1}: (7, {})} | custom-call | flops 24999999488 | bytes 1048576 | tf_op jit(solution)/shard_map/g3/pallas_call | solution.py:162
  40.0 2.5 %collective-permute-start.6 = (f32[1032,512]{1,0:T(8,128)S(1)}, f32[1032,512]{1,0:T(8,128)S(1)}, u32[]{:S(2)}, u32[]{:S(2)}) collective-permute-start(f32[1032,512]{1,0:T(8,128)S(1)} %get-tuple-element.103.rest_0_), channel_id=1, source_target_pairs={{0,1},{1,0},{2,3},{3,2},{4,5},{5,4},{6,7},{7,6},{8,9},{9,8},{10,11... | collective-permute-start | bytes 6340616 | tf_op jit(solution)/shard_map/ppermute | solution.py:359
  42.6 4.4 %f0.1 = (bf16[1024,2048]{1,0:T(8,128)(2,1)}, f32[8,128]{1,0:T(8,128)S(1)}) custom-call(s32[4]{0:T(128)S(1)} %pad_add_fusion.base_ref, bf16[1024,2048]{1,0:T(8,128)(2,1)S(1)} %get-tuple-element.100.gp_ref, bf16[2048,2048]{1,0:T(8,128)(2,1)S(1)} %copy-done.6, bf16[8,128,128]{2,1,0:T(8,128)(2,1)S(1)} %get-tuple-element.81.rest_0_.prop_ref, ...), custom_call_target="tpu_custom_call" | custom-call | flops 24999999488 | bytes 1048576 | tf_op jit(solution)/shard_map/f0/pallas_call | solution.py:328
  53.3 2.2 %r11.1 = (f32[264,512]{1,0:T(8,128)}, f32[264,512]{1,0:T(8,128)S(1)}) custom-call(f32[520,512]{1,0:T(8,128)S(1)} %get-tuple-element.109.refs_0_, f32[520,512]{1,0:T(8,128)} %collective-permute-done.9.refs_1_, f32[520,512]{1,0:T(8,128)S(1)} %get-tuple-element.111.refs_2_), custom_call_target="tpu_custom_call" | custom-call | flops 24999999488 | bytes 1048576 | tf_op jit(solution)/shard_map/r11/pallas_call | solution.py:210
  56.3 2.1 %collective-permute-done.8.refs_1_ = f32[136,512]{1,0:T(8,128)S(1)} collective-permute-done((f32[136,512]{1,0:T(8,128)S(1)}, f32[136,512]{1,0:T(8,128)S(1)}, u32[]{:S(2)}, u32[]{:S(2)}) %collective-permute-start.8) | collective-permute-done | bytes 278560 | tf_op jit(solution)/shard_map/ppermute | solution.py:359
  58.7 3.7 %collective-permute-done.7.refs_1_ = f32[264,512]{1,0:T(8,128)S(1)} collective-permute-done((f32[264,512]{1,0:T(8,128)S(1)}, f32[264,512]{1,0:T(8,128)S(1)}, u32[]{:S(2)}, u32[]{:S(2)}) %collective-permute-start.7) | collective-permute-done | bytes 540704 | tf_op jit(solution)/shard_map/ppermute | solution.py:359
  63.8 4.4 %f1.1 = (bf16[1024,2048]{1,0:T(8,128)(2,1)}, f32[8,128]{1,0:T(8,128)S(1)}) custom-call(s32[4]{0:T(128)S(1)} %pad_add_fusion.base_ref, bf16[1024,2048]{1,0:T(8,128)(2,1)S(1)} %get-tuple-element.100.gp_ref, bf16[2048,2048]{1,0:T(8,128)(2,1)S(1)} %copy-done.6, ...), custom_call_target="tpu_custom_call", output_to_operand_aliasing={{0}: (5, {})} | custom-call | flops 24999999488 | bytes 1048576 | tf_op jit(solution)/shard_map/f1/pallas_call | solution.py:328
  68.2 3.9 %collective-permute-done.12.refs_1_ = f32[520,512]{1,0:T(8,128)S(1)} collective-permute-done((f32[520,512]{1,0:T(8,128)S(1)}, f32[520,512]{1,0:T(8,128)S(1)}, u32[]{:S(2)}, u32[]{:S(2)}) %collective-permute-start.12) | collective-permute-done | bytes 1064992 | tf_op jit(solution)/shard_map/ppermute | solution.py:359
  74.7 4.2 %collective-permute-done.14.refs_1_ = f32[264,512]{1,0:T(8,128)} collective-permute-done((f32[264,512]{1,0:T(8,128)}, f32[264,512]{1,0:T(8,128)}, u32[]{:S(2)}, u32[]{:S(2)}) %collective-permute-start.14) | collective-permute-done | bytes 540704 | tf_op jit(solution)/shard_map/ppermute | solution.py:359
  88.9 3.6 %collective-permute-done.21.refs_1_ = f32[256,512]{1,0:T(8,128)S(1)} collective-permute-done((f32[256,512]{1,0:T(8,128)S(1)}, f32[256,512]{1,0:T(8,128)S(1)}, u32[]{:S(2)}, u32[]{:S(2)}) %collective-permute-start.21) | collective-permute-done | bytes 524320 | tf_op jit(solution)/shard_map/ppermute | solution.py:359
  92.6 2.5 %collective-permute-start.22 = (f32[512,512]{1,0:T(8,128)S(1)}, f32[512,512]{1,0:T(8,128)S(1)}, u32[]{:S(2)}, u32[]{:S(2)}) collective-permute-start(f32[512,512]{1,0:T(8,128)S(1)} %a02.1.rest_0_), channel_id=1, source_target_pairs={{0,1},{1,0},{2,3},{3,2},{4,5},{5,4},{6,7},{7,6},{8,9},{9,8},{10,11... | collective-permute-start | bytes 3145736 | tf_op jit(solution)/shard_map/ppermute | solution.py:359
  96.3 4.4 %f2.1 = (bf16[1024,2048]{1,0:T(8,128)(2,1)}, f32[8,128]{1,0:T(8,128)S(1)}) custom-call(s32[4]{0:T(128)S(1)} %pad_add_fusion.base_ref, bf16[1024,2048]{1,0:T(8,128)(2,1)S(1)} %get-tuple-element.100.gp_ref, bf16[2048,2048]{1,0:T(8,128)(2,1)S(1)} %copy-done.6, ...), custom_call_target="tpu_custom_call", output_to_operand_aliasing={{0}: (5, {})} | custom-call | flops 24999999488 | bytes 1048576 | tf_op jit(solution)/shard_map/f2/pallas_call | solution.py:328
  104.3 8.3 %collective-permute-done.26.refs_3_.rest_1_ = f32[512,512]{1,0:T(8,128)S(1)} collective-permute-done((f32[512,512]{1,0:T(8,128)S(1)}, f32[512,512]{1,0:T(8,128)S(1)}, u32[]{:S(2)}, u32[]{:S(2)}) %collective-permute-start.26) | collective-permute-done | bytes 1048608 | tf_op jit(solution)/shard_map/ppermute | solution.py:359
  112.5 3.4 %collective-permute-done.25.refs_1_ = f32[136,512]{1,0:T(8,128)S(1)} collective-permute-done((f32[136,512]{1,0:T(8,128)S(1)}, f32[136,512]{1,0:T(8,128)S(1)}, u32[]{:S(2)}, u32[]{:S(2)}) %collective-permute-start.25) | collective-permute-done | bytes 278560 | tf_op jit(solution)/shard_map/ppermute | solution.py:359
  118.1 2.3 %collective-permute-start.27 = (f32[512,512]{1,0:T(8,128)S(1)}, f32[512,512]{1,0:T(8,128)S(1)}, u32[]{:S(2)}, u32[]{:S(2)}) collective-permute-start(f32[512,512]{1,0:T(8,128)S(1)} %a22.1.refs_2_.rest_0_), channel_id=1, source_target_pairs={{0,1},{1,0},{2,3},{3,2},{4,5},{5,4},{6,7},{7,6},{8,9},{9,8},{10,11... | collective-permute-start | bytes 3145736 | tf_op jit(solution)/shard_map/ppermute | solution.py:359
  120.4 2.1 %collective-permute-start.31 = (f32[512,512]{1,0:T(8,128)S(1)}, f32[512,512]{1,0:T(8,128)S(1)}, u32[]{:S(2)}, u32[]{:S(2)}) collective-permute-start(f32[512,512]{1,0:T(8,128)S(1)} %collective-permute-done.26.refs_3_.rest_1_), channel_id=1, source_target_pairs={{0,1},{1,0},{2,3},{3,2},{4,5},{5,4},{6,7},{7,6},{8,9},{9,8},{10,11... | collective-permute-start | bytes 3145736 | tf_op jit(solution)/shard_map/ppermute | solution.py:359
  125.0 3.7 %collective-permute-start.33 = (f32[512,512]{1,0:T(8,128)S(1)}, f32[512,512]{1,0:T(8,128)S(1)}, u32[]{:S(2)}, u32[]{:S(2)}) collective-permute-start(f32[512,512]{1,0:T(8,128)S(1)} %a12.1.rest_2_.rest_0_), channel_id=1, source_target_pairs={{0,1},{1,0},{2,3},{3,2},{4,5},{5,4},{6,7},{7,6},{8,9},{9,8},{10,11... | collective-permute-start | bytes 3145736 | tf_op jit(solution)/shard_map/ppermute | solution.py:359
  129.7 1.9 %w01.1 = (f32[2048,2048]{1,0:T(8,128)}, f32[8,128]{1,0:T(8,128)S(1)}) custom-call(s32[4]{0:T(128)S(1)} %copy-done.5, f32[512,512]{1,0:T(8,128)S(1)} %copy-done.10, f32[512,512]{1,0:T(8,128)S(1)} %collective-permute-done.31.refs_3_.rest_1_, f32[512,512]{1,0:T(8,128)S(1)} %a12.1.rest_2_.rest_0_), custom_call_target="tpu_custom_call" | custom-call | flops 24999999488 | bytes 1048576 | tf_op jit(solution)/shard_map/w01/pallas_call | solution.py:250
  131.6 6.8 %collective-permute-done.30.refs_1_ = f32[256,512]{1,0:T(8,128)S(1)} collective-permute-done((f32[256,512]{1,0:T(8,128)S(1)}, f32[256,512]{1,0:T(8,128)S(1)}, u32[]{:S(2)}, u32[]{:S(2)}) %collective-permute-start.30) | collective-permute-done | bytes 524320 | tf_op jit(solution)/shard_map/ppermute | solution.py:359
  138.5 2.5 %collective-permute-start.35 = (f32[512,512]{1,0:T(8,128)S(1)}, f32[512,512]{1,0:T(8,128)S(1)}, u32[]{:S(2)}, u32[]{:S(2)}) collective-permute-start(f32[512,512]{1,0:T(8,128)S(1)} %a32.1.rest_2_.rest_0_), channel_id=1, source_target_pairs={{0,1},{1,0},{2,3},{3,2},{4,5},{5,4},{6,7},{7,6},{8,9},{9,8},{10,11... | collective-permute-start | bytes 3145736 | tf_op jit(solution)/shard_map/ppermute | solution.py:359
  141.0 1.9 %w00.1 = (f32[2048,2048]{1,0:T(8,128)}, f32[8,128]{1,0:T(8,128)S(1)}) custom-call(s32[4]{0:T(128)S(1)} %copy-done.5, f32[512,512]{1,0:T(8,128)S(1)} %copy-done.8, f32[512,512]{1,0:T(8,128)S(1)} %collective-permute-done.26.refs_3_.rest_1_, f32[512,512]{1,0:T(8,128)S(1)} %a32.1.rest_2_.rest_0_, ...), custom_call_target="tpu_custom_call", output_to_operand_aliasing={{0}: (4, {})} | custom-call | flops 24999999488 | bytes 1048576 | tf_op jit(solution)/shard_map/w00/pallas_call | solution.py:250
  143.0 2.0 %collective-permute-start.34 = (f32[512,512]{1,0:T(8,128)S(1)}, f32[512,512]{1,0:T(8,128)S(1)}, u32[]{:S(2)}, u32[]{:S(2)}) collective-permute-start(f32[512,512]{1,0:T(8,128)S(1)} %collective-permute-done.28.rest_1_), channel_id=1, source_target_pairs={{0,1},{1,0},{2,3},{3,2},{4,5},{5,4},{6,7},{7,6},{8,9},{9,8},{10,11... | collective-permute-start | bytes 3145736 | tf_op jit(solution)/shard_map/ppermute | solution.py:359
  144.9 1.9 %w20.1 = (f32[2048,2048]{1,0:T(8,128)}, f32[8,128]{1,0:T(8,128)S(1)}) custom-call(s32[4]{0:T(128)S(1)} %copy-done.5, f32[512,512]{1,0:T(8,128)S(1)} %a22.1.refs_2_.rest_0_, f32[512,512]{1,0:T(8,128)S(1)} %collective-permute-done.28.rest_1_, f32[8,128]{1,0:T(8,128)S(1)} %get-tuple-element.134.rest_2_, ...), custom_call_target="tpu_custom_call", output_to_operand_aliasing={{0}: (4, {})} | custom-call | flops 24999999488 | bytes 1048576 | tf_op jit(solution)/shard_map/w20/pallas_call | solution.py:250
  149.2 4.5 %f3.1 = (bf16[1024,2048]{1,0:T(8,128)(2,1)}, f32[8,128]{1,0:T(8,128)S(1)}, f32[2048,2048]{1,0:T(8,128)}) custom-call(s32[4]{0:T(128)S(1)} %copy-done.5, bf16[1024,2048]{1,0:T(8,128)(2,1)S(1)} %copy-done.15, bf16[2048,2048]{1,0:T(8,128)(2,1)S(1)} %bitcast.11, bf16[8,128,128]{2,1,0:T(8,128)(2,1)S(1)} %copy-done.13, ...), custom_call_target="tpu_custom_call", output_to_operand_aliasing={{0}: (8, {}), {2}: (9, {})} | custom-call | flops 24999999488 | bytes 1048576 | tf_op jit(solution)/shard_map/f3/pallas_call | solution.py:328
  154.3 1.9 %w10.1 = (f32[2048,2048]{1,0:T(8,128)}, f32[8,128]{1,0:T(8,128)S(1)}) custom-call(s32[4]{0:T(128)S(1)} %copy-done.5, f32[512,512]{1,0:T(8,128)S(1)} %a12.1.rest_2_.rest_0_, f32[512,512]{1,0:T(8,128)S(1)} %collective-permute-done.37.rest_1_, f32[8,128]{1,0:T(8,128)S(1)} %get-tuple-element.141.rest_2_, ...), custom_call_target="tpu_custom_call", output_to_operand_aliasing={{0}: (4, {})} | custom-call | flops 24999999488 | bytes 1048576 | tf_op jit(solution)/shard_map/w10/pallas_call | solution.py:250
  156.6 1.9 %w11.1 = (f32[2048,2048]{1,0:T(8,128)}, f32[8,128]{1,0:T(8,128)S(1)}) custom-call(s32[4]{0:T(128)S(1)} %copy-done.5, f32[512,512]{1,0:T(8,128)S(1)} %collective-permute-done.33.refs_3_.rest_0_, f32[512,512]{1,0:T(8,128)S(1)} %collective-permute-done.39.rest_1_, f32[8,128]{1,0:T(8,128)S(1)} %get-tuple-element.144.rest_2_, ...), custom_call_target="tpu_custom_call", output_to_operand_aliasing={{0}: (4, {})} | custom-call | flops 24999999488 | bytes 1048576 | tf_op jit(solution)/shard_map/w11/pallas_call | solution.py:250
  158.5 1.9 %w30.1 = (f32[2048,2048]{1,0:T(8,128)}, f32[8,128]{1,0:T(8,128)S(1)}) custom-call(s32[4]{0:T(128)S(1)} %copy-done.5, f32[512,512]{1,0:T(8,128)S(1)} %a32.1.rest_2_.rest_0_, f32[512,512]{1,0:T(8,128)S(1)} %collective-permute-done.36.rest_1_, f32[8,128]{1,0:T(8,128)S(1)} %get-tuple-element.147.rest_2_, ...), custom_call_target="tpu_custom_call", output_to_operand_aliasing={{0}: (4, {})} | custom-call | flops 24999999488 | bytes 1048576 | tf_op jit(solution)/shard_map/w30/pallas_call | solution.py:250
  160.5 2.5 %w31.1 = (f32[2048,2048]{1,0:T(8,128)}, f32[8,128]{1,0:T(8,128)}) custom-call(s32[4]{0:T(128)S(1)} %copy-done.5, f32[512,512]{1,0:T(8,128)S(1)} %collective-permute-done.35.rest_3_.rest_0_, f32[512,512]{1,0:T(8,128)S(1)} %collective-permute-done.38.rest_1_, f32[8,128]{1,0:T(8,128)S(1)} %get-tuple-element.149.rest_2_, ...), custom_call_target="tpu_custom_call", output_to_operand_aliasing={{0}: (4, {})} | custom-call | flops 24999999488 | bytes 1048576 | tf_op jit(solution)/shard_map/w31/pallas_call | solution.py:250
  (131 shorter events, 44.9 us)
Async XLA Ops:
  18.6 7.9 %collective-permute-start.3 = (f32[1032,512]{1,0:T(8,128)S(1)}, f32[1032,512]{1,0:T(8,128)S(1)}, u32[]{:S(2)}, u32[]{:S(2)}) collective-permute-start(f32[1032,512]{1,0:T(8,128)S(1)} %get-tuple-element.86.refs_2_), channel_id=1, source_target_pairs={{0,1},{1,0},{2,3},{3,2},{4,5},{5,4},{6,7},{7,6},{8,9},{9,8},{10,11... | collective-permute-start | bytes 6340616 | tf_op jit(solution)/shard_map/ppermute | solution.py:359
  18.9 14.3 %collective-permute-start.1 = (f32[520,512]{1,0:T(8,128)S(1)}, f32[520,512]{1,0:T(8,128)S(1)}, u32[]{:S(2)}, u32[]{:S(2)}) collective-permute-start(f32[520,512]{1,0:T(8,128)S(1)} %get-tuple-element.88.rest_0_), channel_id=1, source_target_pairs={{0,4},{1,3},{2,6},{3,1},{4,0},{5,7},{6,2},{7,5},{8,12},{9,11},{10,... | collective-permute-start | bytes 3194888 | tf_op jit(solution)/shard_map/ppermute | solution.py:359
  27.7 25.6 %collective-permute-start.9 = (f32[520,512]{1,0:T(8,128)}, f32[520,512]{1,0:T(8,128)}, u32[]{:S(2)}, u32[]{:S(2)}) collective-permute-start(f32[520,512]{1,0:T(8,128)} %get-tuple-element.94.refs_2_), channel_id=1, source_target_pairs={{0,8},{1,9},{2,10},{3,11},{4,12},{5,13},{6,14},{7,15},{8,0},{9,1},... | collective-permute-start | bytes 3194888 | tf_op jit(solution)/shard_map/ppermute | solution.py:359
  30.9 20.1 %collective-permute-start.4 = (f32[520,512]{1,0:T(8,128)S(1)}, f32[520,512]{1,0:T(8,128)S(1)}, u32[]{:S(2)}, u32[]{:S(2)}) collective-permute-start(f32[520,512]{1,0:T(8,128)S(1)} %get-tuple-element.95.refs_2_), channel_id=1, source_target_pairs={{0,4},{1,3},{2,6},{3,1},{4,0},{5,7},{6,2},{7,5},{8,12},{9,11},{10,... | collective-permute-start | bytes 3194888 | tf_op jit(solution)/shard_map/ppermute | solution.py:359
  33.3 14.5 %collective-permute-start.5 = (f32[264,512]{1,0:T(8,128)S(1)}, f32[264,512]{1,0:T(8,128)S(1)}, u32[]{:S(2)}, u32[]{:S(2)}) collective-permute-start(f32[264,512]{1,0:T(8,128)S(1)} %get-tuple-element.96.rest_0_), channel_id=1, source_target_pairs={{0,2},{1,5},{2,0},{3,7},{4,6},{5,1},{6,4},{7,3},{8,10},{9,13},{10,... | collective-permute-start | bytes 1622024 | tf_op jit(solution)/shard_map/ppermute | solution.py:359
  40.0 7.8 %collective-permute-start.6 = (f32[1032,512]{1,0:T(8,128)S(1)}, f32[1032,512]{1,0:T(8,128)S(1)}, u32[]{:S(2)}, u32[]{:S(2)}) collective-permute-start(f32[1032,512]{1,0:T(8,128)S(1)} %get-tuple-element.103.rest_0_), channel_id=1, source_target_pairs={{0,1},{1,0},{2,3},{3,2},{4,5},{5,4},{6,7},{7,6},{8,9},{9,8},{10,11... | collective-permute-start | bytes 6340616 | tf_op jit(solution)/shard_map/ppermute | solution.py:359
  47.9 10.5 %collective-permute-start.8 = (f32[136,512]{1,0:T(8,128)S(1)}, f32[136,512]{1,0:T(8,128)S(1)}, u32[]{:S(2)}, u32[]{:S(2)}) collective-permute-start(f32[136,512]{1,0:T(8,128)S(1)} %get-tuple-element.105.refs_2_), channel_id=1, source_target_pairs={{0,8},{1,9},{2,10},{3,11},{4,12},{5,13},{6,14},{7,15},{8,0},{9,1},... | collective-permute-start | bytes 835592 | tf_op jit(solution)/shard_map/ppermute | solution.py:359
  51.1 11.3 %collective-permute-start.7 = (f32[264,512]{1,0:T(8,128)S(1)}, f32[264,512]{1,0:T(8,128)S(1)}, u32[]{:S(2)}, u32[]{:S(2)}) collective-permute-start(f32[264,512]{1,0:T(8,128)S(1)} %get-tuple-element.107.refs_2_), channel_id=1, source_target_pairs={{0,2},{1,5},{2,0},{3,7},{4,6},{5,1},{6,4},{7,3},{8,10},{9,13},{10,... | collective-permute-start | bytes 1622024 | tf_op jit(solution)/shard_map/ppermute | solution.py:359
  52.0 20.1 %collective-permute-start.12 = (f32[520,512]{1,0:T(8,128)S(1)}, f32[520,512]{1,0:T(8,128)S(1)}, u32[]{:S(2)}, u32[]{:S(2)}) collective-permute-start(f32[520,512]{1,0:T(8,128)S(1)} %get-tuple-element.111.refs_2_), channel_id=1, source_target_pairs={{0,4},{1,3},{2,6},{3,1},{4,0},{5,7},{6,2},{7,5},{8,12},{9,11},{10,... | collective-permute-start | bytes 3194888 | tf_op jit(solution)/shard_map/ppermute | solution.py:359
  55.5 23.4 %collective-permute-start.14 = (f32[264,512]{1,0:T(8,128)}, f32[264,512]{1,0:T(8,128)}, u32[]{:S(2)}, u32[]{:S(2)}) collective-permute-start(f32[264,512]{1,0:T(8,128)} %get-tuple-element.112.refs_2_), channel_id=1, source_target_pairs={{0,4},{1,3},{2,6},{3,1},{4,0},{5,7},{6,2},{7,5},{8,12},{9,11},{10,... | collective-permute-start | bytes 1622024 | tf_op jit(solution)/shard_map/ppermute | solution.py:359
  58.5 14.7 %collective-permute-start.11 = (f32[136,512]{1,0:T(8,128)S(1)}, f32[136,512]{1,0:T(8,128)S(1)}, u32[]{:S(2)}, u32[]{:S(2)}) collective-permute-start(f32[136,512]{1,0:T(8,128)S(1)} %r03.1.refs_2_.refs_0_), channel_id=1, source_target_pairs={{0,24},{1,25},{2,26},{3,27},{4,28},{5,29},{6,30},{7,31},{8,16},{9,... | collective-permute-start | bytes 835592 | tf_op jit(solution)/shard_map/ppermute | solution.py:359
  62.5 12.1 %collective-permute-start.10 = (f32[136,512]{1,0:T(8,128)S(1)}, f32[136,512]{1,0:T(8,128)S(1)}, u32[]{:S(2)}, u32[]{:S(2)}) collective-permute-start(f32[136,512]{1,0:T(8,128)S(1)} %get-tuple-element.114.rest_0_), channel_id=1, source_target_pairs={{0,8},{1,9},{2,10},{3,11},{4,12},{5,13},{6,14},{7,15},{8,0},{9,1},... | collective-permute-start | bytes 835592 | tf_op jit(solution)/shard_map/ppermute | solution.py:359
  72.2 10.4 %collective-permute-start.17 = (f32[264,512]{1,0:T(8,128)S(1)}, f32[264,512]{1,0:T(8,128)S(1)}, u32[]{:S(2)}, u32[]{:S(2)}) collective-permute-start(f32[264,512]{1,0:T(8,128)S(1)} %get-tuple-element.118.refs_2_), channel_id=1, source_target_pairs={{0,2},{1,5},{2,0},{3,7},{4,6},{5,1},{6,4},{7,3},{8,10},{9,13},{10,... | collective-permute-start | bytes 1622024 | tf_op jit(solution)/shard_map/ppermute | solution.py:359
  73.2 10.9 %collective-permute-start.16 = (f32[128,512]{1,0:T(8,128)S(1)}, f32[128,512]{1,0:T(8,128)S(1)}, u32[]{:S(2)}, u32[]{:S(2)}) collective-permute-start(f32[128,512]{1,0:T(8,128)S(1)} %get-tuple-element.119.refs_2_.refs_0_), channel_id=1, source_target_pairs={{0,8},{1,9},{2,10},{3,11},{4,12},{5,13},{6,14},{7,15},{8,0},{9,1},... | collective-permute-start | bytes 786440 | tf_op jit(solution)/shard_map/ppermute | solution.py:359
  74.6 12.8 %collective-permute-start.13 = (f32[136,512]{1,0:T(8,128)S(1)}, f32[136,512]{1,0:T(8,128)S(1)}, u32[]{:S(2)}, u32[]{:S(2)}) collective-permute-start(f32[136,512]{1,0:T(8,128)S(1)} %r23.1.refs_2_.refs_0_), channel_id=1, source_target_pairs={{0,24},{1,25},{2,26},{3,27},{4,28},{5,29},{6,30},{7,31},{8,16},{9,... | collective-permute-start | bytes 835592 | tf_op jit(solution)/shard_map/ppermute | solution.py:359
  82.7 18.0 %collective-permute-start.20 = (f32[136,512]{1,0:T(8,128)S(1)}, f32[136,512]{1,0:T(8,128)S(1)}, u32[]{:S(2)}, u32[]{:S(2)}) collective-permute-start(f32[136,512]{1,0:T(8,128)S(1)} %get-tuple-element.124.refs_2_), channel_id=1, source_target_pairs={{0,8},{1,9},{2,10},{3,11},{4,12},{5,13},{6,14},{7,15},{8,0},{9,1},... | collective-permute-start | bytes 835592 | tf_op jit(solution)/shard_map/ppermute | solution.py:359
  84.1 8.4 %collective-permute-start.21 = (f32[256,512]{1,0:T(8,128)S(1)}, f32[256,512]{1,0:T(8,128)S(1)}, u32[]{:S(2)}, u32[]{:S(2)}) collective-permute-start(f32[256,512]{1,0:T(8,128)S(1)} %a01.1.refs_2_.refs_0_), channel_id=1, source_target_pairs={{0,2},{1,5},{2,0},{3,7},{4,6},{5,1},{6,4},{7,3},{8,10},{9,13},{10,... | collective-permute-start | bytes 1572872 | tf_op jit(solution)/shard_map/ppermute | solution.py:359
  85.8 15.9 %collective-permute-start.19 = (f32[136,512]{1,0:T(8,128)S(1)}, f32[136,512]{1,0:T(8,128)S(1)}, u32[]{:S(2)}, u32[]{:S(2)}) collective-permute-start(f32[136,512]{1,0:T(8,128)S(1)} %r13.1.refs_2_.refs_0_), channel_id=1, source_target_pairs={{0,24},{1,25},{2,26},{3,27},{4,28},{5,29},{6,30},{7,31},{8,16},{9,... | collective-permute-start | bytes 835592 | tf_op jit(solution)/shard_map/ppermute | solution.py:359
  88.0 15.9 %collective-permute-start.18 = (f32[128,512]{1,0:T(8,128)S(1)}, f32[128,512]{1,0:T(8,128)S(1)}, u32[]{:S(2)}, u32[]{:S(2)}) collective-permute-start(f32[128,512]{1,0:T(8,128)S(1)} %get-tuple-element.125.refs_2_.refs_0_), channel_id=1, source_target_pairs={{0,8},{1,9},{2,10},{3,11},{4,12},{5,13},{6,14},{7,15},{8,0},{9,1},... | collective-permute-start | bytes 786440 | tf_op jit(solution)/shard_map/ppermute | solution.py:359
  92.6 8.1 %collective-permute-start.22 = (f32[512,512]{1,0:T(8,128)S(1)}, f32[512,512]{1,0:T(8,128)S(1)}, u32[]{:S(2)}, u32[]{:S(2)}) collective-permute-start(f32[512,512]{1,0:T(8,128)S(1)} %a02.1.rest_0_), channel_id=1, source_target_pairs={{0,1},{1,0},{2,3},{3,2},{4,5},{5,4},{6,7},{7,6},{8,9},{9,8},{10,11... | collective-permute-start | bytes 3145736 | tf_op jit(solution)/shard_map/ppermute | solution.py:359
  95.1 17.5 %collective-permute-start.26 = (f32[512,512]{1,0:T(8,128)S(1)}, f32[512,512]{1,0:T(8,128)S(1)}, u32[]{:S(2)}, u32[]{:S(2)}) collective-permute-start(f32[512,512]{1,0:T(8,128)S(1)} %a02.1.rest_0_), channel_id=1, source_target_pairs={{0,4},{1,3},{2,6},{3,1},{4,0},{5,7},{6,2},{7,5},{8,12},{9,11},{10,... | collective-permute-start | bytes 3145736 | tf_op jit(solution)/shard_map/ppermute | solution.py:359
  101.7 14.3 %collective-permute-start.25 = (f32[136,512]{1,0:T(8,128)S(1)}, f32[136,512]{1,0:T(8,128)S(1)}, u32[]{:S(2)}, u32[]{:S(2)}) collective-permute-start(f32[136,512]{1,0:T(8,128)S(1)} %r33.1.refs_2_.refs_0_), channel_id=1, source_target_pairs={{0,24},{1,25},{2,26},{3,27},{4,28},{5,29},{6,30},{7,31},{8,16},{9,... | collective-permute-start | bytes 835592 | tf_op jit(solution)/shard_map/ppermute | solution.py:359
  102.3 10.2 %collective-permute-start.24 = (f32[128,512]{1,0:T(8,128)S(1)}, f32[128,512]{1,0:T(8,128)S(1)}, u32[]{:S(2)}, u32[]{:S(2)}) collective-permute-start(f32[128,512]{1,0:T(8,128)S(1)} %get-tuple-element.129.refs_2_.refs_0_), channel_id=1, source_target_pairs={{0,2},{1,5},{2,0},{3,7},{4,6},{5,1},{6,4},{7,3},{8,10},{9,13},{10,... | collective-permute-start | bytes 786440 | tf_op jit(solution)/shard_map/ppermute | solution.py:359
  104.0 14.0 %collective-permute-start.23 = (f32[256,512]{1,0:T(8,128)S(1)}, f32[256,512]{1,0:T(8,128)S(1)}, u32[]{:S(2)}, u32[]{:S(2)}) collective-permute-start(f32[256,512]{1,0:T(8,128)S(1)} %a21.1.refs_2_.refs_0_), channel_id=1, source_target_pairs={{0,2},{1,5},{2,0},{3,7},{4,6},{5,1},{6,4},{7,3},{8,10},{9,13},{10,... | collective-permute-start | bytes 1572872 | tf_op jit(solution)/shard_map/ppermute | solution.py:359
  116.0 7.3 %collective-permute-start.29 = (f32[128,512]{1,0:T(8,128)S(1)}, f32[128,512]{1,0:T(8,128)}, u32[]{:S(2)}, u32[]{:S(2)}) collective-permute-start(f32[128,512]{1,0:T(8,128)S(1)} %get-tuple-element.130.refs_2_.refs_0_), channel_id=1, source_target_pairs={{0,8},{1,9},{2,10},{3,11},{4,12},{5,13},{6,14},{7,15},{8,0},{9,1},... | collective-permute-start | bytes 786440 | tf_op jit(solution)/shard_map/ppermute | solution.py:359
  116.6 8.3 %collective-permute-start.32 = (f32[256,512]{1,0:T(8,128)S(1)}, f32[256,512]{1,0:T(8,128)S(1)}, u32[]{:S(2)}, u32[]{:S(2)}) collective-permute-start(f32[256,512]{1,0:T(8,128)S(1)} %a11.1.refs_2_.refs_0_), channel_id=1, source_target_pairs={{0,4},{1,3},{2,6},{3,1},{4,0},{5,7},{6,2},{7,5},{8,12},{9,11},{10,... | collective-permute-start | bytes 1572872 | tf_op jit(solution)/shard_map/ppermute | solution.py:359
  120.4 22.5 %collective-permute-start.28 = (f32[512,512]{1,0:T(8,128)S(1)}, f32[512,512]{1,0:T(8,128)S(1)}, u32[]{:S(2)}, u32[]{:S(2)}) collective-permute-start(f32[512,512]{1,0:T(8,128)S(1)} %a22.1.refs_2_.rest_0_), channel_id=1, source_target_pairs={{0,4},{1,3},{2,6},{3,1},{4,0},{5,7},{6,2},{7,5},{8,12},{9,11},{10,... | collective-permute-start | bytes 3145736 | tf_op jit(solution)/shard_map/ppermute | solution.py:359
  124.3 14.1 %collective-permute-start.30 = (f32[256,512]{1,0:T(8,128)S(1)}, f32[256,512]{1,0:T(8,128)S(1)}, u32[]{:S(2)}, u32[]{:S(2)}) collective-permute-start(f32[256,512]{1,0:T(8,128)S(1)} %a31.1.refs_2_.refs_0_), channel_id=1, source_target_pairs={{0,2},{1,5},{2,0},{3,7},{4,6},{5,1},{6,4},{7,3},{8,10},{9,13},{10,... | collective-permute-start | bytes 1572872 | tf_op jit(solution)/shard_map/ppermute | solution.py:359
  125.0 13.4 %collective-permute-start.33 = (f32[512,512]{1,0:T(8,128)S(1)}, f32[512,512]{1,0:T(8,128)S(1)}, u32[]{:S(2)}, u32[]{:S(2)}) collective-permute-start(f32[512,512]{1,0:T(8,128)S(1)} %a12.1.rest_2_.rest_0_), channel_id=1, source_target_pairs={{0,1},{1,0},{2,3},{3,2},{4,5},{5,4},{6,7},{7,6},{8,9},{9,8},{10,11... | collective-permute-start | bytes 3145736 | tf_op jit(solution)/shard_map/ppermute | solution.py:359
  128.7 25.0 %collective-permute-start.37 = (f32[512,512]{1,0:T(8,128)S(1)}, f32[512,512]{1,0:T(8,128)S(1)}, u32[]{:S(2)}, u32[]{:S(2)}) collective-permute-start(f32[512,512]{1,0:T(8,128)S(1)} %a12.1.rest_2_.rest_0_), channel_id=1, source_target_pairs={{0,8},{1,9},{2,10},{3,11},{4,12},{5,13},{6,14},{7,15},{8,0},{9,1},... | collective-permute-start | bytes 3145736 | tf_op jit(solution)/shard_map/ppermute | solution.py:359
  138.5 8.7 %collective-permute-start.35 = (f32[512,512]{1,0:T(8,128)S(1)}, f32[512,512]{1,0:T(8,128)S(1)}, u32[]{:S(2)}, u32[]{:S(2)}) collective-permute-start(f32[512,512]{1,0:T(8,128)S(1)} %a32.1.rest_2_.rest_0_), channel_id=1, source_target_pairs={{0,1},{1,0},{2,3},{3,2},{4,5},{5,4},{6,7},{7,6},{8,9},{9,8},{10,11... | collective-permute-start | bytes 3145736 | tf_op jit(solution)/shard_map/ppermute | solution.py:359
  141.0 15.3 %collective-permute-start.36 = (f32[512,512]{1,0:T(8,128)S(1)}, f32[512,512]{1,0:T(8,128)S(1)}, u32[]{:S(2)}, u32[]{:S(2)}) collective-permute-start(f32[512,512]{1,0:T(8,128)S(1)} %a32.1.rest_2_.rest_0_), channel_id=1, source_target_pairs={{0,4},{1,3},{2,6},{3,1},{4,0},{5,7},{6,2},{7,5},{8,12},{9,11},{10,... | collective-permute-start | bytes 3145736 | tf_op jit(solution)/shard_map/ppermute | solution.py:359
  (26 other events, 334.4 us)
